TPU v7x, 32 devices: a whole 2x2x4 slice. The times are simulated.
32 devices in a mesh: ctx: 16 (over z, y, core), fsdp: 2 (over x).
Axes of the slice: x: 2, y: 2, z: 4, core: 2. Of those that a mesh axis runs over, the one named last changes fastest.
Arguments:
- resid: bfloat16 [2, 4096, 767], P('fsdp', 'ctx'), may hold values from -6 to 6
- lengths: int32 [2], P('fsdp'), may hold values from 1024 to 4096, as said below
- gain_one: bfloat16 [768], P('fsdp'), may hold values from 0.099609375 to 1.8984375
- w_qkv: bfloat16 [768, 2304], P('fsdp'), may hold values from -0.21875 to 0.21875
- w_out: bfloat16 [768, 767], P('fsdp'), may hold values from -3.5 to 3.5
- gain_two: bfloat16 [768], P('fsdp'), may hold values from 0.099609375 to 1.8984375
- w_up: bfloat16 [768, 3072], P(None, 'fsdp'), may hold values from -0.21875 to 0.21875
- w_down: bfloat16 [3072, 767], P('fsdp'), may hold values from -0.109375 to 0.109375
- cotangent: bfloat16 [2, 4096, 767], P('fsdp', 'ctx'), may hold values from -6 to 6
Outputs:
- output: bfloat16 [2, 4096, 767], P('fsdp', 'ctx')
- grad_input: float32 [2, 4096, 767], P('fsdp', 'ctx')
- grad_gain_one: float32 [768], P('fsdp')
- grad_qkv: float32 [768, 2304], P('fsdp')
- grad_out: float32 [768, 767], P('fsdp')
- grad_gain_two: float32 [768], P('fsdp')
- grad_up: float32 [768, 3072], P(None, 'fsdp')
- grad_down: float32 [3072, 767], P('fsdp')
Inputs may be any that keep to these rules, and one draw needn't show every extreme that they name: `lengths`: live slots of each sequence, counted from its first slot; one sequence has all 4096 live and one has 1024.
All inputs are finite; a program needn't handle non-finite values.
Results may differ from a plain program's by a relative error of at most 0.024.
Values may be sent and summed in bfloat16 or wider, within the bound.
A program may use at most 128 MiB of HBM per device.

v0:
```python
import jax
import jax.numpy as jnp
from jax import lax
from jax.sharding import PartitionSpec as P

HDIM = 64


epsilon = 1e-05
masked = -1e30


def passed_along(block, axis, distance):
    devices = range(lax.axis_size(axis))
    route = [((i - distance) % len(devices), i) for i in devices]
    return lax.ppermute(block, axis, route)


def crms(residual, gain):
    extended = jnp.concatenate([residual, -jnp.sum(residual, axis=-1, keepdims=True)], axis=-1)
    inverse = lax.rsqrt(jnp.mean(extended * extended, axis=-1, keepdims=True) + epsilon)
    return extended * inverse * gain


def gelu_tanh(values):
    return jax.nn.gelu(values, approximate=True)


def slot_positions(index, slot_count):
    return index * slot_count + jnp.arange(slot_count, dtype=jnp.int32)


def block_scores(queries, key_block, query_pos, key_pos, lengths, factor):
    scores = (
        jnp.einsum("bqhd,bkhd->bqhk", queries, key_block, preferred_element_type=jnp.float32)
        * factor
    )
    allowed = (key_pos[None, None, None, :] <= query_pos[None, :, None, None]) & (
        key_pos[None, None, None, :] < lengths[:, None, None, None]
    )
    return jnp.where(allowed, scores, masked)


def circle_forward(queries, kv_block, query_pos, lengths, direction, move_block):
    circle_size = lax.axis_size("ctx")
    my_index = lax.axis_index("ctx")
    slot_count = queries.shape[1]
    factor = queries.shape[-1] ** (-0.5)
    longest = jnp.max(lengths)
    last_query = jnp.max(query_pos)

    def visit(state, held, source):
        key_pos = slot_positions(source, slot_count)

        def work(carried):
            running, totals, weighted = carried
            scores = block_scores(queries, held[0], query_pos, key_pos, lengths, factor)
            newest = jnp.maximum(running, jnp.max(scores, axis=-1))
            shrink = jnp.exp(running - newest)
            weights_block = jnp.exp(scores - newest[..., None])
            totals = totals * shrink + jnp.sum(weights_block, axis=-1)
            weighted = weighted * shrink[..., None] + jnp.einsum(
                "bqhk,bkhd->bqhd",
                weights_block.astype(jnp.bfloat16),
                held[1],
                preferred_element_type=jnp.float32,
            )
            return (newest, totals, weighted)

        first_key = jnp.min(key_pos)
        needed = (first_key <= last_query) & (first_key < longest)
        return lax.cond(needed, work, lambda carried: carried, state)

    stat_shape = queries.shape[:3]
    state = (
        jnp.full(stat_shape, masked, jnp.float32),
        jnp.zeros(stat_shape, jnp.float32),
        jnp.zeros(queries.shape, jnp.float32),
    )
    state = visit(state, kv_block, my_index)

    def one_turn(step_no, carried):
        held, current = carried
        held = move_block(held)
        source = (my_index - direction * step_no) % circle_size
        return (held, visit(current, held, source))

    held, state = lax.fori_loop(1, circle_size, one_turn, (kv_block, state))
    running, totals, weighted = state
    return (weighted / totals[..., None], running + jnp.log(totals))


def circle_backward(
    queries,
    kv_block,
    grad_attn,
    log_total,
    row_delta,
    query_pos,
    lengths,
    direction,
    move_block,
    move_grads,
):
    circle_size = lax.axis_size("ctx")
    my_index = lax.axis_index("ctx")
    slot_count = queries.shape[1]
    factor = queries.shape[-1] ** (-0.5)
    longest = jnp.max(lengths)
    last_query = jnp.max(query_pos)

    def visit(grad_query, held_grads, held, source):
        key_pos = slot_positions(source, slot_count)

        def work(carried):
            query_acc, grad_held = carried
            scores = block_scores(queries, held[0], query_pos, key_pos, lengths, factor)
            weights_block = jnp.exp(scores - log_total[..., None])
            grad_values = jnp.einsum(
                "bqhk,bqhd->bkhd",
                weights_block.astype(jnp.bfloat16),
                grad_attn,
                preferred_element_type=jnp.float32,
            )
            grad_weights = jnp.einsum(
                "bqhd,bkhd->bqhk", grad_attn, held[1], preferred_element_type=jnp.float32
            )
            grad_scores = (weights_block * (grad_weights - row_delta[..., None])).astype(
                jnp.bfloat16
            )
            query_acc = (
                query_acc
                + jnp.einsum(
                    "bqhk,bkhd->bqhd", grad_scores, held[0], preferred_element_type=jnp.float32
                )
                * factor
            )
            grad_keys = (
                jnp.einsum(
                    "bqhk,bqhd->bkhd", grad_scores, queries, preferred_element_type=jnp.float32
                )
                * factor
            )
            return (query_acc, grad_held + jnp.stack([grad_keys, grad_values]))

        first_key = jnp.min(key_pos)
        needed = (first_key <= last_query) & (first_key < longest)
        return lax.cond(needed, work, lambda carried: carried, (grad_query, held_grads))

    grad_query, held_grads = visit(
        jnp.zeros(queries.shape, jnp.float32),
        jnp.zeros(kv_block.shape, jnp.float32),
        kv_block,
        my_index,
    )

    def one_turn(step_no, carried):
        held, query_acc, grad_held = carried
        held = move_block(held)
        grad_held = move_grads(grad_held)
        source = (my_index - direction * step_no) % circle_size
        query_acc, grad_held = visit(query_acc, grad_held, held, source)
        return (held, query_acc, grad_held)

    held, grad_query, held_grads = lax.fori_loop(
        1, circle_size, one_turn, (kv_block, grad_query, held_grads)
    )
    return (grad_query, move_grads(held_grads))


def shards(resid, lengths, gain_one, w_qkv, w_out, gain_two, w_up, w_down, cotangent):
    gain_first, qkv_full, out_full, gain_second, up_full, down_full = (
        lax.all_gather(gain_one, "fsdp", axis=0, tiled=True),
        lax.all_gather(w_qkv, "fsdp", axis=0, tiled=True),
        lax.all_gather(w_out, "fsdp", axis=0, tiled=True),
        lax.all_gather(gain_two, "fsdp", axis=0, tiled=True),
        lax.all_gather(w_up, "fsdp", axis=1, tiled=True),
        lax.all_gather(w_down, "fsdp", axis=0, tiled=True),
    )
    batch_count, slot_count, narrow = resid.shape
    model_width = qkv_full.shape[0]
    head_count = model_width // HDIM
    row_count = batch_count * slot_count
    my_index = lax.axis_index("ctx")
    query_pos = slot_positions(my_index, slot_count)
    resid_wide = resid.astype(jnp.float32)
    normed_one, norm_one_back = jax.vjp(crms, resid_wide, gain_first.astype(jnp.float32))
    hidden_one = normed_one.astype(jnp.bfloat16).reshape(row_count, model_width)
    projected = jnp.dot(hidden_one, qkv_full, preferred_element_type=jnp.float32).astype(
        jnp.bfloat16
    )
    queries = projected[:, :model_width].reshape(batch_count, slot_count, head_count, HDIM)
    kv_block = jnp.stack(
        [projected[:, model_width : 2 * model_width], projected[:, 2 * model_width :]]
    ).reshape(2, batch_count, slot_count, head_count, HDIM)
    attended, log_total = circle_forward(
        queries, kv_block, query_pos, lengths, -1, lambda stacked: passed_along(stacked, "ctx", -1)
    )
    attended_low = attended.astype(jnp.bfloat16).reshape(row_count, model_width)
    branch = jnp.dot(attended_low, out_full, preferred_element_type=jnp.float32)
    middle = resid_wide + branch.reshape(batch_count, slot_count, narrow)
    normed_two, norm_two_back = jax.vjp(crms, middle, gain_second.astype(jnp.float32))
    hidden_two = normed_two.astype(jnp.bfloat16).reshape(row_count, model_width)
    pre_act = jnp.dot(hidden_two, up_full, preferred_element_type=jnp.float32)
    activ_wide, gelu_back = jax.vjp(gelu_tanh, pre_act)
    activated = activ_wide.astype(jnp.bfloat16)
    mlp_out = jnp.dot(activated, down_full, preferred_element_type=jnp.float32)
    final_wide = middle + mlp_out.reshape(batch_count, slot_count, narrow)
    live = (query_pos[None, :] < lengths[:, None]).astype(jnp.float32)
    grad_top = cotangent.astype(jnp.float32) * live[:, :, None]
    grad_mlp = grad_top.astype(jnp.bfloat16).reshape(row_count, narrow)
    grad_down = jnp.dot(activated.T, grad_mlp, preferred_element_type=jnp.float32)
    grad_activ = jnp.dot(grad_mlp, down_full.T, preferred_element_type=jnp.float32)
    grad_pre = gelu_back(grad_activ)[0].astype(jnp.bfloat16)
    grad_up = jnp.dot(hidden_two.T, grad_pre, preferred_element_type=jnp.float32)
    grad_hidden_two = jnp.dot(grad_pre, up_full.T, preferred_element_type=jnp.float32)
    grad_middle_norm, grad_gain_two = norm_two_back(
        grad_hidden_two.reshape(batch_count, slot_count, model_width)
    )
    grad_middle = grad_top + grad_middle_norm
    grad_branch = grad_middle.astype(jnp.bfloat16).reshape(row_count, narrow)
    grad_out = jnp.dot(attended_low.T, grad_branch, preferred_element_type=jnp.float32)
    grad_attn = (
        jnp.dot(grad_branch, out_full.T, preferred_element_type=jnp.float32)
        .astype(jnp.bfloat16)
        .reshape(batch_count, slot_count, head_count, HDIM)
    )
    row_delta = jnp.sum(grad_attn.astype(jnp.float32) * attended, axis=-1)
    grad_query, grad_kv = circle_backward(
        queries,
        kv_block,
        grad_attn,
        log_total,
        row_delta,
        query_pos,
        lengths,
        -1,
        lambda stacked: passed_along(stacked, "ctx", -1),
        lambda stacked: passed_along(stacked.astype(jnp.bfloat16), "ctx", -1).astype(stacked.dtype),
    )
    grad_projected = jnp.concatenate(
        [
            grad_query.reshape(row_count, model_width),
            grad_kv[0].reshape(row_count, model_width),
            grad_kv[1].reshape(row_count, model_width),
        ],
        axis=1,
    ).astype(jnp.bfloat16)
    grad_qkv = jnp.dot(hidden_one.T, grad_projected, preferred_element_type=jnp.float32)
    grad_hidden_one = jnp.dot(grad_projected, qkv_full.T, preferred_element_type=jnp.float32)
    grad_resid_norm, grad_gain_one = norm_one_back(
        grad_hidden_one.reshape(batch_count, slot_count, model_width)
    )
    grad_input = grad_middle + grad_resid_norm
    final = final_wide.astype(jnp.bfloat16)
    shard_sums = (
        lax.psum_scatter(
            grad_gain_one.astype(jnp.bfloat16), "fsdp", scatter_dimension=0, tiled=True
        ).astype(jnp.float32),
        lax.psum_scatter(
            grad_qkv.astype(jnp.bfloat16), "fsdp", scatter_dimension=0, tiled=True
        ).astype(jnp.float32),
        lax.psum_scatter(
            grad_out.astype(jnp.bfloat16), "fsdp", scatter_dimension=0, tiled=True
        ).astype(jnp.float32),
        lax.psum_scatter(
            grad_gain_two.astype(jnp.bfloat16), "fsdp", scatter_dimension=0, tiled=True
        ).astype(jnp.float32),
        lax.psum_scatter(
            grad_up.astype(jnp.bfloat16), "fsdp", scatter_dimension=1, tiled=True
        ).astype(jnp.float32),
        lax.psum_scatter(
            grad_down.astype(jnp.bfloat16), "fsdp", scatter_dimension=0, tiled=True
        ).astype(jnp.float32),
    )
    totals_all = lax.psum(
        (shard_sums[0], shard_sums[1], shard_sums[2], shard_sums[3], shard_sums[4], shard_sums[5]),
        "ctx",
    )
    return (
        final,
        grad_input,
        totals_all[0],
        totals_all[1],
        totals_all[2],
        totals_all[3],
        totals_all[4],
        totals_all[5],
    )


def solution(mesh):
    return jax.shard_map(
        shards,
        mesh=mesh,
        in_specs=(
            P("fsdp", "ctx", None),
            P("fsdp"),
            P("fsdp"),
            P("fsdp", None),
            P("fsdp", None),
            P("fsdp"),
            P(None, "fsdp"),
            P("fsdp", None),
            P("fsdp", "ctx", None),
        ),
        out_specs=(
            P("fsdp", "ctx", None),
            P("fsdp", "ctx", None),
            P("fsdp"),
            P("fsdp", None),
            P("fsdp", None),
            P("fsdp"),
            P(None, "fsdp"),
            P("fsdp", None),
        ),
        check_vma=False,
    )
```

profile of v0, /device:TPU:0, one launch (start us, length us, event | category | flops | bytes accessed | tf_op | source)
XLA Modules:
  0.0 1341.1 jit_solution(15695101697606549651)
XLA Ops:
  26.3 35.3 %all-gather.7.cloned.1.call-done = bf16[768,2304]{1,0:T(8,128)(2,1)} async-done(((bf16[384,2304]{1,0:T(8,128)(2,1)}), bf16[768,2304]{1,0:T(8,128)(2,1)}) %all-gather.7.cloned.1.call-update) | async-done | bytes 3538960 | tf_op jit(solution)/shard_map/all_gather | solution.py:174
  67.5 6.7 conditional.4
  74.2 221.6 %while.42 = (s32[]{:T(128)}, bf16[2,1,256,12,64]{2,4,3,1,0:T(8,128)(2,1)S(1)}, f32[1,256,12]{1,2,0:T(8,128)S(1)}, f32[1,256,12]{1,2,0:T(8,128)S(1)}, f32[1,256,1...) while((s32[]{:T(128)}, ...), condition=%wide.region_14.15_spmd.clone, body=%wide.region_8.14_spmd.clone.sunk | while | flops 210512144 | bytes 17383428 | solution.py:88
  83.8 7.8 collective-permute-start
  94.9 6.2 collective-permute-done
  101.2 7.8 collective-permute-start
  112.3 6.2 collective-permute-done
  118.6 7.8 collective-permute-start
  129.7 6.2 collective-permute-done
  136.0 7.8 collective-permute-start
  147.1 6.2 collective-permute-done
  175.6 6.2 collective-permute-done
  189.8 6.2 collective-permute-done
  204.1 6.2 collective-permute-done
  218.3 6.2 collective-permute-done
  232.5 6.2 collective-permute-done
  246.8 6.2 collective-permute-done
  261.0 6.2 collective-permute-done
  275.3 6.2 collective-permute-done
  289.5 6.2 collective-permute-done
  304.4 6.8 fusion.153
  320.5 10.3 conditional.5
  330.8 393.1 %while.43 = (s32[]{:T(128)}, bf16[2,1,256,12,64]{2,4,3,1,0:T(8,128)(2,1)}, f32[1,256,12,64]{1,3,2,0:T(8,128)S(1)}, f32[2,1,256,12,64]{2,4,3,1,0:T(8,128)S(1)}, s...) while((s32[]{:T(128)}, ...), condition=%wide.region_25.26_spmd.clone, body=%wide.region_21.0_spmd.clone.sunk | while | flops 513475872 | bytes 37650520 | solution.py:165
  335.1 6.5 collective-permute-done.2
  343.0 7.1 collective-permute-done.1
  352.0 11.4 collective-permute-start.2
  366.7 6.5 collective-permute-done.2
  374.5 7.1 collective-permute-done.1
  383.6 11.4 collective-permute-start.2
  398.2 6.5 collective-permute-done.2
  406.1 7.1 collective-permute-done.1
  415.1 11.4 collective-permute-start.2
  429.8 6.5 collective-permute-done.2
  437.6 7.1 collective-permute-done.1
  446.6 11.4 collective-permute-start.2
  461.3 6.5 collective-permute-done.2
  469.1 7.1 collective-permute-done.1
  486.0 6.5 collective-permute-done.2
  493.8 7.1 collective-permute-done.1
  510.7 6.5 collective-permute-done.2
  518.5 7.1 collective-permute-done.1
  535.4 6.5 collective-permute-done.2
  543.2 7.1 collective-permute-done.1
  560.0 6.5 collective-permute-done.2
  567.8 7.1 collective-permute-done.1
  584.7 6.5 collective-permute-done.2
  592.5 7.1 collective-permute-done.1
  609.4 6.5 collective-permute-done.2
  617.2 7.1 collective-permute-done.1
  634.1 6.5 collective-permute-done.2
  641.9 7.1 collective-permute-done.1
  658.7 6.5 collective-permute-done.2
  666.6 7.1 collective-permute-done.1
  683.4 6.5 collective-permute-done.2
  691.2 7.1 collective-permute-done.1
  708.1 6.5 collective-permute-done.2
  715.9 7.1 collective-permute-done.1
  728.6 9.4 collective-permute-done.3
  742.3 6.4 convolution_convert_fusion
  767.3 122.3 %all-reduce.3 = (bf16[768]{0:T(1024)(128)(2,1)S(1)}, bf16[768]{0:T(1024)(128)(2,1)S(1)}) all-reduce(bf16[768]{0:T(1024)(128)(2,1)S(1)} %get-tuple-element.855, bf16[768]{0:T(1024)(128)(2,1)S(1)} %copy-done.38), channel_id=2, replica_groups=mesh['ctx'=16,'fsdp'=2] {'fsdp'}, use_global_device_ids=true, to_apply=%region_28.29.clone | all-reduce | flops 1536 | bytes 6144
  889.8 18.1 %reduce-scatter.5.cloned.1.call-done = bf16[384,2304]{1,0:T(8,128)(2,1)} async-done(((bf16[768,2304]{1,0:T(8,128)(2,1)}), bf16[384,2304]{1,0:T(8,128)(2,1)}) %reduce-scatter.5.cloned.1.call-update) | async-done | bytes 1769488 | tf_op jit(solution)/shard_map/reduce_scatter | solution.py:260
  907.9 63.0 %reduce-scatter.11.cloned.1.call-done = bf16[1536,767]{1,0:T(8,128)(2,1)} async-done(((bf16[3072,767]{1,0:T(8,128)(2,1)}), bf16[1536,767]{1,0:T(8,128)(2,1)}) %reduce-scatter.11.cloned.1.call-update) | async-done | bytes 2356240 | tf_op jit(solution)/shard_map/reduce_scatter | solution.py:272
  970.9 63.0 %reduce-scatter.9.cloned.1.call-done = bf16[768,1536]{1,0:T(8,128)(2,1)} async-done(((bf16[768,3072]{1,0:T(8,128)(2,1)}), bf16[768,1536]{1,0:T(8,128)(2,1)}) %reduce-scatter.9.cloned.1.call-update) | async-done | bytes 2359312 | tf_op jit(solution)/shard_map/reduce_scatter | solution.py:269
  1033.9 300.4 %all-reduce.5 = (f32[384]{0:T(512)}, f32[384,2304]{1,0:T(8,128)}, f32[384,767]{1,0:T(8,128)}, f32[384]{0:T(512)}, f32[768,1536]{1,0:T(8,128)}, /*index=5*/f32[1536,767]{1,0:T(8,128)}) all-reduce(f32[384]{0:T(512)S(1)} %dynamic-slice_convert_fusion.1, ...), channel_id=1, replica_groups=mesh['ctx'=16,'fsdp'=2] {'ctx'}, use_global_device_ids=true, to_apply=%region_29.30 | all-reduce | flops 3537792 | bytes 21228288 | tf_op jit(solution)/shard_map/psum | solution.py:276
  (399 shorter events, 256.0 us)
Async XLA Ops:
  7.2 54.4 %all-gather.7.cloned.1.call-start = ((), (), s32[]{:S(2)}) async-start(), calls=%async_computation.4 | async-start | bytes 5308416 | tf_op jit(solution)/shard_map/all_gather | solution.py:174
  7.9 288.0 %all-gather.9.cloned.1.call-start = ((), (), s32[]{:S(2)}) async-start(), calls=%async_computation.5 | async-start | bytes 1769472 | tf_op jit(solution)/shard_map/all_gather | solution.py:175
  8.7 290.2 %all-gather.11.cloned.1.call-start = ((), (), s32[]{:S(2)}) async-start(), calls=%async_computation.6 | async-start | bytes 7077888 | tf_op jit(solution)/shard_map/all_gather | solution.py:177
  9.4 295.0 %all-gather.13.cloned.1.call-start = ((), (), s32[]{:S(2)}) async-start(), calls=%async_computation.7 | async-start | bytes 7077888 | tf_op jit(solution)/shard_map/all_gather | solution.py:178
  10.0 879.8 %reduce-scatter.7.cloned.1.call-start = ((), (), s32[]{:S(2)}) async-start(), calls=%async_computation.9 | async-start | bytes 1769472 | tf_op jit(solution)/shard_map/reduce_scatter | solution.py:263
  16.8 47.9 %copy-start.23 = (f32[768]{0:T(1024)}, f32[768]{0:T(1024)S(1)}, u32[]{:S(2)}) copy-start(f32[768]{0:T(1024)S(1)} %reshape.752) | copy-start | bytes 9220
  25.3 39.5 %copy-start.14 = (f32[256,1]{1,0:T(8,128)}, f32[256,1]{1,0:T(8,128)S(1)}, u32[]{:S(2)}) copy-start(f32[256,1]{1,0:T(8,128)S(1)} %copy.60) | copy-start | bytes 3076
  25.5 39.3 %copy-start.6 = (f32[256,767]{1,0:T(8,128)}, f32[256,767]{1,0:T(8,128)S(1)}, u32[]{:S(2)}) copy-start(f32[256,767]{1,0:T(8,128)S(1)} %get-tuple-element.928) | copy-start | bytes 2356228
  25.7 39.2 %copy-start.32 = (f32[256]{0:T(256)}, f32[256]{0:T(256)S(1)}, u32[]{:S(2)}) copy-start(f32[256]{0:T(256)S(1)} %fusion.161) | copy-start | bytes 3076
  26.3 38.6 %copy-start.36 = (f32[256]{0:T(256)}, f32[256]{0:T(256)S(1)}, u32[]{:S(2)}) copy-start(f32[256]{0:T(256)S(1)} %fusion.178) | copy-start | bytes 3076
  74.2 9.6 collective-permute-start
  83.8 17.3 %collective-permute-start = (bf16[2,1,256,12,64]{2,4,3,1,0:T(8,128)(2,1)S(1)}, bf16[2,1,256,12,64]{2,4,3,1,0:T(8,128)(2,1)S(1)}, u32[]{:S(2)}, u32[]{:S(2)}) collective-permute-start(bf16[2,1,256,12,64]{2,4,3,1,0:T(8,128)(2,1)S(1)} %get-tuple-element.1126), channel_id=1, source_target_pairs={{2,0},{4,2},{6,4},{8,6},{10,8},{12,10},{14,12},{16,14},{18,16},{20... | collective-permute-start | bytes 2359304 | tf_op jit(solution)/shard_map/while/body/eval_jaxpr/ppermute | solution.py:16
  101.2 17.3 %collective-permute-start = (bf16[2,1,256,12,64]{2,4,3,1,0:T(8,128)(2,1)S(1)}, bf16[2,1,256,12,64]{2,4,3,1,0:T(8,128)(2,1)S(1)}, u32[]{:S(2)}, u32[]{:S(2)}) collective-permute-start(bf16[2,1,256,12,64]{2,4,3,1,0:T(8,128)(2,1)S(1)} %get-tuple-element.1126), channel_id=1, source_target_pairs={{2,0},{4,2},{6,4},{8,6},{10,8},{12,10},{14,12},{16,14},{18,16},{20... | collective-permute-start | bytes 2359304 | tf_op jit(solution)/shard_map/while/body/eval_jaxpr/ppermute | solution.py:16
  118.6 17.3 %collective-permute-start = (bf16[2,1,256,12,64]{2,4,3,1,0:T(8,128)(2,1)S(1)}, bf16[2,1,256,12,64]{2,4,3,1,0:T(8,128)(2,1)S(1)}, u32[]{:S(2)}, u32[]{:S(2)}) collective-permute-start(bf16[2,1,256,12,64]{2,4,3,1,0:T(8,128)(2,1)S(1)} %get-tuple-element.1126), channel_id=1, source_target_pairs={{2,0},{4,2},{6,4},{8,6},{10,8},{12,10},{14,12},{16,14},{18,16},{20... | collective-permute-start | bytes 2359304 | tf_op jit(solution)/shard_map/while/body/eval_jaxpr/ppermute | solution.py:16
  136.0 17.3 %collective-permute-start = (bf16[2,1,256,12,64]{2,4,3,1,0:T(8,128)(2,1)S(1)}, bf16[2,1,256,12,64]{2,4,3,1,0:T(8,128)(2,1)S(1)}, u32[]{:S(2)}, u32[]{:S(2)}) collective-permute-start(bf16[2,1,256,12,64]{2,4,3,1,0:T(8,128)(2,1)S(1)} %get-tuple-element.1126), channel_id=1, source_target_pairs={{2,0},{4,2},{6,4},{8,6},{10,8},{12,10},{14,12},{16,14},{18,16},{20... | collective-permute-start | bytes 2359304 | tf_op jit(solution)/shard_map/while/body/eval_jaxpr/ppermute | solution.py:16
  153.4 14.2 %collective-permute-start = (bf16[2,1,256,12,64]{2,4,3,1,0:T(8,128)(2,1)S(1)}, bf16[2,1,256,12,64]{2,4,3,1,0:T(8,128)(2,1)S(1)}, u32[]{:S(2)}, u32[]{:S(2)}) collective-permute-start(bf16[2,1,256,12,64]{2,4,3,1,0:T(8,128)(2,1)S(1)} %get-tuple-element.1126), channel_id=1, source_target_pairs={{2,0},{4,2},{6,4},{8,6},{10,8},{12,10},{14,12},{16,14},{18,16},{20... | collective-permute-start | bytes 2359304 | tf_op jit(solution)/shard_map/while/body/eval_jaxpr/ppermute | solution.py:16
  167.6 14.2 %collective-permute-start = (bf16[2,1,256,12,64]{2,4,3,1,0:T(8,128)(2,1)S(1)}, bf16[2,1,256,12,64]{2,4,3,1,0:T(8,128)(2,1)S(1)}, u32[]{:S(2)}, u32[]{:S(2)}) collective-permute-start(bf16[2,1,256,12,64]{2,4,3,1,0:T(8,128)(2,1)S(1)} %get-tuple-element.1126), channel_id=1, source_target_pairs={{2,0},{4,2},{6,4},{8,6},{10,8},{12,10},{14,12},{16,14},{18,16},{20... | collective-permute-start | bytes 2359304 | tf_op jit(solution)/shard_map/while/body/eval_jaxpr/ppermute | solution.py:16
  181.9 14.2 %collective-permute-start = (bf16[2,1,256,12,64]{2,4,3,1,0:T(8,128)(2,1)S(1)}, bf16[2,1,256,12,64]{2,4,3,1,0:T(8,128)(2,1)S(1)}, u32[]{:S(2)}, u32[]{:S(2)}) collective-permute-start(bf16[2,1,256,12,64]{2,4,3,1,0:T(8,128)(2,1)S(1)} %get-tuple-element.1126), channel_id=1, source_target_pairs={{2,0},{4,2},{6,4},{8,6},{10,8},{12,10},{14,12},{16,14},{18,16},{20... | collective-permute-start | bytes 2359304 | tf_op jit(solution)/shard_map/while/body/eval_jaxpr/ppermute | solution.py:16
  196.1 14.2 %collective-permute-start = (bf16[2,1,256,12,64]{2,4,3,1,0:T(8,128)(2,1)S(1)}, bf16[2,1,256,12,64]{2,4,3,1,0:T(8,128)(2,1)S(1)}, u32[]{:S(2)}, u32[]{:S(2)}) collective-permute-start(bf16[2,1,256,12,64]{2,4,3,1,0:T(8,128)(2,1)S(1)} %get-tuple-element.1126), channel_id=1, source_target_pairs={{2,0},{4,2},{6,4},{8,6},{10,8},{12,10},{14,12},{16,14},{18,16},{20... | collective-permute-start | bytes 2359304 | tf_op jit(solution)/shard_map/while/body/eval_jaxpr/ppermute | solution.py:16
  210.4 14.2 %collective-permute-start = (bf16[2,1,256,12,64]{2,4,3,1,0:T(8,128)(2,1)S(1)}, bf16[2,1,256,12,64]{2,4,3,1,0:T(8,128)(2,1)S(1)}, u32[]{:S(2)}, u32[]{:S(2)}) collective-permute-start(bf16[2,1,256,12,64]{2,4,3,1,0:T(8,128)(2,1)S(1)} %get-tuple-element.1126), channel_id=1, source_target_pairs={{2,0},{4,2},{6,4},{8,6},{10,8},{12,10},{14,12},{16,14},{18,16},{20... | collective-permute-start | bytes 2359304 | tf_op jit(solution)/shard_map/while/body/eval_jaxpr/ppermute | solution.py:16
  224.6 14.2 %collective-permute-start = (bf16[2,1,256,12,64]{2,4,3,1,0:T(8,128)(2,1)S(1)}, bf16[2,1,256,12,64]{2,4,3,1,0:T(8,128)(2,1)S(1)}, u32[]{:S(2)}, u32[]{:S(2)}) collective-permute-start(bf16[2,1,256,12,64]{2,4,3,1,0:T(8,128)(2,1)S(1)} %get-tuple-element.1126), channel_id=1, source_target_pairs={{2,0},{4,2},{6,4},{8,6},{10,8},{12,10},{14,12},{16,14},{18,16},{20... | collective-permute-start | bytes 2359304 | tf_op jit(solution)/shard_map/while/body/eval_jaxpr/ppermute | solution.py:16
  238.8 14.2 %collective-permute-start = (bf16[2,1,256,12,64]{2,4,3,1,0:T(8,128)(2,1)S(1)}, bf16[2,1,256,12,64]{2,4,3,1,0:T(8,128)(2,1)S(1)}, u32[]{:S(2)}, u32[]{:S(2)}) collective-permute-start(bf16[2,1,256,12,64]{2,4,3,1,0:T(8,128)(2,1)S(1)} %get-tuple-element.1126), channel_id=1, source_target_pairs={{2,0},{4,2},{6,4},{8,6},{10,8},{12,10},{14,12},{16,14},{18,16},{20... | collective-permute-start | bytes 2359304 | tf_op jit(solution)/shard_map/while/body/eval_jaxpr/ppermute | solution.py:16
  253.1 14.2 %collective-permute-start = (bf16[2,1,256,12,64]{2,4,3,1,0:T(8,128)(2,1)S(1)}, bf16[2,1,256,12,64]{2,4,3,1,0:T(8,128)(2,1)S(1)}, u32[]{:S(2)}, u32[]{:S(2)}) collective-permute-start(bf16[2,1,256,12,64]{2,4,3,1,0:T(8,128)(2,1)S(1)} %get-tuple-element.1126), channel_id=1, source_target_pairs={{2,0},{4,2},{6,4},{8,6},{10,8},{12,10},{14,12},{16,14},{18,16},{20... | collective-permute-start | bytes 2359304 | tf_op jit(solution)/shard_map/while/body/eval_jaxpr/ppermute | solution.py:16
  267.3 14.2 %collective-permute-start = (bf16[2,1,256,12,64]{2,4,3,1,0:T(8,128)(2,1)S(1)}, bf16[2,1,256,12,64]{2,4,3,1,0:T(8,128)(2,1)S(1)}, u32[]{:S(2)}, u32[]{:S(2)}) collective-permute-start(bf16[2,1,256,12,64]{2,4,3,1,0:T(8,128)(2,1)S(1)} %get-tuple-element.1126), channel_id=1, source_target_pairs={{2,0},{4,2},{6,4},{8,6},{10,8},{12,10},{14,12},{16,14},{18,16},{20... | collective-permute-start | bytes 2359304 | tf_op jit(solution)/shard_map/while/body/eval_jaxpr/ppermute | solution.py:16
  281.6 14.2 %collective-permute-start = (bf16[2,1,256,12,64]{2,4,3,1,0:T(8,128)(2,1)S(1)}, bf16[2,1,256,12,64]{2,4,3,1,0:T(8,128)(2,1)S(1)}, u32[]{:S(2)}, u32[]{:S(2)}) collective-permute-start(bf16[2,1,256,12,64]{2,4,3,1,0:T(8,128)(2,1)S(1)} %get-tuple-element.1126), channel_id=1, source_target_pairs={{2,0},{4,2},{6,4},{8,6},{10,8},{12,10},{14,12},{16,14},{18,16},{20... | collective-permute-start | bytes 2359304 | tf_op jit(solution)/shard_map/while/body/eval_jaxpr/ppermute | solution.py:16
  297.8 15.6 %copy-start = (f32[1,256,767]{2,1,0:T(8,128)}, f32[1,256,767]{2,1,0:T(8,128)S(1)}, u32[]{:S(2)}) copy-start(f32[1,256,767]{2,1,0:T(8,128)S(1)} %get-tuple-element.931) | copy-start | bytes 2356228
  320.4 587.5 %reduce-scatter.5.cloned.1.call-start = ((), (), s32[]{:S(2)}) async-start(), calls=%async_computation.8 | async-start | bytes 5308416 | tf_op jit(solution)/shard_map/reduce_scatter | solution.py:260
  331.8 9.8 collective-permute-start.2
  331.8 18.3 %collective-permute-start.1 = (bf16[2,1,256,12,64]{2,4,3,1,0:T(8,128)(2,1)}, bf16[2,1,256,12,64]{2,4,3,1,0:T(8,128)(2,1)S(1)}, u32[]{:S(2)}, u32[]{:S(2)}) collective-permute-start(bf16[2,1,256,12,64]{2,4,3,1,0:T(8,128)(2,1)} %get-tuple-element.1183), channel_id=1, source_target_pairs={{2,0},{4,2},{6,4},{8,6},{10,8},{12,10},{14,12},{16,14},{18,16},{20... | collective-permute-start | bytes 2359304 | tf_op jit(solution)/shard_map/while/body/eval_jaxpr/ppermute | solution.py:16
  352.0 21.2 %collective-permute-start.2 = (bf16[2,1,256,12,64]{2,4,3,1,0:T(8,128)(2,1)}, bf16[2,1,256,12,64]{2,4,3,1,0:T(8,128)(2,1)}, u32[]{:S(2)}, u32[]{:S(2)}) collective-permute-start(bf16[2,1,256,12,64]{2,4,3,1,0:T(8,128)(2,1)} %convert_element_type.298), channel_id=1, source_target_pairs={{2,0},{4,2},{6,4},{8,6},{10,8},{12,10},{14,12},{16,14},{18,16},{20... | collective-permute-start | bytes 2359304 | tf_op jit(solution)/shard_map/while/body/eval_jaxpr/ppermute | solution.py:16
  363.4 18.3 %collective-permute-start.1 = (bf16[2,1,256,12,64]{2,4,3,1,0:T(8,128)(2,1)}, bf16[2,1,256,12,64]{2,4,3,1,0:T(8,128)(2,1)S(1)}, u32[]{:S(2)}, u32[]{:S(2)}) collective-permute-start(bf16[2,1,256,12,64]{2,4,3,1,0:T(8,128)(2,1)} %get-tuple-element.1183), channel_id=1, source_target_pairs={{2,0},{4,2},{6,4},{8,6},{10,8},{12,10},{14,12},{16,14},{18,16},{20... | collective-permute-start | bytes 2359304 | tf_op jit(solution)/shard_map/while/body/eval_jaxpr/ppermute | solution.py:16
  383.6 21.2 %collective-permute-start.2 = (bf16[2,1,256,12,64]{2,4,3,1,0:T(8,128)(2,1)}, bf16[2,1,256,12,64]{2,4,3,1,0:T(8,128)(2,1)}, u32[]{:S(2)}, u32[]{:S(2)}) collective-permute-start(bf16[2,1,256,12,64]{2,4,3,1,0:T(8,128)(2,1)} %convert_element_type.298), channel_id=1, source_target_pairs={{2,0},{4,2},{6,4},{8,6},{10,8},{12,10},{14,12},{16,14},{18,16},{20... | collective-permute-start | bytes 2359304 | tf_op jit(solution)/shard_map/while/body/eval_jaxpr/ppermute | solution.py:16
  394.9 18.3 %collective-permute-start.1 = (bf16[2,1,256,12,64]{2,4,3,1,0:T(8,128)(2,1)}, bf16[2,1,256,12,64]{2,4,3,1,0:T(8,128)(2,1)S(1)}, u32[]{:S(2)}, u32[]{:S(2)}) collective-permute-start(bf16[2,1,256,12,64]{2,4,3,1,0:T(8,128)(2,1)} %get-tuple-element.1183), channel_id=1, source_target_pairs={{2,0},{4,2},{6,4},{8,6},{10,8},{12,10},{14,12},{16,14},{18,16},{20... | collective-permute-start | bytes 2359304 | tf_op jit(solution)/shard_map/while/body/eval_jaxpr/ppermute | solution.py:16
  415.1 21.2 %collective-permute-start.2 = (bf16[2,1,256,12,64]{2,4,3,1,0:T(8,128)(2,1)}, bf16[2,1,256,12,64]{2,4,3,1,0:T(8,128)(2,1)}, u32[]{:S(2)}, u32[]{:S(2)}) collective-permute-start(bf16[2,1,256,12,64]{2,4,3,1,0:T(8,128)(2,1)} %convert_element_type.298), channel_id=1, source_target_pairs={{2,0},{4,2},{6,4},{8,6},{10,8},{12,10},{14,12},{16,14},{18,16},{20... | collective-permute-start | bytes 2359304 | tf_op jit(solution)/shard_map/while/body/eval_jaxpr/ppermute | solution.py:16
  426.5 18.3 %collective-permute-start.1 = (bf16[2,1,256,12,64]{2,4,3,1,0:T(8,128)(2,1)}, bf16[2,1,256,12,64]{2,4,3,1,0:T(8,128)(2,1)S(1)}, u32[]{:S(2)}, u32[]{:S(2)}) collective-permute-start(bf16[2,1,256,12,64]{2,4,3,1,0:T(8,128)(2,1)} %get-tuple-element.1183), channel_id=1, source_target_pairs={{2,0},{4,2},{6,4},{8,6},{10,8},{12,10},{14,12},{16,14},{18,16},{20... | collective-permute-start | bytes 2359304 | tf_op jit(solution)/shard_map/while/body/eval_jaxpr/ppermute | solution.py:16
  446.6 21.2 %collective-permute-start.2 = (bf16[2,1,256,12,64]{2,4,3,1,0:T(8,128)(2,1)}, bf16[2,1,256,12,64]{2,4,3,1,0:T(8,128)(2,1)}, u32[]{:S(2)}, u32[]{:S(2)}) collective-permute-start(bf16[2,1,256,12,64]{2,4,3,1,0:T(8,128)(2,1)} %convert_element_type.298), channel_id=1, source_target_pairs={{2,0},{4,2},{6,4},{8,6},{10,8},{12,10},{14,12},{16,14},{18,16},{20... | collective-permute-start | bytes 2359304 | tf_op jit(solution)/shard_map/while/body/eval_jaxpr/ppermute | solution.py:16
  458.0 18.3 %collective-permute-start.1 = (bf16[2,1,256,12,64]{2,4,3,1,0:T(8,128)(2,1)}, bf16[2,1,256,12,64]{2,4,3,1,0:T(8,128)(2,1)S(1)}, u32[]{:S(2)}, u32[]{:S(2)}) collective-permute-start(bf16[2,1,256,12,64]{2,4,3,1,0:T(8,128)(2,1)} %get-tuple-element.1183), channel_id=1, source_target_pairs={{2,0},{4,2},{6,4},{8,6},{10,8},{12,10},{14,12},{16,14},{18,16},{20... | collective-permute-start | bytes 2359304 | tf_op jit(solution)/shard_map/while/body/eval_jaxpr/ppermute | solution.py:16
  478.2 14.3 %collective-permute-start.2 = (bf16[2,1,256,12,64]{2,4,3,1,0:T(8,128)(2,1)}, bf16[2,1,256,12,64]{2,4,3,1,0:T(8,128)(2,1)}, u32[]{:S(2)}, u32[]{:S(2)}) collective-permute-start(bf16[2,1,256,12,64]{2,4,3,1,0:T(8,128)(2,1)} %convert_element_type.298), channel_id=1, source_target_pairs={{2,0},{4,2},{6,4},{8,6},{10,8},{12,10},{14,12},{16,14},{18,16},{20... | collective-permute-start | bytes 2359304 | tf_op jit(solution)/shard_map/while/body/eval_jaxpr/ppermute | solution.py:16
  482.7 18.3 %collective-permute-start.1 = (bf16[2,1,256,12,64]{2,4,3,1,0:T(8,128)(2,1)}, bf16[2,1,256,12,64]{2,4,3,1,0:T(8,128)(2,1)S(1)}, u32[]{:S(2)}, u32[]{:S(2)}) collective-permute-start(bf16[2,1,256,12,64]{2,4,3,1,0:T(8,128)(2,1)} %get-tuple-element.1183), channel_id=1, source_target_pairs={{2,0},{4,2},{6,4},{8,6},{10,8},{12,10},{14,12},{16,14},{18,16},{20... | collective-permute-start | bytes 2359304 | tf_op jit(solution)/shard_map/while/body/eval_jaxpr/ppermute | solution.py:16
  502.9 14.3 %collective-permute-start.2 = (bf16[2,1,256,12,64]{2,4,3,1,0:T(8,128)(2,1)}, bf16[2,1,256,12,64]{2,4,3,1,0:T(8,128)(2,1)}, u32[]{:S(2)}, u32[]{:S(2)}) collective-permute-start(bf16[2,1,256,12,64]{2,4,3,1,0:T(8,128)(2,1)} %convert_element_type.298), channel_id=1, source_target_pairs={{2,0},{4,2},{6,4},{8,6},{10,8},{12,10},{14,12},{16,14},{18,16},{20... | collective-permute-start | bytes 2359304 | tf_op jit(solution)/shard_map/while/body/eval_jaxpr/ppermute | solution.py:16
  507.4 18.3 %collective-permute-start.1 = (bf16[2,1,256,12,64]{2,4,3,1,0:T(8,128)(2,1)}, bf16[2,1,256,12,64]{2,4,3,1,0:T(8,128)(2,1)S(1)}, u32[]{:S(2)}, u32[]{:S(2)}) collective-permute-start(bf16[2,1,256,12,64]{2,4,3,1,0:T(8,128)(2,1)} %get-tuple-element.1183), channel_id=1, source_target_pairs={{2,0},{4,2},{6,4},{8,6},{10,8},{12,10},{14,12},{16,14},{18,16},{20... | collective-permute-start | bytes 2359304 | tf_op jit(solution)/shard_map/while/body/eval_jaxpr/ppermute | solution.py:16
  527.5 14.3 %collective-permute-start.2 = (bf16[2,1,256,12,64]{2,4,3,1,0:T(8,128)(2,1)}, bf16[2,1,256,12,64]{2,4,3,1,0:T(8,128)(2,1)}, u32[]{:S(2)}, u32[]{:S(2)}) collective-permute-start(bf16[2,1,256,12,64]{2,4,3,1,0:T(8,128)(2,1)} %convert_element_type.298), channel_id=1, source_target_pairs={{2,0},{4,2},{6,4},{8,6},{10,8},{12,10},{14,12},{16,14},{18,16},{20... | collective-permute-start | bytes 2359304 | tf_op jit(solution)/shard_map/while/body/eval_jaxpr/ppermute | solution.py:16
  532.0 18.3 %collective-permute-start.1 = (bf16[2,1,256,12,64]{2,4,3,1,0:T(8,128)(2,1)}, bf16[2,1,256,12,64]{2,4,3,1,0:T(8,128)(2,1)S(1)}, u32[]{:S(2)}, u32[]{:S(2)}) collective-permute-start(bf16[2,1,256,12,64]{2,4,3,1,0:T(8,128)(2,1)} %get-tuple-element.1183), channel_id=1, source_target_pairs={{2,0},{4,2},{6,4},{8,6},{10,8},{12,10},{14,12},{16,14},{18,16},{20... | collective-permute-start | bytes 2359304 | tf_op jit(solution)/shard_map/while/body/eval_jaxpr/ppermute | solution.py:16
  552.2 14.3 %collective-permute-start.2 = (bf16[2,1,256,12,64]{2,4,3,1,0:T(8,128)(2,1)}, bf16[2,1,256,12,64]{2,4,3,1,0:T(8,128)(2,1)}, u32[]{:S(2)}, u32[]{:S(2)}) collective-permute-start(bf16[2,1,256,12,64]{2,4,3,1,0:T(8,128)(2,1)} %convert_element_type.298), channel_id=1, source_target_pairs={{2,0},{4,2},{6,4},{8,6},{10,8},{12,10},{14,12},{16,14},{18,16},{20... | collective-permute-start | bytes 2359304 | tf_op jit(solution)/shard_map/while/body/eval_jaxpr/ppermute | solution.py:16
  556.7 18.3 %collective-permute-start.1 = (bf16[2,1,256,12,64]{2,4,3,1,0:T(8,128)(2,1)}, bf16[2,1,256,12,64]{2,4,3,1,0:T(8,128)(2,1)S(1)}, u32[]{:S(2)}, u32[]{:S(2)}) collective-permute-start(bf16[2,1,256,12,64]{2,4,3,1,0:T(8,128)(2,1)} %get-tuple-element.1183), channel_id=1, source_target_pairs={{2,0},{4,2},{6,4},{8,6},{10,8},{12,10},{14,12},{16,14},{18,16},{20... | collective-permute-start | bytes 2359304 | tf_op jit(solution)/shard_map/while/body/eval_jaxpr/ppermute | solution.py:16
  576.9 14.3 %collective-permute-start.2 = (bf16[2,1,256,12,64]{2,4,3,1,0:T(8,128)(2,1)}, bf16[2,1,256,12,64]{2,4,3,1,0:T(8,128)(2,1)}, u32[]{:S(2)}, u32[]{:S(2)}) collective-permute-start(bf16[2,1,256,12,64]{2,4,3,1,0:T(8,128)(2,1)} %convert_element_type.298), channel_id=1, source_target_pairs={{2,0},{4,2},{6,4},{8,6},{10,8},{12,10},{14,12},{16,14},{18,16},{20... | collective-permute-start | bytes 2359304 | tf_op jit(solution)/shard_map/while/body/eval_jaxpr/ppermute | solution.py:16
  581.4 18.3 %collective-permute-start.1 = (bf16[2,1,256,12,64]{2,4,3,1,0:T(8,128)(2,1)}, bf16[2,1,256,12,64]{2,4,3,1,0:T(8,128)(2,1)S(1)}, u32[]{:S(2)}, u32[]{:S(2)}) collective-permute-start(bf16[2,1,256,12,64]{2,4,3,1,0:T(8,128)(2,1)} %get-tuple-element.1183), channel_id=1, source_target_pairs={{2,0},{4,2},{6,4},{8,6},{10,8},{12,10},{14,12},{16,14},{18,16},{20... | collective-permute-start | bytes 2359304 | tf_op jit(solution)/shard_map/while/body/eval_jaxpr/ppermute | solution.py:16
  601.6 14.3 %collective-permute-start.2 = (bf16[2,1,256,12,64]{2,4,3,1,0:T(8,128)(2,1)}, bf16[2,1,256,12,64]{2,4,3,1,0:T(8,128)(2,1)}, u32[]{:S(2)}, u32[]{:S(2)}) collective-permute-start(bf16[2,1,256,12,64]{2,4,3,1,0:T(8,128)(2,1)} %convert_element_type.298), channel_id=1, source_target_pairs={{2,0},{4,2},{6,4},{8,6},{10,8},{12,10},{14,12},{16,14},{18,16},{20... | collective-permute-start | bytes 2359304 | tf_op jit(solution)/shard_map/while/body/eval_jaxpr/ppermute | solution.py:16
  606.1 18.3 %collective-permute-start.1 = (bf16[2,1,256,12,64]{2,4,3,1,0:T(8,128)(2,1)}, bf16[2,1,256,12,64]{2,4,3,1,0:T(8,128)(2,1)S(1)}, u32[]{:S(2)}, u32[]{:S(2)}) collective-permute-start(bf16[2,1,256,12,64]{2,4,3,1,0:T(8,128)(2,1)} %get-tuple-element.1183), channel_id=1, source_target_pairs={{2,0},{4,2},{6,4},{8,6},{10,8},{12,10},{14,12},{16,14},{18,16},{20... | collective-permute-start | bytes 2359304 | tf_op jit(solution)/shard_map/while/body/eval_jaxpr/ppermute | solution.py:16
  626.2 14.3 %collective-permute-start.2 = (bf16[2,1,256,12,64]{2,4,3,1,0:T(8,128)(2,1)}, bf16[2,1,256,12,64]{2,4,3,1,0:T(8,128)(2,1)}, u32[]{:S(2)}, u32[]{:S(2)}) collective-permute-start(bf16[2,1,256,12,64]{2,4,3,1,0:T(8,128)(2,1)} %convert_element_type.298), channel_id=1, source_target_pairs={{2,0},{4,2},{6,4},{8,6},{10,8},{12,10},{14,12},{16,14},{18,16},{20... | collective-permute-start | bytes 2359304 | tf_op jit(solution)/shard_map/while/body/eval_jaxpr/ppermute | solution.py:16
  630.7 18.3 %collective-permute-start.1 = (bf16[2,1,256,12,64]{2,4,3,1,0:T(8,128)(2,1)}, bf16[2,1,256,12,64]{2,4,3,1,0:T(8,128)(2,1)S(1)}, u32[]{:S(2)}, u32[]{:S(2)}) collective-permute-start(bf16[2,1,256,12,64]{2,4,3,1,0:T(8,128)(2,1)} %get-tuple-element.1183), channel_id=1, source_target_pairs={{2,0},{4,2},{6,4},{8,6},{10,8},{12,10},{14,12},{16,14},{18,16},{20... | collective-permute-start | bytes 2359304 | tf_op jit(solution)/shard_map/while/body/eval_jaxpr/ppermute | solution.py:16
  650.9 14.3 %collective-permute-start.2 = (bf16[2,1,256,12,64]{2,4,3,1,0:T(8,128)(2,1)}, bf16[2,1,256,12,64]{2,4,3,1,0:T(8,128)(2,1)}, u32[]{:S(2)}, u32[]{:S(2)}) collective-permute-start(bf16[2,1,256,12,64]{2,4,3,1,0:T(8,128)(2,1)} %convert_element_type.298), channel_id=1, source_target_pairs={{2,0},{4,2},{6,4},{8,6},{10,8},{12,10},{14,12},{16,14},{18,16},{20... | collective-permute-start | bytes 2359304 | tf_op jit(solution)/shard_map/while/body/eval_jaxpr/ppermute | solution.py:16
  655.4 18.3 %collective-permute-start.1 = (bf16[2,1,256,12,64]{2,4,3,1,0:T(8,128)(2,1)}, bf16[2,1,256,12,64]{2,4,3,1,0:T(8,128)(2,1)S(1)}, u32[]{:S(2)}, u32[]{:S(2)}) collective-permute-start(bf16[2,1,256,12,64]{2,4,3,1,0:T(8,128)(2,1)} %get-tuple-element.1183), channel_id=1, source_target_pairs={{2,0},{4,2},{6,4},{8,6},{10,8},{12,10},{14,12},{16,14},{18,16},{20... | collective-permute-start | bytes 2359304 | tf_op jit(solution)/shard_map/while/body/eval_jaxpr/ppermute | solution.py:16
  675.6 14.3 %collective-permute-start.2 = (bf16[2,1,256,12,64]{2,4,3,1,0:T(8,128)(2,1)}, bf16[2,1,256,12,64]{2,4,3,1,0:T(8,128)(2,1)}, u32[]{:S(2)}, u32[]{:S(2)}) collective-permute-start(bf16[2,1,256,12,64]{2,4,3,1,0:T(8,128)(2,1)} %convert_element_type.298), channel_id=1, source_target_pairs={{2,0},{4,2},{6,4},{8,6},{10,8},{12,10},{14,12},{16,14},{18,16},{20... | collective-permute-start | bytes 2359304 | tf_op jit(solution)/shard_map/while/body/eval_jaxpr/ppermute | solution.py:16
  680.1 18.3 %collective-permute-start.1 = (bf16[2,1,256,12,64]{2,4,3,1,0:T(8,128)(2,1)}, bf16[2,1,256,12,64]{2,4,3,1,0:T(8,128)(2,1)S(1)}, u32[]{:S(2)}, u32[]{:S(2)}) collective-permute-start(bf16[2,1,256,12,64]{2,4,3,1,0:T(8,128)(2,1)} %get-tuple-element.1183), channel_id=1, source_target_pairs={{2,0},{4,2},{6,4},{8,6},{10,8},{12,10},{14,12},{16,14},{18,16},{20... | collective-permute-start | bytes 2359304 | tf_op jit(solution)/shard_map/while/body/eval_jaxpr/ppermute | solution.py:16
  700.3 14.3 %collective-permute-start.2 = (bf16[2,1,256,12,64]{2,4,3,1,0:T(8,128)(2,1)}, bf16[2,1,256,12,64]{2,4,3,1,0:T(8,128)(2,1)}, u32[]{:S(2)}, u32[]{:S(2)}) collective-permute-start(bf16[2,1,256,12,64]{2,4,3,1,0:T(8,128)(2,1)} %convert_element_type.298), channel_id=1, source_target_pairs={{2,0},{4,2},{6,4},{8,6},{10,8},{12,10},{14,12},{16,14},{18,16},{20... | collective-permute-start | bytes 2359304 | tf_op jit(solution)/shard_map/while/body/eval_jaxpr/ppermute | solution.py:16
  704.8 18.3 %collective-permute-start.1 = (bf16[2,1,256,12,64]{2,4,3,1,0:T(8,128)(2,1)}, bf16[2,1,256,12,64]{2,4,3,1,0:T(8,128)(2,1)S(1)}, u32[]{:S(2)}, u32[]{:S(2)}) collective-permute-start(bf16[2,1,256,12,64]{2,4,3,1,0:T(8,128)(2,1)} %get-tuple-element.1183), channel_id=1, source_target_pairs={{2,0},{4,2},{6,4},{8,6},{10,8},{12,10},{14,12},{16,14},{18,16},{20... | collective-permute-start | bytes 2359304 | tf_op jit(solution)/shard_map/while/body/eval_jaxpr/ppermute | solution.py:16
  723.9 14.2 %copy-start.7 = (f32[256,767]{1,0:T(8,128)S(1)}, f32[256,767]{1,0:T(8,128)}, u32[]{:S(2)}) copy-start(f32[256,767]{1,0:T(8,128)} %copy-done.6) | copy-start | bytes 2356228
  723.9 14.3 %copy-start.15 = (f32[256,1]{1,0:T(8,128)S(1)}, f32[256,1]{1,0:T(8,128)}, u32[]{:S(2)}) copy-start(f32[256,1]{1,0:T(8,128)} %copy-done.14) | copy-start | bytes 3076
  723.9 14.3 %copy-start.24 = (f32[768]{0:T(1024)S(1)}, f32[768]{0:T(1024)}, u32[]{:S(2)}) copy-start(f32[768]{0:T(1024)} %copy-done.23) | copy-start | bytes 9220
  723.9 14.3 %copy-start.37 = (f32[256]{0:T(256)S(1)}, f32[256]{0:T(256)}, u32[]{:S(2)}) copy-start(f32[256]{0:T(256)} %copy-done.36) | copy-start | bytes 3076
  724.0 14.1 %collective-permute-start.3 = (bf16[2,1,256,12,64]{2,4,3,1,0:T(8,128)(2,1)S(1)}, bf16[2,1,256,12,64]{2,4,3,1,0:T(8,128)(2,1)S(1)}, u32[]{:S(2)}, u32[]{:S(2)}) collective-permute-start(bf16[2,1,256,12,64]{2,4,3,1,0:T(8,128)(2,1)S(1)} %convert_element_type.188), channel_id=1, source_target_pairs={{2,0},{4,2},{6,4},{8,6},{10,8},{12,10},{14,12},{16,14},{18,16},{20... | collective-permute-start | bytes 2359304 | tf_op jit(solution)/shard_map/ppermute | solution.py:16
  741.3 229.6 %reduce-scatter.11.cloned.1.call-start = ((), (), s32[]{:S(2)}) async-start(), calls=%async_computation.11 | async-start | bytes 7077888 | tf_op jit(solution)/shard_map/reduce_scatter | solution.py:272
  748.7 285.2 %reduce-scatter.9.cloned.1.call-start = ((), (), s32[]{:S(2)}) async-start(), calls=%async_computation.10 | async-start | bytes 7077888 | tf_op jit(solution)/shard_map/reduce_scatter | solution.py:269
  (33 other events, 128.2 us)
Sparse Core Ops, SparseCore 0:
  9.5 52.0 all-gather.6
  63.2 22.7 all-gather.8
  87.5 62.6 all-gather.10
  151.6 62.6 all-gather.12
  320.5 60.3 reduce-scatter.6
  741.4 166.4 reduce-scatter.4
  910.8 60.0 reduce-scatter.10
  973.8 60.0 reduce-scatter.8
where the time goes:
time: 1350 us; the launch traced here: 1340 us
  waiting for transfers between devices  489 us (36%)
  blocking collectives  432 us (32%)
  starting transfers between devices  174 us (13%)
  loops' own time  80.4 us (6%)
  other arithmetic  68.6 us (5%)
  matrix products  54.5 us (4%)
  local copies, waits for them, and re-layouts  24.1 us (2%)
  between operations  18.1 us (1%)
    ppermute x46, waiting for transfers between devices, passed_along(): return lax.ppermute(block, axis, route)  307 us
    psum x1, blocking collectives, shards(): lax.psum((shard_sums[0], shard_sums[1], shard_sums[2], shard_sums[3], sha...  300 us
    ppermute x46, starting transfers between devices, passed_along(): return lax.ppermute(block, axis, route)  173 us
    unnamed x1, blocking collectives  122 us
    reduce_scatter x1, waiting for transfers between devices, shards(): lax.psum_scatter(grad_down.astype(jnp.bfloat16), 'fsdp', scatter_dimensio...  63 us
    reduce_scatter x1, waiting for transfers between devices, shards(): lax.psum_scatter(grad_up.astype(jnp.bfloat16), 'fsdp', scatter_dimension=...  63 us
    another operation x1, loops' own time, circle_forward(): held, state = lax.fori_loop(1, circle_size, one_turn, (kv_block, state))  40 us
    another operation x1, loops' own time, circle_backward(): lax.fori_loop(1, circle_size, one_turn, (kv_block, grad_query, held_grads))  39.8 us
  transfers between devices with their start and end apart: 54, of which 50 were waited for; matrix products, arithmetic and copies ran while one was open for 10% of the time, Pallas kernels for 0%

commit v1 on v0

v1 whole, which is shorter than its diff:
```python
import functools

import jax
import jax.numpy as jnp
from jax import lax
from jax.experimental import pallas as pl
from jax.experimental.pallas import tpu as pltpu
from jax.sharding import PartitionSpec as P

F32 = jnp.float32
BF16 = jnp.bfloat16
MESH = pl.DeviceIdType.MESH
NT = (((1,), (1,)), ((), ()))
TN = (((0,), (0,)), ((), ()))
EPS = 1e-05
MASKED = -1e30
LOG2E = 1.4426950408889634
SCALE = 0.125
GROUPS = 4
GH = 3
HD = 64
SUB = 1024
VLIM = 60 * 1024 * 1024

VM = pl.BlockSpec(memory_space=pltpu.VMEM)
SM = pl.BlockSpec(memory_space=pltpu.SMEM)
ANY = pl.BlockSpec(memory_space=pl.ANY)
DMA = pltpu.SemaphoreType.DMA


def dot(a, b):
    return jnp.dot(a, b, preferred_element_type=F32)


def dg(a, b, dims):
    return lax.dot_general(a, b, dims, preferred_element_type=F32)


def rcopy(src, dst, send, recv, dev):
    return pltpu.make_async_remote_copy(
        src_ref=src, dst_ref=dst, send_sem=send, recv_sem=recv, device_id=dev, device_id_type=MESH
    )


class Place:
    def __init__(self, n):
        self.n = n
        self.m = n // GROUPS
        self.chips = self.m // 2
        c = lax.axis_index("ctx")
        self.x = lax.axis_index("fsdp")
        self.a = c // self.m
        self.b = c % self.m
        self.chip = self.b // 2
        self.k = self.b % 2

    def xpeer(self):
        return {"fsdp": 1 - self.x}

    def sibling(self):
        return {"ctx": self.a * self.m + self.chip * 2 + 1 - self.k}

    def on_chip(self, chip):
        return {"ctx": self.a * self.m + chip * 2 + self.k}

    def on_line(self, a):
        return {"ctx": a * self.m + self.b}


def greet(p, xpeer=False, sibling=False, chips=False, line=False):
    bar = pltpu.get_barrier_semaphore()
    count = 0
    if xpeer:
        pl.semaphore_signal(bar, inc=1, device_id=p.xpeer(), device_id_type=MESH)
        count += 1
    if sibling:
        pl.semaphore_signal(bar, inc=1, device_id=p.sibling(), device_id_type=MESH)
        count += 1
    if chips:
        for d in range(1, p.chips):
            pl.semaphore_signal(
                bar, inc=1, device_id=p.on_chip((p.chip + d) % p.chips), device_id_type=MESH
            )
            count += 1
    if line:
        for d in range(1, GROUPS):
            pl.semaphore_signal(
                bar, inc=1, device_id=p.on_line((p.a + d) % GROUPS), device_id_type=MESH
            )
            count += 1
    return lambda: pl.semaphore_wait(bar, count)


def ext_of(v):
    last = lax.broadcasted_iota(jnp.int32, v.shape, 1) == v.shape[1] - 1
    return jnp.where(last, -jnp.sum(v, axis=1, keepdims=True), v)


def inv_rms(u):
    return lax.rsqrt(jnp.mean(u * u, axis=1, keepdims=True) + EPS)


def crms_back(u, inv, gain, dy):
    dx = dy * gain
    du = inv * (dx - u * (inv * inv * jnp.mean(dx * u, axis=1, keepdims=True)))
    width = u.shape[1]
    last = lax.broadcasted_iota(jnp.int32, u.shape, 1) == width - 1
    return jnp.where(last, 0.0, du - du[:, width - 1 :])


def low_half(shape):
    return lax.broadcasted_iota(jnp.int32, shape, len(shape) - 1) < HD


def pack_tail(t):
    half = t.shape[0] // 2
    top, bottom = t[:half], t[half:]
    return jnp.where(low_half(top.shape), pltpu.roll(bottom, HD, 1), top)


def unpack_tail(t):
    low = low_half(t.shape)
    zero = jnp.zeros_like(t)
    return jnp.where(low, zero, t), jnp.where(low, zero, pltpu.roll(t, HD, 1))


def project_kernel(n, rp, gains, wg, wo, h1, q3, kv, wa, woa, gfull, ss, rs, ls, hs, hr, ks, kr, fs):
    p = Place(n)
    rows, width = rp.shape
    half = width // 2
    ready = greet(p, xpeer=True, sibling=True, chips=True, line=True)
    own = pltpu.make_async_copy(
        wg.at[p.a], wa.at[pl.ds(pl.multiple_of(p.x * half, half), half)], ls.at[0]
    )
    own.start()
    zero_rows = jnp.zeros((HD, width), BF16)
    for g in range(GROUPS):
        woa[pl.ds(g * 256 + 128, HD), :] = zero_rows
    local = []
    for i in range(2):
        g = p.x * 2 + i
        for j, (src, size, dst) in enumerate(((0, 128, 0), (128, 64, 192))):
            c = pltpu.make_async_copy(
                wo.at[pl.ds(i * 192 + src, size)],
                woa.at[pl.ds(pl.multiple_of(g * 256 + dst, 64), size)],
                ls.at[1 + 2 * i + j],
            )
            c.start()
            local.append(c)
    gfull[p.x] = gains[...]
    u = ext_of(rp[...].astype(F32))
    normed = u * inv_rms(u)
    ready()
    xg = rcopy(gains, gfull.at[p.x], ss.at[0], rs.at[0], p.xpeer())
    xg.start()
    xw = rcopy(
        wg.at[p.a],
        wa.at[pl.ds(pl.multiple_of(p.x * half, half), half)],
        ss.at[1],
        rs.at[1],
        p.xpeer(),
    )
    xw.start()
    xg.wait()
    gain = jnp.concatenate([gfull[0, 0:1, :], gfull[1, 0:1, :]], axis=1)
    h1[p.a] = (normed * gain).astype(BF16)

    def line_copy(block, dst, sem):
        return rcopy(h1.at[block], h1.at[block], hs.at[sem], hr.at[block], p.on_line(dst))

    def kv_rows(block, b):
        return kv.at[pl.ds(pl.multiple_of((block * p.m + b) * rows, rows), rows)]

    def kv_copy(block, b, dev, send):
        r = kv_rows(block, b)
        return rcopy(r, r, send, kr.at[block, b], dev)

    @pl.when(p.a < GROUPS - 1)
    def _():
        line_copy(p.a, p.a + 1, 0).start()

    @pl.when(p.a > 0)
    def _():
        line_copy(p.a, p.a - 1, 1).start()

    xo = []
    for i in range(2):
        g = p.x * 2 + i
        for j, (src, size, dst) in enumerate(((0, 128, 0), (128, 64, 192))):
            c = rcopy(
                wo.at[pl.ds(i * 192 + src, size)],
                woa.at[pl.ds(pl.multiple_of(g * 256 + dst, 64), size)],
                ss.at[2 + 2 * i + j],
                rs.at[2 + 2 * i + j],
                p.xpeer(),
            )
            c.start()
            xo.append(c)
    own.wait()
    xw.wait()

    def produce(block):
        y = dot(h1[block], wa[...]).astype(BF16)
        low = low_half((rows, 128))
        zero = jnp.zeros((rows, 128), BF16)
        at = pl.ds(pl.multiple_of(block * rows, rows), rows)
        q3[0, at, :] = jnp.where(low, y[:, :128], zero)
        q3[1, at, :] = jnp.where(low, zero, y[:, :128])
        q3[2, at, :] = y[:, 128:256]
        kv[pl.ds(pl.multiple_of((block * p.m + p.b) * rows, rows), rows), :] = y[:, 256:]
        for d in range(1, p.chips):
            kv_copy(block, p.b, p.on_chip((p.chip + d) % p.chips), ks.at[block, d]).start()
        kv_copy(block, p.b, p.sibling(), ks.at[block, 0]).start()

    def pass_on(block):
        for d in range(1, p.chips):
            b = ((p.chip + d) % p.chips) * 2 + p.k
            kv_copy(block, b, p.sibling(), fs.at[block, d]).wait_recv()
            kv_copy(block, b, p.sibling(), fs.at[block, d]).start()

    produce(p.a)
    for s in range(1, GROUPS):

        @pl.when(p.a - s >= 0)
        def _():
            line_copy(p.a - s, p.a, 0).wait_recv()

            @pl.when(p.a < GROUPS - 1)
            def _():
                line_copy(p.a - s, p.a + 1, 2 * s).start()

        @pl.when(p.a + s < GROUPS)
        def _():
            line_copy(p.a + s, p.a, 0).wait_recv()

            @pl.when(p.a > 0)
            def _():
                line_copy(p.a + s, p.a - 1, 2 * s + 1).start()

        @pl.when(p.a - s >= 0)
        def _():
            produce(p.a - s)

        @pl.when(p.a + s < GROUPS)
        def _():
            produce(p.a + s)

        @pl.when(p.a - s + 1 >= 0)
        def _():
            pass_on(p.a - s + 1)

        if s > 1:

            @pl.when(p.a + s - 1 < GROUPS)
            def _():
                pass_on(p.a + s - 1)

    @pl.when(p.a - GROUPS + 1 >= 0)
    def _():
        pass_on(p.a - GROUPS + 1)

    @pl.when(p.a + GROUPS - 1 < GROUPS)
    def _():
        pass_on(p.a + GROUPS - 1)

    for block in range(GROUPS):
        kv_copy(block, p.b, p.sibling(), ks.at[block, 0]).wait_send()
        sib = p.chip * 2 + 1 - p.k
        kv_copy(block, sib, p.sibling(), ks.at[block, 0]).wait_recv()
        for d in range(1, p.chips):
            kv_copy(block, p.b, p.sibling(), ks.at[block, d]).wait_send()
            b = ((p.chip + d) % p.chips) * 2
            kv_copy(block, b + p.k, p.sibling(), fs.at[block, d]).wait_send()
            kv_copy(block, b + 1 - p.k, p.sibling(), fs.at[block, d]).wait_recv()
    for s in range(GROUPS):

        @pl.when((p.a - s >= 0) & (p.a < GROUPS - 1))
        def _():
            line_copy(p.a - s, p.a + 1, 2 * s).wait_send()

        @pl.when((p.a + s < GROUPS) & (p.a > 0))
        def _():
            line_copy(p.a + s, p.a - 1, 2 * s + 1).wait_send()

    for c in xo:
        c.wait()
    for c in local:
        c.wait()


def project(n, rp, gains, wg, wo):
    rows, width = rp.shape
    m = n // GROUPS
    lanes = wg.shape[2]
    sds = jax.ShapeDtypeStruct
    return pl.pallas_call(
        functools.partial(project_kernel, n),
        name="project",
        out_shape=(
            sds((GROUPS, rows, width), BF16),
            sds((GH, GROUPS * rows, 128), BF16),
            sds((n * rows, 384), BF16),
            sds((width, lanes), BF16),
            sds((GROUPS * 256, width), BF16),
            sds((2,) + gains.shape, F32),
        ),
        in_specs=[VM, VM, ANY, VM],
        out_specs=[VM] * 6,
        scratch_shapes=[
            DMA((6,)),
            DMA((6,)),
            DMA((5,)),
            DMA((2 * GROUPS,)),
            DMA((GROUPS,)),
            DMA((GROUPS, m // 2)),
            DMA((GROUPS, m)),
            DMA((GROUPS, m // 2)),
        ],
        compiler_params=pltpu.CompilerParams(
            collective_id=0, has_side_effects=True, vmem_limit_bytes=VLIM
        ),
    )(rp, gains, wg, wo)


def key_steps(z, keys):
    subs = keys // min(SUB, keys)
    return [(z, s) for s in range(subs)] + [(c, s) for c in range(z) for s in range(subs)]


def causal(shape, sub, size, first_query):
    col = lax.broadcasted_iota(jnp.int32, shape, 1) + sub * size
    row = lax.broadcasted_iota(jnp.int32, shape, 0) + first_query
    return col <= row


def attend_kernel(meta, q3, kv, att, o3, l3):
    rows = q3.shape[1] // GROUPS
    keys = kv.shape[0] // GROUPS
    size = min(SUB, keys)
    first_query = meta[0] * rows
    dead = jnp.where(meta[1] > keys, 0.0, MASKED).astype(F32)

    def head(h, carry):
        kt = pl.multiple_of(128 * (h // 2), 128)
        vt = pl.multiple_of(128 * (2 - h // 2 - (h + 1) % 2 * 0), 128)
        vt = pl.multiple_of(jnp.where(h == 2, 128, 256), 128)
        for z in range(GROUPS):
            q = q3[h, pl.ds(z * rows, rows), :]
            top = total = acc = None
            for c, s in key_steps(z, keys):
                at = pl.ds(c * keys + s * size, size)
                scores = dg(q, kv[at, pl.ds(kt, 128)], NT) * (SCALE * LOG2E)
                if c == z:
                    scores = jnp.where(
                        causal(scores.shape, s, size, first_query), scores, MASKED
                    )
                bias = dead if c > 0 else 0.0
                if c == z and c > 0:
                    bias = dead
                here = jnp.max(scores, axis=1, keepdims=True) + bias
                newest = here if top is None else jnp.maximum(top, here)
                weights = jnp.exp2(scores - (newest - bias))
                sums = jnp.sum(weights, axis=1, keepdims=True)
                part = dot(weights.astype(BF16), kv[at, pl.ds(vt, 128)])
                if top is None:
                    total, acc = sums, part
                else:
                    shrink = jnp.exp2(top - newest)
                    total = total * shrink + sums
                    acc = acc * shrink + part
                top = newest
            o3[h, pl.ds(z * rows, rows), :] = acc / total
            l3[h, pl.ds(z * rows, rows), :] = jnp.broadcast_to(top + jnp.log2(total), (rows, 128))
        return carry

    lax.fori_loop(0, GH, head, 0)
    for z in range(GROUPS):
        at = pl.ds(z * rows, rows)
        both = jnp.where(low_half((rows, 128)), o3[0, at, :], o3[1, at, :])
        att[z, 0:rows, :] = both.astype(BF16)
        att[z, rows : rows + rows // 2, :] = pack_tail(o3[2, at, :]).astype(BF16)


def attend(meta, q3, kv):
    sds = jax.ShapeDtypeStruct
    rows = q3.shape[1] // GROUPS
    return pl.pallas_call(
        attend_kernel,
        name="attend",
        out_shape=(
            sds((GROUPS, rows * 3 // 2, 128), BF16),
            sds(q3.shape, F32),
            sds(q3.shape, F32),
        ),
        in_specs=[SM, VM, VM],
        out_specs=[VM] * 3,
        compiler_params=pltpu.CompilerParams(vmem_limit_bytes=VLIM),
    )(meta, q3, kv)


def gelu_both(a):
    c = 0.7978845608028654
    a2 = a * a
    t = jnp.tanh(c * a * (1.0 + 0.044715 * a2))
    half = 0.5 * (1.0 + t)
    slope = half + 0.5 * a * (1.0 - t * t) * (c * (1.0 + 0.134145 * a2))
    return a * half, slope


def mlp_kernel(
    n, att, rp, cp, gfull, woa, wu, wd,
    out, gmid, gm, dog, dg2,
    attg, attp, wide, hid, gmb, act, gpre, osum, osend, orecv, esend, erecv, dsend, gbb, mid,
    ss, rs, ls, as_, ar, ds_, dr,
):
    p = Place(n)
    rows, width = rp.shape
    ff = wu.shape[1]
    pk = rows * 3 // 2
    ready = greet(p, xpeer=True, line=True)
    gmb[0] = cp[...]
    ready()

    def xc(i, src, dst):
        return rcopy(src, dst, ss.at[i], rs.at[i], p.xpeer())

    def ac(i, to):
        return rcopy(att.at[to], attg.at[i], as_.at[to], ar.at[i], p.on_line(to))

    def dc(i, to):
        return rcopy(dsend.at[to], dog.at[i], ds_.at[to], dr.at[i], p.on_line(to))

    for d in range(1, GROUPS):
        to = (p.a + d) % GROUPS
        ac(p.a, to).start()
    attg[p.a] = att[p.a]
    x_gm = xc(0, cp, gmb.at[1])
    x_gm.start()
    for d in range(1, GROUPS):
        fr = (p.a + d) % GROUPS
        ac(fr, fr).wait_recv()
    other = 1 - p.x
    x_att = [xc(1 + i, attg.at[other * 2 + i], attp.at[i]) for i in range(2)]
    for g in range(GROUPS):
        wide[:, g * 256 : g * 256 + 128] = attg[g, 0:rows, :]
        top, bottom = unpack_tail(attg[g, rows:pk, :])
        wide[0 : rows // 2, g * 256 + 128 : g * 256 + 256] = top
        wide[rows // 2 : rows, g * 256 + 128 : g * 256 + 256] = bottom
    mid[...] = rp[...].astype(F32) + dot(wide[...], woa[...])
    u = ext_of(mid[...])
    gain = jnp.concatenate([gfull[0, 1:2, :], gfull[1, 1:2, :]], axis=1)
    hid[0] = (u * inv_rms(u) * gain).astype(BF16)
    x_hid = xc(3, hid.at[0], hid.at[1])
    x_hid.start()
    for c in x_att:
        c.start()
    x_gm.wait()
    x_hid.wait()
    tiles = ff // 256

    def up(t, carry):
        at = pl.ds(pl.multiple_of(t * 256, 256), 256)
        for i in range(2):
            pre = dot(hid[i], wu[:, at])
            a, slope = gelu_both(pre)
            act[i, :, at] = a.astype(BF16)
            gpre[i, :, at] = (slope * dg(gmb[i], wd[at, :], NT)).astype(BF16)
        return carry

    lax.fori_loop(0, tiles, up, 0)
    esend[...] = dg(gpre[1], wu[...], NT).astype(BF16)
    x_e = xc(4, esend, erecv)
    x_e.start()
    osend[...] = dot(act[1], wd[...]).astype(BF16)
    x_o = xc(5, osend, orecv)
    x_o.start()
    e_own = dg(gpre[0], wu[...], NT)
    osum[...] = dot(act[0], wd[...])

    def grads(t, carry):
        at = pl.ds(pl.multiple_of(t * 256, 256), 256)
        g = dg(hid[0], gpre[0, :, at], TN) + dg(hid[1], gpre[1, :, at], TN)
        per = width // 256
        r0 = pl.multiple_of((t // per) * width, width)
        c0 = pl.multiple_of((t % per) * 256, 256)
        gm[pl.ds(r0, width), pl.ds(c0, 256)] = g.astype(BF16)
        g = dg(act[0, :, at], gmb[0], TN) + dg(act[1, :, at], gmb[1], TN)
        gm[pl.ds(pl.multiple_of(ff + t * 256, 256), 256), :] = g.astype(BF16)
        return carry

    lax.fori_loop(0, tiles, grads, 0)
    x_e.wait()
    e = e_own + erecv[...].astype(F32)
    u = ext_of(mid[...])
    inv = inv_rms(u)
    dg2[...] = jnp.broadcast_to(jnp.sum(e * (u * inv), axis=0, keepdims=True), dg2.shape)
    gmid[...] = cp[...].astype(F32) + crms_back(u, inv, gain, e)
    gbb[0] = gmid[...].astype(BF16)
    x_gb = xc(6, gbb.at[0], gbb.at[1])
    x_gb.start()
    for g in range(GROUPS):
        da = dg(gbb[0], woa[g * 256 : (g + 1) * 256, :], NT).astype(BF16)
        dsend[g, 0:rows, :] = da[:, 0:128]
        dsend[g, rows:pk, :] = pack_tail(da[:, 128:256])
    for d in range(1, GROUPS):
        dc(p.a, (p.a + d) % GROUPS).start()
    dog[p.a] = dsend[p.a]
    x_o.wait()
    final = mid[...] + osum[...] + orecv[...].astype(F32)
    out[...] = final[:, : width - 1].astype(BF16)
    for c in x_att:
        c.wait()
    x_gb.wait()
    for i in range(2):
        own_tail = jnp.concatenate(unpack_tail(attg[p.x * 2 + i, rows:pk, :]), axis=0)
        peer_tail = jnp.concatenate(unpack_tail(attp[i, rows:pk, :]), axis=0)
        g = dg(attg[p.x * 2 + i, 0:rows, :], gbb[0], TN) + dg(attp[i, 0:rows, :], gbb[1], TN)
        base = 2 * ff + i * 192
        gm[base : base + 128, :] = g.astype(BF16)
        g = dg(own_tail, gbb[0], TN) + dg(peer_tail, gbb[1], TN)
        gm[base + 128 : base + 192, :] = g[HD:, :].astype(BF16)
    for d in range(1, GROUPS):
        to = (p.a + d) % GROUPS
        ac(p.a, to).wait_send()
        dc(p.a, to).wait_send()
        dc(to, to).wait_recv()


def mlp(n, att, rp, cp, gfull, woa, wu, wd):
    rows, width = rp.shape
    ff = wu.shape[1]
    pk = rows * 3 // 2
    sds = jax.ShapeDtypeStruct
    v = pltpu.VMEM
    return pl.pallas_call(
        functools.partial(mlp_kernel, n),
        name="mlp",
        out_shape=(
            sds((rows, width - 1), BF16),
            sds((rows, width), F32),
            sds((2 * ff + width // 2, width), BF16),
            sds((GROUPS, pk, 128), BF16),
            sds((8, width), F32),
        ),
        in_specs=[VM] * 7,
        out_specs=[VM] * 5,
        scratch_shapes=[
            v((GROUPS, pk, 128), BF16),
            v((2, pk, 128), BF16),
            v((rows, GROUPS * 256), BF16),
            v((2, rows, width), BF16),
            v((2, rows, width), BF16),
            v((2, rows, ff), BF16),
            v((2, rows, ff), BF16),
            v((rows, width), F32),
            v((rows, width), BF16),
            v((rows, width), BF16),
            v((rows, width), BF16),
            v((rows, width), BF16),
            v((GROUPS, pk, 128), BF16),
            v((2, rows, width), BF16),
            v((rows, width), F32),
            DMA((8,)),
            DMA((8,)),
            DMA((2,)),
            DMA((GROUPS,)),
            DMA((GROUPS,)),
            DMA((GROUPS,)),
            DMA((GROUPS,)),
        ],
        compiler_params=pltpu.CompilerParams(
            collective_id=1, has_side_effects=True, vmem_limit_bytes=VLIM
        ),
    )(att, rp, cp, gfull, woa, wu, wd)


def attend_back_kernel(meta, q3, kv, o3, l3, dog, dqp, dkvb, do3, dkv):
    rows = q3.shape[1] // GROUPS
    keys = kv.shape[0] // GROUPS
    size = min(SUB, keys)
    first_query = meta[0] * rows
    dead = jnp.where(meta[1] > keys, 0.0, -MASKED).astype(F32)
    low = low_half((rows, 128))
    for z in range(GROUPS):
        at = pl.ds(z * rows, rows)
        both = dog[z, 0:rows, :]
        zero = jnp.zeros_like(both)
        do3[0, at, :] = jnp.where(low, both, zero)
        do3[1, at, :] = jnp.where(low, zero, both)
        top, bottom = unpack_tail(dog[z, rows:, :])
        do3[2, pl.ds(z * rows, rows // 2), :] = top
        do3[2, pl.ds(z * rows + rows // 2, rows // 2), :] = bottom
    dkv[...] = jnp.zeros_like(dkv)

    def head(h, carry):
        kt = pl.multiple_of(128 * (h // 2), 128)
        vt = pl.multiple_of(jnp.where(h == 2, 128, 256), 128)
        for z in range(GROUPS):
            at_q = pl.ds(z * rows, rows)
            q = q3[h, at_q, :]
            do = do3[h, at_q, :]
            lse = l3[h, at_q, 0:1]
            delta = jnp.sum(o3[h, at_q, :] * do.astype(F32), axis=1, keepdims=True)
            dq = jnp.zeros((rows, 128), F32)
            for c, s in key_steps(z, keys):
                at = pl.ds(c * keys + s * size, size)
                k = kv[at, pl.ds(kt, 128)]
                scores = dg(q, k, NT) * (SCALE * LOG2E)
                if c == z:
                    scores = jnp.where(
                        causal(scores.shape, s, size, first_query), scores, MASKED
                    )
                weights = jnp.exp2(scores - (lse + dead if c > 0 else lse))
                gp = dg(do, kv[at, pl.ds(vt, 128)], NT)
                gs = (weights * (gp - delta)).astype(BF16)
                dq = dq + dot(gs, k)
                dkv[at, pl.ds(vt, 128)] += dg(weights.astype(BF16), do, TN)
                dkv[at, pl.ds(kt, 128)] += dg(gs, q, TN) * SCALE
            dq = dq * SCALE

            @pl.when(h == 0)
            def _():
                dqp[at_q, 0:128] = dq.astype(BF16)

            @pl.when(h == 1)
            def _():
                dqp[at_q, 0:128] = jnp.where(low, dqp[at_q, 0:128], dq.astype(BF16))

            @pl.when(h == 2)
            def _():
                dqp[at_q, 128:256] = jnp.where(low, dq, 0.0).astype(BF16)

        return carry

    lax.fori_loop(0, GH, head, 0)
    dkvb[...] = dkv[...].astype(BF16)


def attend_back(meta, q3, kv, o3, l3, dog):
    sds = jax.ShapeDtypeStruct
    return pl.pallas_call(
        attend_back_kernel,
        name="attend_back",
        out_shape=(sds((q3.shape[1], 256), BF16), sds(kv.shape, BF16)),
        in_specs=[SM] + [VM] * 5,
        out_specs=[VM] * 2,
        scratch_shapes=[pltpu.VMEM(q3.shape, BF16), pltpu.VMEM(kv.shape, F32)],
        compiler_params=pltpu.CompilerParams(vmem_limit_bytes=VLIM),
    )(meta, q3, kv, o3, l3, dog)


def finish_kernel(
    n, dqp, dkvb, wg, h1, rp, gmid, gfull, dg2,
    gin, gq, gains,
    wfull, rk, sy, ry, gps, gpr, gqb, qk, q1, qx, q2, qy, g0, gk, gx, gy, ga,
    xs, xr, ls, ks, kr, ys, yr, zs, zr, qs, qr, ns, nr, bs, br, cs, cr,
):
    p = Place(n)
    rows, width = rp.shape
    half = width // 2
    quarter = width // 4
    ready = greet(p, xpeer=True, sibling=True, chips=True, line=True)
    at_x = pl.ds(pl.multiple_of(p.x * half, half), half)
    local = [
        pltpu.make_async_copy(wg.at[g], wfull.at[g, at_x], ls.at[g]) for g in range(GROUPS)
    ]
    for c in local:
        c.start()
    ready()
    wx = [
        rcopy(wg.at[g], wfull.at[g, at_x], xs.at[g], xr.at[g], p.xpeer()) for g in range(GROUPS)
    ]

    def block(ref, z, b):
        return ref.at[pl.ds(pl.multiple_of((z * p.m + b) * rows, rows), rows)]

    def kc(z, chip):
        return rcopy(
            block(dkvb, z, chip * 2 + 1 - p.k), rk.at[z, chip], ks.at[z, chip], kr.at[z, chip],
            p.sibling(),
        )

    def yc(z, chip, slot):
        return rcopy(sy.at[z, chip], ry.at[z, slot], ys.at[z, chip], yr.at[z, slot], p.on_chip(chip))

    def zc(slot, to):
        return rcopy(gps.at[to], gpr.at[slot], zs.at[to], zr.at[slot], p.on_line(to))

    order = [(p.a + d) % GROUPS for d in range(1, GROUPS)] + [p.a]
    for z in order:
        for d in range(1, p.chips):
            kc(z, (p.chip + d) % p.chips).start()
        kc(z, p.chip).start()
    for c in wx:
        c.start()
    for z in order:
        for d in range(1, p.chips):
            chip = (p.chip + d) % p.chips
            kc(z, chip).wait()
            mine = dkvb[pl.ds(pl.multiple_of((z * p.m + chip * 2 + p.k) * rows, rows), rows), :]
            sy[z, chip] = (mine.astype(F32) + rk[z, chip].astype(F32)).astype(BF16)
            yc(z, chip, p.chip).start()
    for i, z in enumerate(order):
        kc(z, p.chip).wait()
        mine = dkvb[pl.ds(pl.multiple_of((z * p.m + p.b) * rows, rows), rows), :]
        total = mine.astype(F32) + rk[z, p.chip].astype(F32)
        for d in range(1, p.chips):
            chip = (p.chip + d) % p.chips
            yc(z, chip, chip).wait_recv()
            total = total + ry[z, chip].astype(F32)
        gps[z, :, 0:256] = dqp[pl.ds(pl.multiple_of(z * rows, rows), rows), :]
        gps[z, :, 256:640] = total.astype(BF16)
        if i < GROUPS - 1:
            zc(p.a, z).start()
    gpr[p.a] = gps[p.a]

    def rowdot(z, carry):
        for t in range(width // 256):
            at = pl.ds(t * 256, 256)
            gqb[at, :] += dg(h1[z, :, at], gps[z], TN)
        return carry

    gqb[...] = jnp.zeros_like(gqb)
    lax.fori_loop(0, GROUPS, rowdot, 0)

    def part(i, core):
        return pl.ds(pl.multiple_of(i * half + core * quarter, quarter), quarter)

    for i in range(2):
        qk[0, i] = gqb[part(i, 1 - p.k), :].astype(BF16)
    q_k = rcopy(qk.at[0], qk.at[1], qs.at[0], qr.at[0], p.sibling())
    q_k.start()
    q_k.wait()
    for i in range(2):
        q1[i] = gqb[part(i, p.k), :] + qk[1, i].astype(F32)
    qx[0] = q1[1 - p.x].astype(BF16)
    q_x = rcopy(qx.at[0], qx.at[1], qs.at[1], qr.at[1], p.xpeer())
    q_x.start()
    q_x.wait()
    q2[...] = q1[p.x] + qx[1].astype(F32)
    qy[p.chip] = q2[...].astype(BF16)

    def qc(chip, slot):
        return rcopy(qy.at[p.chip], qy.at[slot], ns.at[chip], nr.at[slot], p.on_chip(chip))

    for d in range(1, p.chips):
        qc((p.chip + d) % p.chips, p.chip).start()
    total = q2[...]
    for d in range(1, p.chips):
        chip = (p.chip + d) % p.chips
        qc(chip, chip).wait_recv()
        total = total + qy[chip].astype(F32)
    gq[p.a, p.k] = total.astype(BF16)

    def bc(slot, to):
        return rcopy(gq.at[slot, p.k], gq.at[slot, p.k], bs.at[to], br.at[slot], p.on_line(to))

    def sc(slot, core):
        return rcopy(gq.at[slot, core], gq.at[slot, core], cs.at[slot], cr.at[slot], p.sibling())

    for d in range(1, GROUPS):
        bc(p.a, (p.a + d) % GROUPS).start()
    sc(p.a, p.k).start()
    for c in local:
        c.wait()
    for c in wx:
        c.wait()
    h = dg(gpr[p.a], wfull[p.a], NT)
    for d in range(1, GROUPS):
        g = (p.a + d) % GROUPS
        zc(g, g).wait_recv()
        h = h + dg(gpr[g], wfull[g], NT)
    u = ext_of(rp[...].astype(F32))
    inv = inv_rms(u)
    gain = jnp.concatenate([gfull[0, 0:1, :], gfull[1, 0:1, :]], axis=1)
    result = gmid[...] + crms_back(u, inv, gain, h)
    gin[...] = result[:, : width - 1]
    first = jnp.sum(h * (u * inv), axis=0, keepdims=True)
    which = lax.broadcasted_iota(jnp.int32, (8, width), 0)
    g0[...] = jnp.where(which == 0, first, dg2[...])
    g_k = rcopy(g0, gk, qs.at[2], qr.at[2], p.sibling())
    g_k.start()
    g_k.wait()
    g0[...] += gk[...]
    g_x = rcopy(g0, gx, qs.at[3], qr.at[3], p.xpeer())
    g_x.start()
    g_x.wait()
    gy[p.chip] = g0[...] + gx[...]

    def gc(chip, slot):
        return rcopy(gy.at[p.chip], gy.at[slot], ys.at[GROUPS, chip], yr.at[GROUPS, slot], p.on_chip(chip))

    for d in range(1, p.chips):
        gc((p.chip + d) % p.chips, p.chip).start()
    for d in range(1, p.chips):
        chip = (p.chip + d) % p.chips
        gc(chip, chip).wait_recv()
    total = gy[0]
    for chip in range(1, p.chips):
        total = total + gy[chip]
    ga[p.a] = total

    def lc(slot, to):
        return rcopy(ga.at[p.a], ga.at[slot], zs.at[GROUPS + to], zr.at[GROUPS + slot], p.on_line(to))

    for d in range(1, GROUPS):
        lc(p.a, (p.a + d) % GROUPS).start()
    for d in range(1, GROUPS):
        g = (p.a + d) % GROUPS
        lc(g, g).wait_recv()
    total = ga[0]
    for g in range(1, GROUPS):
        total = total + ga[g]
    gains[...] = total
    for d in range(1, GROUPS):
        g = (p.a + d) % GROUPS
        bc(g, g).wait_recv()
        sc(g, p.k).start()
    for g in range(GROUPS):
        sc(g, 1 - p.k).wait_recv()
        sc(g, p.k).wait_send()
    for d in range(1, p.chips):
        chip = (p.chip + d) % p.chips
        qc(chip, p.chip).wait_send()
        gc(chip, p.chip).wait_send()
        for z in range(GROUPS):
            yc(z, chip, p.chip).wait_send()
    for d in range(1, GROUPS):
        to = (p.a + d) % GROUPS
        zc(p.a, to).wait_send()
        bc(p.a, to).wait_send()
        lc(p.a, to).wait_send()


def finish(n, dqp, dkvb, wg, h1, rp, gmid, gfull, dg2):
    rows, width = rp.shape
    half = width // 2
    quarter = width // 4
    lanes = wg.shape[2]
    chips = n // GROUPS // 2
    sds = jax.ShapeDtypeStruct
    v = pltpu.VMEM
    return pl.pallas_call(
        functools.partial(finish_kernel, n),
        name="finish",
        out_shape=(
            sds((rows, width - 1), F32),
            sds((GROUPS, 2, quarter, lanes), BF16),
            sds((8, width), F32),
        ),
        in_specs=[VM, VM, ANY] + [VM] * 5,
        out_specs=[VM] * 3,
        scratch_shapes=[
            v((GROUPS, width, lanes), BF16),
            v((GROUPS, chips, rows, 384), BF16),
            v((GROUPS, chips, rows, 384), BF16),
            v((GROUPS, chips, rows, 384), BF16),
            v((GROUPS, rows, lanes), BF16),
            v((GROUPS, rows, lanes), BF16),
            v((width, lanes), F32),
            v((2, 2, quarter, lanes), BF16),
            v((2, quarter, lanes), F32),
            v((2, quarter, lanes), BF16),
            v((quarter, lanes), F32),
            v((chips, quarter, lanes), BF16),
            v((8, width), F32),
            v((8, width), F32),
            v((8, width), F32),
            v((chips, 8, width), F32),
            v((GROUPS, 8, width), F32),
            DMA((GROUPS,)),
            DMA((GROUPS,)),
            DMA((GROUPS,)),
            DMA((GROUPS, chips)),
            DMA((GROUPS, chips)),
            DMA((GROUPS + 1, chips)),
            DMA((GROUPS + 1, chips)),
            DMA((2 * GROUPS,)),
            DMA((2 * GROUPS,)),
            DMA((4,)),
            DMA((4,)),
            DMA((chips,)),
            DMA((chips,)),
            DMA((GROUPS,)),
            DMA((GROUPS,)),
            DMA((GROUPS,)),
            DMA((GROUPS,)),
        ],
        compiler_params=pltpu.CompilerParams(
            collective_id=2, has_side_effects=True, vmem_limit_bytes=VLIM
        ),
    )(dqp, dkvb, wg, h1, rp, gmid, gfull, dg2)


def sum_kernel(n, gm, res, rk, run, left, right, ry, ks, kr, zs, zr, ys, yr, as_, ar, cs, cr):
    p = Place(n)
    half = gm.shape[0] // 2
    piece = half // GROUPS
    ready = greet(p, sibling=True, chips=True, line=True)
    ready()

    def gm_at(core, z):
        return pl.ds(pl.multiple_of(core * half + z * piece, 16), piece)

    def kc(z):
        return rcopy(gm.at[gm_at(1 - p.k, z)], rk.at[z], ks.at[z], kr.at[z], p.sibling())

    for z in range(GROUPS):
        kc(z).start()
    for z in range(GROUPS):
        kc(z).wait()
        run[z] = (gm[gm_at(p.k, z), :].astype(F32) + rk[z].astype(F32)).astype(BF16)

    def rightward(z):
        return rcopy(run.at[z], left.at[z], zs.at[0, z], zr.at[0, z], p.on_line(p.a + 1))

    def leftward(z):
        return rcopy(run.at[z], right.at[z], zs.at[1, z], zr.at[1, z], p.on_line(p.a - 1))

    for s in range(GROUPS - 1, 0, -1):
        @pl.when(p.a + s < GROUPS)
        def _():
            @pl.when(p.a > 0)
            def _():
                rightward(p.a + s).wait_recv()
                run[p.a + s] = (run[p.a + s].astype(F32) + left[p.a + s].astype(F32)).astype(BF16)

            rightward(p.a + s).start()

        @pl.when(p.a - s >= 0)
        def _():
            @pl.when(p.a < GROUPS - 1)
            def _():
                leftward(p.a - s).wait_recv()
                run[p.a - s] = (run[p.a - s].astype(F32) + right[p.a - s].astype(F32)).astype(BF16)

            leftward(p.a - s).start()

    @pl.when(p.a > 0)
    def _():
        rightward(p.a).wait_recv()
        run[p.a] = (run[p.a].astype(F32) + left[p.a].astype(F32)).astype(BF16)

    @pl.when(p.a < GROUPS - 1)
    def _():
        leftward(p.a).wait_recv()
        run[p.a] = (run[p.a].astype(F32) + right[p.a].astype(F32)).astype(BF16)

    def yc(chip, slot):
        return rcopy(run.at[p.a], ry.at[slot], ys.at[chip], yr.at[slot], p.on_chip(chip))

    for d in range(1, p.chips):
        yc((p.chip + d) % p.chips, p.chip).start()
    ry[p.chip] = run[p.a]
    for d in range(1, p.chips):
        chip = (p.chip + d) % p.chips
        yc(chip, chip).wait_recv()
    total = ry[0].astype(F32)
    for chip in range(1, p.chips):
        total = total + ry[chip].astype(F32)
    res[gm_at(p.k, p.a), :] = total.astype(BF16)

    def ac(z, dst, sem):
        r = res.at[gm_at(p.k, z)]
        return rcopy(r, r, as_.at[sem], ar.at[z], p.on_line(dst))

    def sc(z, core):
        r = res.at[gm_at(core, z)]
        return rcopy(r, r, cs.at[z], cr.at[z], p.sibling())

    @pl.when(p.a < GROUPS - 1)
    def _():
        ac(p.a, p.a + 1, 0).start()

    @pl.when(p.a > 0)
    def _():
        ac(p.a, p.a - 1, 1).start()

    sc(p.a, p.k).start()
    for s in range(1, GROUPS):

        @pl.when(p.a - s >= 0)
        def _():
            ac(p.a - s, p.a, 0).wait_recv()

            @pl.when(p.a < GROUPS - 1)
            def _():
                ac(p.a - s, p.a + 1, 2 * s).start()

            sc(p.a - s, p.k).start()

        @pl.when(p.a + s < GROUPS)
        def _():
            ac(p.a + s, p.a, 0).wait_recv()

            @pl.when(p.a > 0)
            def _():
                ac(p.a + s, p.a - 1, 2 * s + 1).start()

            sc(p.a + s, p.k).start()

    for z in range(GROUPS):
        sc(z, 1 - p.k).wait_recv()
        sc(z, p.k).wait_send()
    for s in range(GROUPS):

        @pl.when((p.a - s >= 0) & (p.a < GROUPS - 1))
        def _():
            ac(p.a - s, p.a + 1, 2 * s).wait_send()

        @pl.when((p.a + s < GROUPS) & (p.a > 0))
        def _():
            ac(p.a + s, p.a - 1, 2 * s + 1).wait_send()

        if s > 0:

            @pl.when(p.a + s < GROUPS)
            def _():
                rightward(p.a + s).wait_send()

            @pl.when(p.a - s >= 0)
            def _():
                leftward(p.a - s).wait_send()

    for d in range(1, p.chips):
        yc((p.chip + d) % p.chips, p.chip).wait_send()


def sum_over_ctx(n, gm):
    chips = n // GROUPS // 2
    piece = gm.shape[0] // 2 // GROUPS
    width = gm.shape[1]
    v = pltpu.VMEM
    return pl.pallas_call(
        functools.partial(sum_kernel, n),
        name="sum_over_ctx",
        out_shape=jax.ShapeDtypeStruct(gm.shape, BF16),
        in_specs=[VM],
        out_specs=VM,
        scratch_shapes=[
            v((GROUPS, piece, width), BF16),
            v((GROUPS, piece, width), BF16),
            v((GROUPS, piece, width), BF16),
            v((GROUPS, piece, width), BF16),
            v((chips, piece, width), BF16),
            DMA((GROUPS,)),
            DMA((GROUPS,)),
            DMA((2, GROUPS)),
            DMA((2, GROUPS)),
            DMA((chips,)),
            DMA((chips,)),
            DMA((2 * GROUPS,)),
            DMA((GROUPS,)),
            DMA((GROUPS,)),
            DMA((GROUPS,)),
        ],
        compiler_params=pltpu.CompilerParams(
            collective_id=3, has_side_effects=True, vmem_limit_bytes=VLIM
        ),
    )(gm)


def by_group(w):
    r = w.shape[0]
    w = w.reshape(r, 3, GROUPS, GH, HD).transpose(2, 0, 1, 3, 4)
    q, k, v = w[:, :, 0], w[:, :, 1], w[:, :, 2]
    zero = jnp.zeros_like(q[:, :, 0])
    return jnp.concatenate(
        [q[:, :, 0], q[:, :, 1], q[:, :, 2], zero, k[:, :, 0], k[:, :, 1], k[:, :, 2], v[:, :, 2],
         v[:, :, 0], v[:, :, 1]],
        axis=-1,
    )


def from_groups(g):
    r = g.shape[1]
    t = g.reshape(GROUPS, r, 10, HD).transpose(1, 0, 2, 3)
    q = t[:, :, 0:3]
    k = t[:, :, 4:7]
    v = jnp.stack([t[:, :, 8], t[:, :, 9], t[:, :, 7]], axis=2)
    return jnp.stack([q, k, v], axis=1).reshape(r, 3 * GROUPS * GH * HD)


def shards(n, resid, lengths, gain_one, w_qkv, w_out, gain_two, w_up, w_down, cotangent):
    _, rows, narrow = resid.shape
    width = narrow + 1
    ff = w_up.shape[1]
    c = lax.axis_index("ctx")
    pos = c * rows + jnp.arange(rows, dtype=jnp.int32)
    pad = ((0, 0), (0, 1))
    rp = jnp.pad(resid[0], pad)
    live = pos[:, None] < lengths[0]
    cp = jnp.pad(jnp.where(live, cotangent[0], jnp.zeros_like(cotangent[0])), pad)
    wo = jnp.pad(w_out, pad)
    wd = jnp.pad(w_down, pad)
    gains = jnp.pad(jnp.stack([gain_one, gain_two]).astype(F32), ((0, 6), (0, 0)))
    wg = by_group(w_qkv)
    meta = jnp.stack([c % (n // GROUPS), lengths[0]]).astype(jnp.int32)

    h1, q3, kv, _, woa, gfull = project(n, rp, gains, wg, wo)
    att, o3, l3 = attend(meta, q3, kv)
    out, gmid, gm, dog, dg2 = mlp(n, att, rp, cp, gfull, woa, w_up, wd)
    dqp, dkvb = attend_back(meta, q3, kv, o3, l3, dog)
    gin, gq, gsum = finish(n, dqp, dkvb, wg, h1, rp, gmid, gfull, dg2)
    res = sum_over_ctx(n, gm)

    half = width // 2
    grad_qkv = from_groups(gq.reshape(GROUPS, half, -1).astype(F32))
    mine = lax.dynamic_slice_in_dim(gsum, lax.axis_index("fsdp") * half, half, 1)
    up = jnp.concatenate([res[:width], res[width : 2 * width]], axis=1).astype(F32)
    down = res[ff : 2 * ff, :narrow].astype(F32)
    gout = res[2 * ff :, :narrow].astype(F32)
    return out[None], gin[None], mine[0], grad_qkv, gout, mine[1], up, down


def solution(mesh):
    n = mesh.shape["ctx"]
    return jax.shard_map(
        functools.partial(shards, n),
        mesh=mesh,
        in_specs=(
            P("fsdp", "ctx", None),
            P("fsdp"),
            P("fsdp"),
            P("fsdp", None),
            P("fsdp", None),
            P("fsdp"),
            P(None, "fsdp"),
            P("fsdp", None),
            P("fsdp", "ctx", None),
        ),
        out_specs=(
            P("fsdp", "ctx", None),
            P("fsdp", "ctx", None),
            P("fsdp"),
            P("fsdp", None),
            P("fsdp", None),
            P("fsdp"),
            P(None, "fsdp"),
            P("fsdp", None),
        ),
        check_vma=False,
    )
```

time: 1350 us -> 428 us (0.32)
  waiting for transfers between devices: 489 us -> 0 us
  blocking collectives: 432 us -> 0 us
  Pallas kernels: 0 us -> 363 us
  starting transfers between devices: 174 us -> 0 us
  loops' own time: 80.4 us -> 0 us
  other arithmetic: 68.6 us -> 10.9 us
  matrix products: 54.5 us -> 0 us
  local copies, waits for them, and re-layouts: 24.1 us -> 48.2 us
  between operations: 18.1 us -> 1.88 us
    pallas_call x0 -> x6, Pallas kernels: none -> 363 us  [the longest x1 121 us: sum_over_ctx(): pl.pallas_call(functools.partial(sum_kernel, n), name='sum_over_ctx', out...]
    ppermute x46 -> x0, waiting for transfers between devices: 307 us -> none  [passed_along(): return lax.ppermute(block, axis, route)]
    psum x1 -> x0, blocking collectives: 300 us -> none  [shards(): lax.psum((shard_sums[0], shard_sums[1], shard_sums[2], shard_sums[3], sha...]
    ppermute x46 -> x0, starting transfers between devices: 173 us -> none  [passed_along(): return lax.ppermute(block, axis, route)]
    reduce_scatter x4 -> x0, waiting for transfers between devices: 144 us -> none  [the longest x1 63 us: shards(): lax.psum_scatter(grad_down.astype(jnp.bfloat16), 'fsdp', scatter_dimensio...]
    unnamed x1 -> x0, blocking collectives: 122 us -> none
    another operation x34 -> x0, loops' own time: 80.4 us -> none  [the longest x1 40 us: circle_forward(): held, state = lax.fori_loop(1, circle_size, one_turn, (kv_block, state))]
    dot_general x19 -> x0, matrix products: 54.5 us -> none  [the longest x1 6.76 us: shards(): jnp.dot(grad_mlp, down_full.T, preferred_element_type=jnp.float32)]
  transfers between devices with their start and end apart: 54 -> 0, of which waited for: 50 -> 0; matrix products, arithmetic and copies ran while one was open for 10% -> 0% of each run, Pallas kernels for 0% -> 0%
where the time goes in v1:
time: 428 us; the launch traced here: 424 us
  Pallas kernels  363 us (85%)
  local copies, waits for them, and re-layouts  48.2 us (11%)
  other arithmetic  10.9 us (3%)
    pallas_call x1, Pallas kernels, sum_over_ctx(): pl.pallas_call(functools.partial(sum_kernel, n), name='sum_over_ctx', out...  121 us
    pallas_call x1, Pallas kernels, finish(): pl.pallas_call(functools.partial(finish_kernel, n), name='finish', out_sh...  83.7 us
    pallas_call x1, Pallas kernels, mlp(): pl.pallas_call(functools.partial(mlp_kernel, n), name='mlp', out_shape=(s...  58.2 us
    pallas_call x1, Pallas kernels, project(): pl.pallas_call(functools.partial(project_kernel, n), name='project', out_...  47.4 us
    pallas_call x1, Pallas kernels, attend_back(): pl.pallas_call(attend_back_kernel, name='attend_back', out_shape=(sds((q3...  32.4 us
    pallas_call x1, Pallas kernels, attend(): pl.pallas_call(attend_kernel, name='attend', out_shape=(sds((GROUPS, rows...  19.5 us
    transpose x2, local copies, waits for them, and re-layouts, from_groups(): t = g.reshape(GROUPS, r, 10, HD).transpose(1, 0, 2, 3)  14.7 us
    unnamed x12, local copies, waits for them, and re-layouts  10.6 us

profile of v1, /device:TPU:0, one launch (start us, length us, event | category | flops | bytes accessed | tf_op | source)
XLA Modules:
  0.0 423.5 jit_solution(14477323707412454181)
XLA Ops:
  1.3 0.6 pad_add_fusion.meta
  1.9 1.8 pad.21.rp
  3.6 0.7 stack.34
  4.3 0.7 stack.33
  5.0 0.6 fusion.3.gains
  5.6 3.9 copy.19
  9.5 3.4 copy.20
  12.8 0.4 slice_bitcast_fusion.2
  13.2 0.1 slice_bitcast_fusion.11
  13.3 0.2 slice_bitcast_fusion.5
  13.5 0.8 broadcast_in_dim.21
  14.3 4.7 %concatenate.6.wg = bf16[4,384,640]{2,1,0:T(8,128)(2,1)} concatenate(bf16[4,384,64]{2,1,0:T(8,128)(2,1)S(1)} %get-tuple-element.77, bf16[4,384,64]{2,1,0:T(8,128)(2,1)S(1)} %get-tuple-element.76, bf16[4,384,64]{2,1,0:T(8,128)(2,1)S(1)} %get-tuple-element.75, bf16[4,384,64]{2,1,0:T(8,128)(2,1)} %broadcast_in_dim.21, bf16[4,384,64]{2,1,0:T(8,128)(2,1)S(1)} %get-tuple-element.78, ...), dimensions={2} | concatenate | bytes 3932160 | tf_op jit(solution)/shard_map/concatenate | solution.py:1068
  19.0 1.9 pad.24.wo
  21.0 47.4 %project.1 = (bf16[4,256,768]{2,1,0:T(8,128)(2,1)}, bf16[3,1024,128]{2,1,0:T(8,128)(2,1)}, bf16[4096,384]{1,0:T(8,128)(2,1)}, bf16[768,640]{1,0:T(8,128)(2,1)}, ...) custom-call(bf16[256,768]{1,0:T(8,128)(2,1)} %pad.21.rp, f32[8,384]{1,0:T(8,128)} %fusion.3.gains, ...), custom_call_target="tpu_custom_call" | custom-call | tf_op jit(solution)/shard_map/project/pallas_call | solution.py:296
  68.4 0.0 copy-start.3
  68.4 0.0 copy-start.1
  68.4 19.5 %attend.1 = (bf16[4,384,128]{2,1,0:T(8,128)(2,1)}, f32[3,1024,128]{2,1,0:T(8,128)}, f32[3,1024,128]{2,1,0:T(8,128)}) custom-call(s32[2]{0:T(128)} %pad_add_fusion.meta, bf16[3,1024,128]{2,1,0:T(8,128)(2,1)} %get-tuple-element.26.q3, bf16[4096,384]{1,0:T(8,128)(2,1)} %get-tuple-element.27.kv), custom_call_target="tpu_custom_call" | custom-call | tf_op jit(solution)/shard_map/attend/pallas_call | solution.py:387
  88.0 0.0 copy-done.3
  88.0 0.1 bitcast_select_fusion
  88.1 0.8 pad.25.cp
  88.9 0.0 copy-done.1
  88.9 1.6 pad.26.wd
  90.5 58.2 %mlp.1 = (bf16[256,767]{1,0:T(8,128)(2,1)}, f32[256,768]{1,0:T(8,128)}, bf16[3456,768]{1,0:T(8,128)(2,1)}, bf16[4,384,128]{2,1,0:T(8,128)(2,1)}, f32[8,768]{1,0:T(8,128)}) custom-call(bf16[4,384,128]{2,1,0:T(8,128)(2,1)} %get-tuple-element.28.att, bf16[256,768]{1,0:T(8,128)(2,1)} %pad.21.rp, bf16[256,768]{1,0:T(8,128)(2,1)} %pad.25.cp, ...), custom_call_target="tpu_custom_call" | custom-call | tf_op jit(solution)/shard_map/mlp/pallas_call | solution.py:535
  148.8 32.4 %attend_back.1 = (bf16[1024,256]{1,0:T(8,128)(2,1)}, bf16[4096,384]{1,0:T(8,128)(2,1)}) custom-call(s32[2]{0:T(128)} %pad_add_fusion.meta, bf16[3,1024,128]{2,1,0:T(8,128)(2,1)} %get-tuple-element.26.q3, bf16[4096,384]{1,0:T(8,128)(2,1)} %get-tuple-element.27.kv, f32[3,1024,128]{2,1,0:T(8,128)} %get-tuple-element.32.o3, ...), custom_call_target="tpu_custom_call" | custom-call | tf_op jit(solution)/shard_map/attend_back/pallas_call | solution.py:641
  181.2 83.7 %finish.1 = (f32[256,767]{1,0:T(8,128)}, bf16[4,2,192,640]{3,2,1,0:T(8,128)(2,1)}, f32[8,768]{1,0:T(8,128)}) custom-call(bf16[1024,256]{1,0:T(8,128)(2,1)} %get-tuple-element.35.dqp, bf16[4096,384]{1,0:T(8,128)(2,1)} %get-tuple-element.36.dkvb, bf16[4,384,640]{2,1,0:T(8,128)(2,1)} %concatenate.6.wg, bf16[4,256,768]{2,1,0:T(8,128)(2,1)} %get-tuple-element.37.h1, ...), custom_call_target="tpu_custom_call" | custom-call | tf_op jit(solution)/shard_map/finish/pallas_call | solution.py:843
  264.9 3.0 copy.22
  268.0 1.4 dynamic-slice_reduce_fusion
  269.4 7.6 %copy.21 = f32[4,2,192,640]{2,1,3,0:T(2,128)} copy(bf16[4,2,192,640]{3,2,1,0:T(8,128)(2,1)} %get-tuple-element.42) | data formatting | bytes 5898240 | tf_op jit(solution)/shard_map/transpose | solution.py:1077
  277.1 7.1 %reshape.35 = f32[4,384,10,64]{1,3,2,0:T(8,128)} reshape(f32[4,2,192,640]{2,1,3,0:T(2,128)} %copy.21) | data formatting | bytes 7864320 | tf_op jit(solution)/shard_map/transpose | solution.py:1077
  284.1 0.0 copy-start
  284.1 1.2 slice.105
  285.3 1.3 slice.104
  286.6 0.1 maximum_bitcast_fusion
  286.7 0.0 copy-done
  286.8 0.2 slice_bitcast_fusion.1
  286.9 0.2 pad_maximum_fusion
  287.2 2.9 copy.23
  290.1 121.2 %sum_over_ctx.1 = bf16[3456,768]{1,0:T(8,128)(2,1)} custom-call(bf16[3456,768]{1,0:T(8,128)(2,1)} %get-tuple-element.43.gm), custom_call_target="tpu_custom_call" | custom-call | tf_op jit(solution)/shard_map/sum_over_ctx/pallas_call | solution.py:1034
  411.3 2.2 slice_convert_fusion.1
  413.5 1.8 fusion.4
  415.3 2.8 maximum_convert_fusion
  418.1 0.0 copy-start.2
  418.1 4.3 %slice_convert_fusion = f32[1536,767]{1,0:T(8,128)} fusion(bf16[3456,768]{1,0:T(8,128)(2,1)} %sum_over_ctx.1), kind=kLoop, calls=%fused_computation.2 | loop fusion | flops 1178112 | bytes 7068672 | tf_op jit(solution)/shard_map/convert_element_type | solution.py:1111
  422.4 0.0 copy-done.2
  422.4 0.7 copy.26
  (1 shorter events, 0.0 us)
Async XLA Ops:
  68.4 19.6 %copy-start.3 = (bf16[1,256,767]{2,1,0:T(8,128)(2,1)S(1)}, bf16[1,256,767]{2,1,0:T(8,128)(2,1)}, u32[]{:S(2)}) copy-start(bf16[1,256,767]{2,1,0:T(8,128)(2,1)} %param.17) | copy-start | bytes 1178116
  68.4 20.5 %copy-start.1 = (bf16[1536,767]{1,0:T(8,128)(2,1)S(1)}, bf16[1536,767]{1,0:T(8,128)(2,1)}, u32[]{:S(2)}) copy-start(bf16[1536,767]{1,0:T(8,128)(2,1)} %param.16) | copy-start | bytes 7068676
  284.1 2.6 copy-start
  418.1 4.3 %copy-start.2 = (bf16[256,767]{1,0:T(8,128)(2,1)S(1)}, bf16[256,767]{1,0:T(8,128)(2,1)}, u32[]{:S(2)}) copy-start(bf16[256,767]{1,0:T(8,128)(2,1)} %get-tuple-element.31) | copy-start | bytes 1178116

commit v2 on v1

--- a/solution.py
+++ b/solution.py
@@ -409,15 +409,18 @@
 
 def mlp_kernel(
     n, att, rp, cp, gfull, woa, wu, wd,
-    out, gmid, gm, dog, dg2,
+    out, gmid, red, go, dog, dg2,
     attg, attp, wide, hid, gmb, act, gpre, osum, osend, orecv, esend, erecv, dsend, gbb, mid,
-    ss, rs, ls, as_, ar, ds_, dr,
+    gm, gk, ys_, yr_,
+    ss, rs, as_, ar, ds_, dr, ks, kr, qs, qr,
 ):
     p = Place(n)
     rows, width = rp.shape
     ff = wu.shape[1]
     pk = rows * 3 // 2
-    ready = greet(p, xpeer=True, line=True)
+    piece = red.shape[1]
+    part = GROUPS * piece
+    ready = greet(p, xpeer=True, sibling=True, chips=True, line=True)
     gmb[0] = cp[...]
     ready()
 
@@ -429,6 +432,13 @@
 
     def dc(i, to):
         return rcopy(dsend.at[to], dog.at[i], ds_.at[to], dr.at[i], p.on_line(to))
+
+    def kc(chip):
+        at = pl.ds(pl.multiple_of(chip * part, part), part)
+        return rcopy(gm.at[1 - p.k, at], gk.at[at], ks.at[chip], kr.at[chip], p.sibling())
+
+    def yc(chip, slot, z):
+        return rcopy(ys_.at[chip, z], yr_.at[slot, z], qs.at[chip, z], qr.at[slot, z], p.on_chip(chip))
 
     for d in range(1, GROUPS):
         to = (p.a + d) % GROUPS
@@ -454,82 +464,131 @@
     x_hid.start()
     for c in x_att:
         c.start()
+    tiles = ff // 256
+
+    def up(i):
+        def tile(t, carry):
+            at = pl.ds(pl.multiple_of(t * 256, 256), 256)
+            a, slope = gelu_both(dot(hid[i], wu[:, at]))
+            act[i, :, at] = a.astype(BF16)
+            gpre[i, :, at] = (slope * dg(gmb[i], wd[at, :], NT)).astype(BF16)
+            return carry
+
+        lax.fori_loop(0, tiles, tile, 0)
+
+    up(0)
     x_gm.wait()
     x_hid.wait()
-    tiles = ff // 256
-
-    def up(t, carry):
-        at = pl.ds(pl.multiple_of(t * 256, 256), 256)
-        for i in range(2):
-            pre = dot(hid[i], wu[:, at])
-            a, slope = gelu_both(pre)
-            act[i, :, at] = a.astype(BF16)
-            gpre[i, :, at] = (slope * dg(gmb[i], wd[at, :], NT)).astype(BF16)
-        return carry
-
-    lax.fori_loop(0, tiles, up, 0)
+    up(1)
     esend[...] = dg(gpre[1], wu[...], NT).astype(BF16)
     x_e = xc(4, esend, erecv)
     x_e.start()
-    osend[...] = dot(act[1], wd[...]).astype(BF16)
-    x_o = xc(5, osend, orecv)
-    x_o.start()
-    e_own = dg(gpre[0], wu[...], NT)
-    osum[...] = dot(act[0], wd[...])
-
-    def grads(t, carry):
+
+    def grad_up(t, carry):
         at = pl.ds(pl.multiple_of(t * 256, 256), 256)
         g = dg(hid[0], gpre[0, :, at], TN) + dg(hid[1], gpre[1, :, at], TN)
         per = width // 256
         r0 = pl.multiple_of((t // per) * width, width)
         c0 = pl.multiple_of((t % per) * 256, 256)
-        gm[pl.ds(r0, width), pl.ds(c0, 256)] = g.astype(BF16)
+        gm[0, pl.ds(r0, width), pl.ds(c0, 256)] = g.astype(BF16)
+        return carry
+
+    def grad_down(t, carry):
+        at = pl.ds(pl.multiple_of(t * 256, 256), 256)
         g = dg(act[0, :, at], gmb[0], TN) + dg(act[1, :, at], gmb[1], TN)
-        gm[pl.ds(pl.multiple_of(ff + t * 256, 256), 256), :] = g.astype(BF16)
+        gm[1, at, :] = g.astype(BF16)
         return carry
 
-    lax.fori_loop(0, tiles, grads, 0)
+    @pl.when(p.k == 0)
+    def _():
+        lax.fori_loop(0, tiles, grad_down, 0)
+
+    @pl.when(p.k == 1)
+    def _():
+        lax.fori_loop(0, tiles, grad_up, 0)
+
+    for d in range(1, p.chips):
+        kc((p.chip + d) % p.chips).start()
+    kc(p.chip).start()
+
+    @pl.when(p.k == 0)
+    def _():
+        lax.fori_loop(0, tiles, grad_up, 0)
+
+    @pl.when(p.k == 1)
+    def _():
+        lax.fori_loop(0, tiles, grad_down, 0)
+
+    for d in range(1, p.chips):
+        chip = (p.chip + d) % p.chips
+        kc(chip).wait()
+        for z in range(GROUPS):
+            at = pl.ds(pl.multiple_of(chip * part + z * piece, 16), piece)
+            ys_[chip, z] = (gm[p.k, at, :].astype(F32) + gk[at, :].astype(F32)).astype(BF16)
+            yc(chip, p.chip, z).start()
+    osend[...] = dot(act[1], wd[...]).astype(BF16)
+    e_own = dg(gpre[0], wu[...], NT)
     x_e.wait()
+    x_o = xc(5, osend, orecv)
+    x_o.start()
     e = e_own + erecv[...].astype(F32)
     u = ext_of(mid[...])
     inv = inv_rms(u)
-    dg2[...] = jnp.broadcast_to(jnp.sum(e * (u * inv), axis=0, keepdims=True), dg2.shape)
     gmid[...] = cp[...].astype(F32) + crms_back(u, inv, gain, e)
     gbb[0] = gmid[...].astype(BF16)
     x_gb = xc(6, gbb.at[0], gbb.at[1])
     x_gb.start()
-    for g in range(GROUPS):
-        da = dg(gbb[0], woa[g * 256 : (g + 1) * 256, :], NT).astype(BF16)
-        dsend[g, 0:rows, :] = da[:, 0:128]
-        dsend[g, rows:pk, :] = pack_tail(da[:, 128:256])
-    for d in range(1, GROUPS):
-        dc(p.a, (p.a + d) % GROUPS).start()
-    dog[p.a] = dsend[p.a]
-    x_o.wait()
-    final = mid[...] + osum[...] + orecv[...].astype(F32)
-    out[...] = final[:, : width - 1].astype(BF16)
+    for d in range(1, GROUPS + 1):
+        to = (p.a + d) % GROUPS
+        w = woa[pl.ds(pl.multiple_of(to * 256, 256), 256), :]
+        da = dg(gbb[0], w, NT).astype(BF16)
+        if d < GROUPS:
+            dsend[to, 0:rows, :] = da[:, 0:128]
+            dsend[to, rows:pk, :] = pack_tail(da[:, 128:256])
+            dc(p.a, to).start()
+        else:
+            dog[to, 0:rows, :] = da[:, 0:128]
+            dog[to, rows:pk, :] = pack_tail(da[:, 128:256])
+    dg2[...] = jnp.broadcast_to(jnp.sum(e * (u * inv), axis=0, keepdims=True), dg2.shape)
+    osum[...] = mid[...] + dot(act[0], wd[...])
     for c in x_att:
         c.wait()
+    x_o.wait()
+    final = osum[...] + orecv[...].astype(F32)
+    out[...] = final[:, : width - 1].astype(BF16)
     x_gb.wait()
     for i in range(2):
         own_tail = jnp.concatenate(unpack_tail(attg[p.x * 2 + i, rows:pk, :]), axis=0)
         peer_tail = jnp.concatenate(unpack_tail(attp[i, rows:pk, :]), axis=0)
         g = dg(attg[p.x * 2 + i, 0:rows, :], gbb[0], TN) + dg(attp[i, 0:rows, :], gbb[1], TN)
-        base = 2 * ff + i * 192
-        gm[base : base + 128, :] = g.astype(BF16)
+        go[i * 192 : i * 192 + 128, :] = g.astype(BF16)
         g = dg(own_tail, gbb[0], TN) + dg(peer_tail, gbb[1], TN)
-        gm[base + 128 : base + 192, :] = g[HD:, :].astype(BF16)
+        go[i * 192 + 128 : i * 192 + 192, :] = g[HD:, :].astype(BF16)
+    kc(p.chip).wait()
+    for z in range(GROUPS):
+        at = pl.ds(pl.multiple_of(p.chip * part + z * piece, 16), piece)
+        total = gm[p.k, at, :].astype(F32) + gk[at, :].astype(F32)
+        for d in range(1, p.chips):
+            chip = (p.chip + d) % p.chips
+            yc(chip, chip, z).wait_recv()
+            total = total + yr_[chip, z].astype(F32)
+        red[z] = total.astype(BF16)
     for d in range(1, GROUPS):
         to = (p.a + d) % GROUPS
         ac(p.a, to).wait_send()
         dc(p.a, to).wait_send()
         dc(to, to).wait_recv()
+    for d in range(1, p.chips):
+        for z in range(GROUPS):
+            yc((p.chip + d) % p.chips, p.chip, z).wait_send()
 
 
 def mlp(n, att, rp, cp, gfull, woa, wu, wd):
     rows, width = rp.shape
     ff = wu.shape[1]
     pk = rows * 3 // 2
+    chips = n // GROUPS // 2
+    piece = ff // GROUPS // chips
     sds = jax.ShapeDtypeStruct
     v = pltpu.VMEM
     return pl.pallas_call(
@@ -538,12 +597,13 @@
         out_shape=(
             sds((rows, width - 1), BF16),
             sds((rows, width), F32),
-            sds((2 * ff + width // 2, width), BF16),
+            sds((GROUPS, piece, width), BF16),
+            sds((width // 2, width), BF16),
             sds((GROUPS, pk, 128), BF16),
             sds((8, width), F32),
         ),
         in_specs=[VM] * 7,
-        out_specs=[VM] * 5,
+        out_specs=[VM] * 6,
         scratch_shapes=[
             v((GROUPS, pk, 128), BF16),
             v((2, pk, 128), BF16),
@@ -560,13 +620,20 @@
             v((GROUPS, pk, 128), BF16),
             v((2, rows, width), BF16),
             v((rows, width), F32),
+            v((2, ff, width), BF16),
+            v((ff, width), BF16),
+            v((chips, GROUPS, piece, width), BF16),
+            v((chips, GROUPS, piece, width), BF16),
             DMA((8,)),
             DMA((8,)),
-            DMA((2,)),
             DMA((GROUPS,)),
             DMA((GROUPS,)),
             DMA((GROUPS,)),
             DMA((GROUPS,)),
+            DMA((chips,)),
+            DMA((chips,)),
+            DMA((chips, GROUPS)),
+            DMA((chips, GROUPS)),
         ],
         compiler_params=pltpu.CompilerParams(
             collective_id=1, has_side_effects=True, vmem_limit_bytes=VLIM
@@ -574,12 +641,251 @@
     )(att, rp, cp, gfull, woa, wu, wd)
 
 
-def attend_back_kernel(meta, q3, kv, o3, l3, dog, dqp, dkvb, do3, dkv):
-    rows = q3.shape[1] // GROUPS
-    keys = kv.shape[0] // GROUPS
+def back_kernel(
+    n, lens, q3, kv, o3, l3, dog, wg, h1, rp, gmid, gfull, dg2, red, go,
+    gin, gq, gains, res, goo,
+    do3, dq3, kvc, dkv, dkvb, rk, ry, wfull, gps, gpr, gqb, qk, qx, qy,
+    g0, gk, gx, gy, ga, left, right, sumr, suml, ok, os_, oy, oz, ozr,
+    xs, xr, ls, vs, ks, kr, ys, yr, zs, zr, ws, wr, qs, qr, ns, nr, bs, br, cs, cr,
+    rs_, rr, ls_, lr, as_, ar, es, er, fs, fr, ts, tr, us, ur, is_, ir,
+):
+    p = Place(n)
+    rows, width = rp.shape
+    half = width // 2
+    quarter = width // 4
+    last = GROUPS - 1
+    keys = dkv.shape[0]
     size = min(SUB, keys)
-    first_query = meta[0] * rows
-    dead = jnp.where(meta[1] > keys, 0.0, -MASKED).astype(F32)
+    subs = keys // size
+    slots = kvc.shape[0]
+    others = [(p.chip + d) % p.chips for d in range(1, p.chips)]
+    line = [(p.a + d) % GROUPS for d in range(1, GROUPS)]
+    ready = greet(p, xpeer=True, sibling=True, chips=True, line=True)
+    at_x = pl.ds(pl.multiple_of(p.x * half, half), half)
+    local = [
+        pltpu.make_async_copy(wg.at[g], wfull.at[g, at_x], ls.at[g]) for g in range(GROUPS)
+    ]
+
+    def chunk_of(i):
+        return (p.a + 1 + i) % GROUPS
+
+    def fetch(i):
+        c = chunk_of(i)
+        src = kv.at[pl.ds(pl.multiple_of(c * keys, keys), keys)]
+        return pltpu.make_async_copy(src, kvc.at[i % slots], vs.at[i % slots])
+
+    fetch(0).start()
+    for c in local:
+        c.start()
+    wx = [
+        rcopy(wg.at[g], wfull.at[g, at_x], xs.at[g], xr.at[g], p.xpeer()) for g in range(GROUPS)
+    ]
+
+    def rightward(z, src):
+        return rcopy(src, left.at[z], rs_.at[z], rr.at[z], p.on_line(p.a + 1))
+
+    def leftward(z, src):
+        return rcopy(src, right.at[z], ls_.at[z], lr.at[z], p.on_line(p.a - 1))
+
+    def reduce_step(s):
+        @pl.when((p.a >= 1) & (p.a <= s))
+        def _():
+            z = last + p.a - s
+            rightward(z, sumr.at[z]).wait_recv()
+            if s < last:
+                sumr[z] = (red[z].astype(F32) + left[z].astype(F32)).astype(BF16)
+                rightward(z, sumr.at[z]).start()
+
+        b = last - p.a
+
+        @pl.when((b >= 1) & (b <= s))
+        def _():
+            z = s - b
+            leftward(z, suml.at[z]).wait_recv()
+            if s < last:
+                suml[z] = (red[z].astype(F32) + right[z].astype(F32)).astype(BF16)
+                leftward(z, suml.at[z]).start()
+
+    def line_share(z, dst, sem):
+        r = res.at[p.k, p.chip, z]
+        return rcopy(r, r, as_.at[sem], ar.at[z], p.on_line(dst))
+
+    def chip_share(chip, z, dst):
+        r = res.at[p.k, chip, z]
+        return rcopy(r, r, es.at[dst, z], er.at[chip, z], p.on_chip(dst))
+
+    def core_share(core, chip, z):
+        r = res.at[core, chip, z]
+        return rcopy(r, r, fs.at[chip, z], fr.at[chip, z], p.sibling())
+
+    def spread(z):
+        for c in others:
+            chip_share(p.chip, z, c).start()
+        core_share(p.k, p.chip, z).start()
+
+    def gather_first():
+        z = p.a
+        res[p.k, p.chip, z] = red[z]
+
+        @pl.when(p.a > 0)
+        def _():
+            cur = res[p.k, p.chip, z].astype(F32)
+            res[p.k, p.chip, z] = (cur + left[z].astype(F32)).astype(BF16)
+
+        @pl.when(p.a < last)
+        def _():
+            cur = res[p.k, p.chip, z].astype(F32)
+            res[p.k, p.chip, z] = (cur + right[z].astype(F32)).astype(BF16)
+            line_share(z, p.a + 1, 0).start()
+
+        @pl.when(p.a > 0)
+        def _():
+            line_share(z, p.a - 1, 1).start()
+
+        spread(z)
+
+    def gather_step(s):
+        @pl.when(p.a - s >= 0)
+        def _():
+            line_share(p.a - s, p.a, 0).wait_recv()
+
+            @pl.when(p.a < last)
+            def _():
+                line_share(p.a - s, p.a + 1, 2 * s).start()
+
+            spread(p.a - s)
+
+        @pl.when(p.a + s <= last)
+        def _():
+            line_share(p.a + s, p.a, 0).wait_recv()
+
+            @pl.when(p.a > 0)
+            def _():
+                line_share(p.a + s, p.a - 1, 2 * s + 1).start()
+
+            spread(p.a + s)
+
+    def pass_on(z):
+        for c in others:
+            chip_share(c, z, c).wait_recv()
+            core_share(p.k, c, z).start()
+
+    orow = go.shape[0] // 2
+    opart = orow // GROUPS
+
+    def out_core():
+        at = pl.ds(pl.multiple_of((1 - p.k) * orow, orow), orow)
+        return rcopy(go.at[at], ok, is_.at[0], ir.at[0], p.sibling())
+
+    def out_chip(chip, slot):
+        return rcopy(os_, oy.at[slot], ts.at[chip], tr.at[slot], p.on_chip(chip))
+
+    def out_line(slot, to):
+        return rcopy(oz.at[to], ozr.at[slot], us.at[to], ur.at[slot], p.on_line(to))
+
+    def out_back(slot, to):
+        r = goo.at[p.k, slot]
+        return rcopy(r, r, us.at[GROUPS + to], ur.at[GROUPS + slot], p.on_line(to))
+
+    def out_share(core, z):
+        r = goo.at[core, z]
+        return rcopy(r, r, is_.at[1 + z], ir.at[1 + z], p.sibling())
+
+    def out_1():
+        out_core().wait()
+        at = pl.ds(pl.multiple_of(p.k * orow, orow), orow)
+        os_[...] = (go[at, :].astype(F32) + ok[...].astype(F32)).astype(BF16)
+        for c in others:
+            out_chip(c, p.chip).start()
+
+    def out_2():
+        total = os_[...].astype(F32)
+        for c in others:
+            out_chip(c, c).wait_recv()
+            total = total + oy[c].astype(F32)
+        for z in range(GROUPS):
+            oz[z] = total[z * opart : (z + 1) * opart].astype(BF16)
+        for z in line:
+            out_line(p.a, z).start()
+
+    def out_3():
+        total = oz[p.a].astype(F32)
+        for z in line:
+            out_line(z, z).wait_recv()
+            total = total + ozr[z].astype(F32)
+        goo[p.k, p.a] = total.astype(BF16)
+        for z in line:
+            out_back(p.a, z).start()
+        out_share(p.k, p.a).start()
+
+    def kc(i, chip):
+        c = chunk_of(i)
+        at = pl.ds(pl.multiple_of((chip * 2 + 1 - p.k) * rows, rows), rows)
+        return rcopy(
+            dkvb.at[at], rk.at[c, chip], ks.at[c, chip], kr.at[c, chip], p.sibling()
+        )
+
+    def yc(c, chip, slot):
+        return rcopy(rk.at[c, chip], ry.at[c, slot], ys.at[c, chip], yr.at[c, slot], p.on_chip(chip))
+
+    def zkv(slot, to):
+        lanes = pl.ds(256, 384)
+        return rcopy(
+            gps.at[to, :, lanes], gpr.at[slot, :, lanes], zs.at[to], zr.at[slot], p.on_line(to)
+        )
+
+    def zq(slot, to):
+        lanes = pl.ds(0, 256)
+        return rcopy(
+            gps.at[to, :, lanes], gpr.at[slot, :, lanes], ws.at[to], wr.at[slot], p.on_line(to)
+        )
+
+    def mine(chip):
+        at = pl.ds(pl.multiple_of((chip * 2 + p.k) * rows, rows), rows)
+        return dkvb[at, :].astype(F32)
+
+    def kv_1(i):
+        dkvb[...] = dkv[...].astype(BF16)
+        for c in others:
+            kc(i, c).start()
+        kc(i, p.chip).start()
+
+    def kv_2(i):
+        c = chunk_of(i)
+        for chip in others:
+            kc(i, chip).wait()
+            rk[c, chip] = (mine(chip) + rk[c, chip].astype(F32)).astype(BF16)
+            yc(c, chip, p.chip).start()
+        kc(i, p.chip).wait()
+        rk[c, p.chip] = (mine(p.chip) + rk[c, p.chip].astype(F32)).astype(BF16)
+
+    def kv_3(i, send):
+        c = chunk_of(i)
+        total = rk[c, p.chip].astype(F32)
+        for chip in others:
+            yc(c, chip, chip).wait_recv()
+            total = total + ry[c, chip].astype(F32)
+        gps[c, :, 256:640] = total.astype(BF16)
+        if send:
+            zkv(p.a, c).start()
+
+    ready()
+    out_core().start()
+
+    @pl.when(p.a == 0)
+    def _():
+        for z in range(last, 0, -1):
+            rightward(z, red.at[z]).start()
+
+    @pl.when(p.a == last)
+    def _():
+        for z in range(last):
+            leftward(z, red.at[z]).start()
+
+    for c in wx:
+        c.start()
+
+    first_query = p.b * rows
     low = low_half((rows, 128))
     for z in range(GROUPS):
         at = pl.ds(z * rows, rows)
@@ -590,129 +896,130 @@
         top, bottom = unpack_tail(dog[z, rows:, :])
         do3[2, pl.ds(z * rows, rows // 2), :] = top
         do3[2, pl.ds(z * rows + rows // 2, rows // 2), :] = bottom
-    dkv[...] = jnp.zeros_like(dkv)
-
-    def head(h, carry):
-        kt = pl.multiple_of(128 * (h // 2), 128)
-        vt = pl.multiple_of(jnp.where(h == 2, 128, 256), 128)
-        for z in range(GROUPS):
-            at_q = pl.ds(z * rows, rows)
-            q = q3[h, at_q, :]
-            do = do3[h, at_q, :]
-            lse = l3[h, at_q, 0:1]
-            delta = jnp.sum(o3[h, at_q, :] * do.astype(F32), axis=1, keepdims=True)
-            dq = jnp.zeros((rows, 128), F32)
-            for c, s in key_steps(z, keys):
-                at = pl.ds(c * keys + s * size, size)
-                k = kv[at, pl.ds(kt, 128)]
-                scores = dg(q, k, NT) * (SCALE * LOG2E)
-                if c == z:
-                    scores = jnp.where(
-                        causal(scores.shape, s, size, first_query), scores, MASKED
-                    )
-                weights = jnp.exp2(scores - (lse + dead if c > 0 else lse))
-                gp = dg(do, kv[at, pl.ds(vt, 128)], NT)
-                gs = (weights * (gp - delta)).astype(BF16)
-                dq = dq + dot(gs, k)
-                dkv[at, pl.ds(vt, 128)] += dg(weights.astype(BF16), do, TN)
-                dkv[at, pl.ds(kt, 128)] += dg(gs, q, TN) * SCALE
-            dq = dq * SCALE
+        for h in range(GH):
+            delta = jnp.sum(o3[h, at, :] * do3[h, at, :].astype(F32), axis=1, keepdims=True)
+            gqb[h * rows : (h + 1) * rows, z * 128 : (z + 1) * 128] = jnp.broadcast_to(delta, (rows, 128))
+    dq3[...] = jnp.zeros_like(dq3)
+    gone = jnp.where(lens[0] > keys, 0.0, -MASKED).astype(F32)
+
+    def chunk(i, carry):
+        c = chunk_of(i)
+        fetch(i).wait()
+
+        if slots > 1:
+
+            @pl.when(i < last)
+            def _():
+                fetch(i + 1).start()
+
+        dead = jnp.where(c > 0, gone, 0.0)
+
+        def head(h, carry):
+            kt = pl.multiple_of(128 * (h // 2), 128)
+            vt = pl.multiple_of(jnp.where(h == 2, 128, 256), 128)
+
+            def step(z, masked):
+                at_q = pl.ds(pl.multiple_of(z * rows, rows), rows)
+                q = q3[h, at_q, :]
+                do = do3[h, at_q, :]
+                lse = l3[h, at_q, 0:1] + dead
+                delta = gqb[
+                    pl.ds(pl.multiple_of(h * rows, rows), rows),
+                    pl.ds(pl.multiple_of(z * 128, 128), 128),
+                ][:, 0:1]
+                for sub in range(subs):
+                    at = pl.ds(sub * size, size)
+                    k = kvc[i % slots, at, pl.ds(kt, 128)]
+                    v = kvc[i % slots, at, pl.ds(vt, 128)]
+                    scores = dg(q, k, NT) * (SCALE * LOG2E)
+                    if masked:
+                        scores = jnp.where(
+                            causal(scores.shape, sub, size, first_query), scores, MASKED
+                        )
+                    weights = jnp.exp2(scores - lse)
+                    gp = dg(do, v, NT)
+                    gs = (weights * (gp - delta)).astype(BF16)
+                    dq3[h, at_q, :] += dot(gs, k)
+                    gv = dg(weights.astype(BF16), do, TN)
+                    gk_ = dg(gs, q, TN) * SCALE
+                    if masked:
+                        dkv[at, pl.ds(kt, 128)] = jnp.where(h == 1, dkv[at, pl.ds(kt, 128)], 0.0) + gk_
+                        dkv[at, pl.ds(vt, 128)] = jnp.where(h == 0, 0.0, dkv[at, pl.ds(vt, 128)]) + gv
+                    else:
+                        dkv[at, pl.ds(kt, 128)] += gk_
+                        dkv[at, pl.ds(vt, 128)] += gv
+
+            step(c, True)
+
+            def rest(z, carry):
+                step(z, False)
+                return carry
+
+            lax.fori_loop(c + 1, GROUPS, rest, 0)
 
             @pl.when(h == 0)
             def _():
-                dqp[at_q, 0:128] = dq.astype(BF16)
+                @pl.when(i >= 1)
+                def _():
+                    kv_2(i - 1)
 
             @pl.when(h == 1)
             def _():
-                dqp[at_q, 0:128] = jnp.where(low, dqp[at_q, 0:128], dq.astype(BF16))
+                @pl.when(i >= 2)
+                def _():
+                    kv_3(i - 2, True)
+
+                @pl.when(i == 2)
+                def _():
+                    reduce_step(2)
+
+                @pl.when(i == 3)
+                def _():
+                    reduce_step(3)
+                    gather_first()
 
             @pl.when(h == 2)
             def _():
-                dqp[at_q, 128:256] = jnp.where(low, dq, 0.0).astype(BF16)
-
+                @pl.when(i == 0)
+                def _():
+                    out_1()
+
+                @pl.when(i == 1)
+                def _():
+                    reduce_step(1)
+                    out_2()
+
+                @pl.when(i == 2)
+                def _():
+                    out_3()
+
+            return carry
+
+        lax.fori_loop(0, GH, head, 0)
+        if slots == 1:
+
+            @pl.when(i < last)
+            def _():
+                fetch(i + 1).start()
+
+        kv_1(i)
         return carry
 
-    lax.fori_loop(0, GH, head, 0)
-    dkvb[...] = dkv[...].astype(BF16)
-
-
-def attend_back(meta, q3, kv, o3, l3, dog):
-    sds = jax.ShapeDtypeStruct
-    return pl.pallas_call(
-        attend_back_kernel,
-        name="attend_back",
-        out_shape=(sds((q3.shape[1], 256), BF16), sds(kv.shape, BF16)),
-        in_specs=[SM] + [VM] * 5,
-        out_specs=[VM] * 2,
-        scratch_shapes=[pltpu.VMEM(q3.shape, BF16), pltpu.VMEM(kv.shape, F32)],
-        compiler_params=pltpu.CompilerParams(vmem_limit_bytes=VLIM),
-    )(meta, q3, kv, o3, l3, dog)
-
-
-def finish_kernel(
-    n, dqp, dkvb, wg, h1, rp, gmid, gfull, dg2,
-    gin, gq, gains,
-    wfull, rk, sy, ry, gps, gpr, gqb, qk, q1, qx, q2, qy, g0, gk, gx, gy, ga,
-    xs, xr, ls, ks, kr, ys, yr, zs, zr, qs, qr, ns, nr, bs, br, cs, cr,
-):
-    p = Place(n)
-    rows, width = rp.shape
-    half = width // 2
-    quarter = width // 4
-    ready = greet(p, xpeer=True, sibling=True, chips=True, line=True)
-    at_x = pl.ds(pl.multiple_of(p.x * half, half), half)
-    local = [
-        pltpu.make_async_copy(wg.at[g], wfull.at[g, at_x], ls.at[g]) for g in range(GROUPS)
-    ]
-    for c in local:
-        c.start()
-    ready()
-    wx = [
-        rcopy(wg.at[g], wfull.at[g, at_x], xs.at[g], xr.at[g], p.xpeer()) for g in range(GROUPS)
-    ]
-
-    def block(ref, z, b):
-        return ref.at[pl.ds(pl.multiple_of((z * p.m + b) * rows, rows), rows)]
-
-    def kc(z, chip):
-        return rcopy(
-            block(dkvb, z, chip * 2 + 1 - p.k), rk.at[z, chip], ks.at[z, chip], kr.at[z, chip],
-            p.sibling(),
-        )
-
-    def yc(z, chip, slot):
-        return rcopy(sy.at[z, chip], ry.at[z, slot], ys.at[z, chip], yr.at[z, slot], p.on_chip(chip))
-
-    def zc(slot, to):
-        return rcopy(gps.at[to], gpr.at[slot], zs.at[to], zr.at[slot], p.on_line(to))
-
-    order = [(p.a + d) % GROUPS for d in range(1, GROUPS)] + [p.a]
-    for z in order:
-        for d in range(1, p.chips):
-            kc(z, (p.chip + d) % p.chips).start()
-        kc(z, p.chip).start()
-    for c in wx:
-        c.start()
-    for z in order:
-        for d in range(1, p.chips):
-            chip = (p.chip + d) % p.chips
-            kc(z, chip).wait()
-            mine = dkvb[pl.ds(pl.multiple_of((z * p.m + chip * 2 + p.k) * rows, rows), rows), :]
-            sy[z, chip] = (mine.astype(F32) + rk[z, chip].astype(F32)).astype(BF16)
-            yc(z, chip, p.chip).start()
-    for i, z in enumerate(order):
-        kc(z, p.chip).wait()
-        mine = dkvb[pl.ds(pl.multiple_of((z * p.m + p.b) * rows, rows), rows), :]
-        total = mine.astype(F32) + rk[z, p.chip].astype(F32)
-        for d in range(1, p.chips):
-            chip = (p.chip + d) % p.chips
-            yc(z, chip, chip).wait_recv()
-            total = total + ry[z, chip].astype(F32)
-        gps[z, :, 0:256] = dqp[pl.ds(pl.multiple_of(z * rows, rows), rows), :]
-        gps[z, :, 256:640] = total.astype(BF16)
-        if i < GROUPS - 1:
-            zc(p.a, z).start()
+    lax.fori_loop(0, GROUPS, chunk, 0)
+    kv_3(2, True)
+    for d in range(1, GROUPS + 1):
+        z = (p.a + d) % GROUPS
+        at = pl.ds(pl.multiple_of(z * rows, rows), rows)
+        gps[z, :, 0:128] = (jnp.where(low, dq3[0, at, :], dq3[1, at, :]) * SCALE).astype(BF16)
+        gps[z, :, 128:256] = (jnp.where(low, dq3[2, at, :], 0.0) * SCALE).astype(BF16)
+        if d < GROUPS:
+            zq(p.a, z).start()
+    kv_2(3)
+    gather_step(1)
+    kv_3(3, False)
     gpr[p.a] = gps[p.a]
+
+    gqb[...] = jnp.zeros_like(gqb)
 
     def rowdot(z, carry):
         for t in range(width // 256):
@@ -720,56 +1027,62 @@
             gqb[at, :] += dg(h1[z, :, at], gps[z], TN)
         return carry
 
-    gqb[...] = jnp.zeros_like(gqb)
     lax.fori_loop(0, GROUPS, rowdot, 0)
 
-    def part(i, core):
+    def rows_of(i, core):
         return pl.ds(pl.multiple_of(i * half + core * quarter, quarter), quarter)
 
     for i in range(2):
-        qk[0, i] = gqb[part(i, 1 - p.k), :].astype(BF16)
+        qk[0, i] = gqb[rows_of(i, 1 - p.k), :].astype(BF16)
     q_k = rcopy(qk.at[0], qk.at[1], qs.at[0], qr.at[0], p.sibling())
     q_k.start()
+    for c in local:
+        c.wait()
     q_k.wait()
     for i in range(2):
-        q1[i] = gqb[part(i, p.k), :] + qk[1, i].astype(F32)
-    qx[0] = q1[1 - p.x].astype(BF16)
+        gqb[rows_of(i, p.k), :] += qk[1, i].astype(F32)
+    qx[0] = gqb[rows_of(1 - p.x, p.k), :].astype(BF16)
     q_x = rcopy(qx.at[0], qx.at[1], qs.at[1], qr.at[1], p.xpeer())
     q_x.start()
+    gather_step(2)
     q_x.wait()
-    q2[...] = q1[p.x] + qx[1].astype(F32)
-    qy[p.chip] = q2[...].astype(BF16)
+    gqb[rows_of(p.x, p.k), :] += qx[1].astype(F32)
+    qy[p.chip] = gqb[rows_of(p.x, p.k), :].astype(BF16)
 
     def qc(chip, slot):
         return rcopy(qy.at[p.chip], qy.at[slot], ns.at[chip], nr.at[slot], p.on_chip(chip))
 
-    for d in range(1, p.chips):
-        qc((p.chip + d) % p.chips, p.chip).start()
-    total = q2[...]
-    for d in range(1, p.chips):
-        chip = (p.chip + d) % p.chips
-        qc(chip, chip).wait_recv()
-        total = total + qy[chip].astype(F32)
-    gq[p.a, p.k] = total.astype(BF16)
-
-    def bc(slot, to):
-        return rcopy(gq.at[slot, p.k], gq.at[slot, p.k], bs.at[to], br.at[slot], p.on_line(to))
-
-    def sc(slot, core):
-        return rcopy(gq.at[slot, core], gq.at[slot, core], cs.at[slot], cr.at[slot], p.sibling())
-
-    for d in range(1, GROUPS):
-        bc(p.a, (p.a + d) % GROUPS).start()
-    sc(p.a, p.k).start()
-    for c in local:
-        c.wait()
+    for c in others:
+        qc(c, p.chip).start()
     for c in wx:
         c.wait()
     h = dg(gpr[p.a], wfull[p.a], NT)
-    for d in range(1, GROUPS):
-        g = (p.a + d) % GROUPS
-        zc(g, g).wait_recv()
+    for g in line:
+        zkv(g, g).wait_recv()
+        zq(g, g).wait_recv()
         h = h + dg(gpr[g], wfull[g], NT)
+    total = gqb[rows_of(p.x, p.k), :]
+    for c in others:
+        qc(c, c).wait_recv()
+        total = total + qy[c].astype(F32)
+    gq[p.a, p.k] = total.astype(BF16)
+
+    def bc(slot, to, sem):
+        r = gq.at[slot, p.k]
+        return rcopy(r, r, bs.at[sem], br.at[slot], p.on_line(to))
+
+    def sc(slot, core):
+        return rcopy(gq.at[slot, core], gq.at[slot, core], cs.at[slot], cr.at[slot], p.sibling())
+
+    @pl.when(p.a < last)
+    def _():
+        bc(p.a, p.a + 1, 0).start()
+
+    @pl.when(p.a > 0)
+    def _():
+        bc(p.a, p.a - 1, 1).start()
+
+    sc(p.a, p.k).start()
     u = ext_of(rp[...].astype(F32))
     inv = inv_rms(u)
     gain = jnp.concatenate([gfull[0, 0:1, :], gfull[1, 0:1, :]], axis=1)
@@ -780,284 +1093,193 @@
     g0[...] = jnp.where(which == 0, first, dg2[...])
     g_k = rcopy(g0, gk, qs.at[2], qr.at[2], p.sibling())
     g_k.start()
+    gather_step(3)
+    for z in range(GROUPS):
+        pass_on(z)
     g_k.wait()
     g0[...] += gk[...]
     g_x = rcopy(g0, gx, qs.at[3], qr.at[3], p.xpeer())
     g_x.start()
-    g_x.wait()
-    gy[p.chip] = g0[...] + gx[...]
-
-    def gc(chip, slot):
-        return rcopy(gy.at[p.chip], gy.at[slot], ys.at[GROUPS, chip], yr.at[GROUPS, slot], p.on_chip(chip))
-
-    for d in range(1, p.chips):
-        gc((p.chip + d) % p.chips, p.chip).start()
-    for d in range(1, p.chips):
-        chip = (p.chip + d) % p.chips
-        gc(chip, chip).wait_recv()
-    total = gy[0]
-    for chip in range(1, p.chips):
-        total = total + gy[chip]
-    ga[p.a] = total
-
-    def lc(slot, to):
-        return rcopy(ga.at[p.a], ga.at[slot], zs.at[GROUPS + to], zr.at[GROUPS + slot], p.on_line(to))
-
-    for d in range(1, GROUPS):
-        lc(p.a, (p.a + d) % GROUPS).start()
-    for d in range(1, GROUPS):
-        g = (p.a + d) % GROUPS
+    for s in range(1, GROUPS):
+
+        @pl.when(p.a - s >= 0)
+        def _():
+            bc(p.a - s, p.a, 0).wait_recv()
+
+            @pl.when(p.a < last)
+            def _():
+                bc(p.a - s, p.a + 1, 2 * s).start()
+
+            sc(p.a - s, p.k).start()
+
+        @pl.when(p.a + s <= last)
+        def _():
+            bc(p.a + s, p.a, 0).wait_recv()
+
+            @pl.when(p.a > 0)
+            def _():
+                bc(p.a + s, p.a - 1, 2 * s + 1).start()
+
+            sc(p.a + s, p.k).start()
+
+        if s == 1:
+            g_x.wait()
+            gy[p.chip] = g0[...] + gx[...]
+
+            def gc(chip, slot):
+                return rcopy(
+                    gy.at[p.chip], gy.at[slot], ys.at[GROUPS, chip], yr.at[GROUPS, slot],
+                    p.on_chip(chip),
+                )
+
+            for c in others:
+                gc(c, p.chip).start()
+        if s == 2:
+            for c in others:
+                gc(c, c).wait_recv()
+            total = gy[0]
+            for c in range(1, p.chips):
+                total = total + gy[c]
+            ga[p.a] = total
+
+            def lc(slot, to):
+                return rcopy(
+                    ga.at[p.a], ga.at[slot], zs.at[GROUPS + to], zr.at[GROUPS + slot], p.on_line(to)
+                )
+
+            for g in line:
+                lc(p.a, g).start()
+    for g in line:
         lc(g, g).wait_recv()
     total = ga[0]
     for g in range(1, GROUPS):
         total = total + ga[g]
     gains[...] = total
-    for d in range(1, GROUPS):
-        g = (p.a + d) % GROUPS
-        bc(g, g).wait_recv()
-        sc(g, p.k).start()
+    for g in line:
+        out_back(g, g).wait_recv()
+        out_share(p.k, g).start()
     for g in range(GROUPS):
         sc(g, 1 - p.k).wait_recv()
         sc(g, p.k).wait_send()
-    for d in range(1, p.chips):
-        chip = (p.chip + d) % p.chips
-        qc(chip, p.chip).wait_send()
-        gc(chip, p.chip).wait_send()
-        for z in range(GROUPS):
-            yc(z, chip, p.chip).wait_send()
-    for d in range(1, GROUPS):
-        to = (p.a + d) % GROUPS
-        zc(p.a, to).wait_send()
-        bc(p.a, to).wait_send()
-        lc(p.a, to).wait_send()
-
-
-def finish(n, dqp, dkvb, wg, h1, rp, gmid, gfull, dg2):
+        out_share(1 - p.k, g).wait_recv()
+        out_share(p.k, g).wait_send()
+        for c in range(p.chips):
+            core_share(1 - p.k, c, g).wait_recv()
+            core_share(p.k, c, g).wait_send()
+        for c in others:
+            chip_share(p.chip, g, c).wait_send()
+            yc(g, c, p.chip).wait_send()
+    for c in others:
+        qc(c, p.chip).wait_send()
+        gc(c, p.chip).wait_send()
+        out_chip(c, p.chip).wait_send()
+    for g in line:
+        zkv(p.a, g).wait_send()
+        zq(p.a, g).wait_send()
+        lc(p.a, g).wait_send()
+        out_line(p.a, g).wait_send()
+        out_back(p.a, g).wait_send()
+    for s in range(GROUPS):
+
+        @pl.when((p.a - s >= 0) & (p.a < last))
+        def _():
+            bc(p.a - s, p.a + 1, 2 * s).wait_send()
+            line_share(p.a - s, p.a + 1, 2 * s).wait_send()
+
+        @pl.when((p.a + s <= last) & (p.a > 0))
+        def _():
+            bc(p.a + s, p.a - 1, 2 * s + 1).wait_send()
+            line_share(p.a + s, p.a - 1, 2 * s + 1).wait_send()
+
+        if s > 0:
+
+            @pl.when(p.a + s <= last)
+            def _():
+                rightward(p.a + s, red.at[0]).wait_send()
+
+            @pl.when(p.a - s >= 0)
+            def _():
+                leftward(p.a - s, red.at[0]).wait_send()
+
+
+def back(n, lens, q3, kv, o3, l3, dog, wg, h1, rp, gmid, gfull, dg2, red, go):
     rows, width = rp.shape
-    half = width // 2
     quarter = width // 4
     lanes = wg.shape[2]
     chips = n // GROUPS // 2
+    keys = kv.shape[0] // GROUPS
+    piece = red.shape[1]
+    orow = go.shape[0] // 2
     sds = jax.ShapeDtypeStruct
     v = pltpu.VMEM
+    sem = lambda *shape: [DMA(shape), DMA(shape)]
     return pl.pallas_call(
-        functools.partial(finish_kernel, n),
-        name="finish",
+        functools.partial(back_kernel, n),
+        name="back",
         out_shape=(
             sds((rows, width - 1), F32),
             sds((GROUPS, 2, quarter, lanes), BF16),
             sds((8, width), F32),
+            sds((2, chips, GROUPS, piece, width), BF16),
+            sds((2, GROUPS, orow // GROUPS, width), BF16),
         ),
-        in_specs=[VM, VM, ANY] + [VM] * 5,
-        out_specs=[VM] * 3,
+        in_specs=[SM, VM, ANY, VM, VM, VM, ANY] + [VM] * 7,
+        out_specs=[VM] * 5,
         scratch_shapes=[
-            v((GROUPS, width, lanes), BF16),
+            v(q3.shape, BF16),
+            v(q3.shape, F32),
+            v((2 if keys <= SUB else 1, keys, 384), BF16),
+            v((keys, 384), F32),
+            v((keys, 384), BF16),
             v((GROUPS, chips, rows, 384), BF16),
             v((GROUPS, chips, rows, 384), BF16),
-            v((GROUPS, chips, rows, 384), BF16),
+            v((GROUPS, width, lanes), BF16),
             v((GROUPS, rows, lanes), BF16),
             v((GROUPS, rows, lanes), BF16),
             v((width, lanes), F32),
             v((2, 2, quarter, lanes), BF16),
-            v((2, quarter, lanes), F32),
             v((2, quarter, lanes), BF16),
-            v((quarter, lanes), F32),
             v((chips, quarter, lanes), BF16),
             v((8, width), F32),
             v((8, width), F32),
             v((8, width), F32),
             v((chips, 8, width), F32),
             v((GROUPS, 8, width), F32),
-            DMA((GROUPS,)),
-            DMA((GROUPS,)),
-            DMA((GROUPS,)),
-            DMA((GROUPS, chips)),
-            DMA((GROUPS, chips)),
-            DMA((GROUPS + 1, chips)),
-            DMA((GROUPS + 1, chips)),
-            DMA((2 * GROUPS,)),
-            DMA((2 * GROUPS,)),
-            DMA((4,)),
-            DMA((4,)),
-            DMA((chips,)),
-            DMA((chips,)),
-            DMA((GROUPS,)),
-            DMA((GROUPS,)),
-            DMA((GROUPS,)),
-            DMA((GROUPS,)),
-        ],
-        compiler_params=pltpu.CompilerParams(
-            collective_id=2, has_side_effects=True, vmem_limit_bytes=VLIM
-        ),
-    )(dqp, dkvb, wg, h1, rp, gmid, gfull, dg2)
-
-
-def sum_kernel(n, gm, res, rk, run, left, right, ry, ks, kr, zs, zr, ys, yr, as_, ar, cs, cr):
-    p = Place(n)
-    half = gm.shape[0] // 2
-    piece = half // GROUPS
-    ready = greet(p, sibling=True, chips=True, line=True)
-    ready()
-
-    def gm_at(core, z):
-        return pl.ds(pl.multiple_of(core * half + z * piece, 16), piece)
-
-    def kc(z):
-        return rcopy(gm.at[gm_at(1 - p.k, z)], rk.at[z], ks.at[z], kr.at[z], p.sibling())
-
-    for z in range(GROUPS):
-        kc(z).start()
-    for z in range(GROUPS):
-        kc(z).wait()
-        run[z] = (gm[gm_at(p.k, z), :].astype(F32) + rk[z].astype(F32)).astype(BF16)
-
-    def rightward(z):
-        return rcopy(run.at[z], left.at[z], zs.at[0, z], zr.at[0, z], p.on_line(p.a + 1))
-
-    def leftward(z):
-        return rcopy(run.at[z], right.at[z], zs.at[1, z], zr.at[1, z], p.on_line(p.a - 1))
-
-    for s in range(GROUPS - 1, 0, -1):
-        @pl.when(p.a + s < GROUPS)
-        def _():
-            @pl.when(p.a > 0)
-            def _():
-                rightward(p.a + s).wait_recv()
-                run[p.a + s] = (run[p.a + s].astype(F32) + left[p.a + s].astype(F32)).astype(BF16)
-
-            rightward(p.a + s).start()
-
-        @pl.when(p.a - s >= 0)
-        def _():
-            @pl.when(p.a < GROUPS - 1)
-            def _():
-                leftward(p.a - s).wait_recv()
-                run[p.a - s] = (run[p.a - s].astype(F32) + right[p.a - s].astype(F32)).astype(BF16)
-
-            leftward(p.a - s).start()
-
-    @pl.when(p.a > 0)
-    def _():
-        rightward(p.a).wait_recv()
-        run[p.a] = (run[p.a].astype(F32) + left[p.a].astype(F32)).astype(BF16)
-
-    @pl.when(p.a < GROUPS - 1)
-    def _():
-        leftward(p.a).wait_recv()
-        run[p.a] = (run[p.a].astype(F32) + right[p.a].astype(F32)).astype(BF16)
-
-    def yc(chip, slot):
-        return rcopy(run.at[p.a], ry.at[slot], ys.at[chip], yr.at[slot], p.on_chip(chip))
-
-    for d in range(1, p.chips):
-        yc((p.chip + d) % p.chips, p.chip).start()
-    ry[p.chip] = run[p.a]
-    for d in range(1, p.chips):
-        chip = (p.chip + d) % p.chips
-        yc(chip, chip).wait_recv()
-    total = ry[0].astype(F32)
-    for chip in range(1, p.chips):
-        total = total + ry[chip].astype(F32)
-    res[gm_at(p.k, p.a), :] = total.astype(BF16)
-
-    def ac(z, dst, sem):
-        r = res.at[gm_at(p.k, z)]
-        return rcopy(r, r, as_.at[sem], ar.at[z], p.on_line(dst))
-
-    def sc(z, core):
-        r = res.at[gm_at(core, z)]
-        return rcopy(r, r, cs.at[z], cr.at[z], p.sibling())
-
-    @pl.when(p.a < GROUPS - 1)
-    def _():
-        ac(p.a, p.a + 1, 0).start()
-
-    @pl.when(p.a > 0)
-    def _():
-        ac(p.a, p.a - 1, 1).start()
-
-    sc(p.a, p.k).start()
-    for s in range(1, GROUPS):
-
-        @pl.when(p.a - s >= 0)
-        def _():
-            ac(p.a - s, p.a, 0).wait_recv()
-
-            @pl.when(p.a < GROUPS - 1)
-            def _():
-                ac(p.a - s, p.a + 1, 2 * s).start()
-
-            sc(p.a - s, p.k).start()
-
-        @pl.when(p.a + s < GROUPS)
-        def _():
-            ac(p.a + s, p.a, 0).wait_recv()
-
-            @pl.when(p.a > 0)
-            def _():
-                ac(p.a + s, p.a - 1, 2 * s + 1).start()
-
-            sc(p.a + s, p.k).start()
-
-    for z in range(GROUPS):
-        sc(z, 1 - p.k).wait_recv()
-        sc(z, p.k).wait_send()
-    for s in range(GROUPS):
-
-        @pl.when((p.a - s >= 0) & (p.a < GROUPS - 1))
-        def _():
-            ac(p.a - s, p.a + 1, 2 * s).wait_send()
-
-        @pl.when((p.a + s < GROUPS) & (p.a > 0))
-        def _():
-            ac(p.a + s, p.a - 1, 2 * s + 1).wait_send()
-
-        if s > 0:
-
-            @pl.when(p.a + s < GROUPS)
-            def _():
-                rightward(p.a + s).wait_send()
-
-            @pl.when(p.a - s >= 0)
-            def _():
-                leftward(p.a - s).wait_send()
-
-    for d in range(1, p.chips):
-        yc((p.chip + d) % p.chips, p.chip).wait_send()
-
-
-def sum_over_ctx(n, gm):
-    chips = n // GROUPS // 2
-    piece = gm.shape[0] // 2 // GROUPS
-    width = gm.shape[1]
-    v = pltpu.VMEM
-    return pl.pallas_call(
-        functools.partial(sum_kernel, n),
-        name="sum_over_ctx",
-        out_shape=jax.ShapeDtypeStruct(gm.shape, BF16),
-        in_specs=[VM],
-        out_specs=VM,
-        scratch_shapes=[
             v((GROUPS, piece, width), BF16),
             v((GROUPS, piece, width), BF16),
             v((GROUPS, piece, width), BF16),
             v((GROUPS, piece, width), BF16),
-            v((chips, piece, width), BF16),
+            v((orow, width), BF16),
+            v((orow, width), BF16),
+            v((chips, orow, width), BF16),
+            v((GROUPS, orow // GROUPS, width), BF16),
+            v((GROUPS, orow // GROUPS, width), BF16),
+            *sem(GROUPS),
             DMA((GROUPS,)),
-            DMA((GROUPS,)),
-            DMA((2, GROUPS)),
-            DMA((2, GROUPS)),
-            DMA((chips,)),
-            DMA((chips,)),
+            DMA((2,)),
+            *sem(GROUPS, chips),
+            *sem(GROUPS + 1, chips),
+            *sem(2 * GROUPS),
+            *sem(GROUPS),
+            *sem(4),
+            *sem(chips),
             DMA((2 * GROUPS,)),
             DMA((GROUPS,)),
+            *sem(GROUPS),
+            *sem(GROUPS),
+            *sem(GROUPS),
+            DMA((2 * GROUPS,)),
             DMA((GROUPS,)),
-            DMA((GROUPS,)),
+            *sem(chips, GROUPS),
+            *sem(chips, GROUPS),
+            *sem(chips),
+            *sem(2 * GROUPS),
+            *sem(1 + GROUPS),
         ],
         compiler_params=pltpu.CompilerParams(
-            collective_id=3, has_side_effects=True, vmem_limit_bytes=VLIM
+            collective_id=2, has_side_effects=True, vmem_limit_bytes=67043328
         ),
-    )(gm)
+    )(lens, q3, kv, o3, l3, dog, wg, h1, rp, gmid, gfull, dg2, red, go)
 
 
 def by_group(w):
@@ -1099,17 +1321,18 @@
 
     h1, q3, kv, _, woa, gfull = project(n, rp, gains, wg, wo)
     att, o3, l3 = attend(meta, q3, kv)
-    out, gmid, gm, dog, dg2 = mlp(n, att, rp, cp, gfull, woa, w_up, wd)
-    dqp, dkvb = attend_back(meta, q3, kv, o3, l3, dog)
-    gin, gq, gsum = finish(n, dqp, dkvb, wg, h1, rp, gmid, gfull, dg2)
-    res = sum_over_ctx(n, gm)
+    out, gmid, red, go, dog, dg2 = mlp(n, att, rp, cp, gfull, woa, w_up, wd)
+    gin, gq, gsum, res, goo = back(
+        n, lengths, q3, kv, o3, l3, dog, wg, h1, rp, gmid, gfull, dg2, red, go
+    )
 
     half = width // 2
     grad_qkv = from_groups(gq.reshape(GROUPS, half, -1).astype(F32))
     mine = lax.dynamic_slice_in_dim(gsum, lax.axis_index("fsdp") * half, half, 1)
-    up = jnp.concatenate([res[:width], res[width : 2 * width]], axis=1).astype(F32)
-    down = res[ff : 2 * ff, :narrow].astype(F32)
-    gout = res[2 * ff :, :narrow].astype(F32)
+    res = res.reshape(2, ff, width)
+    up = jnp.concatenate([res[0, :width], res[0, width:]], axis=1).astype(F32)
+    down = res[1, :, :narrow].astype(F32)
+    gout = goo.reshape(half, width)[:, :narrow].astype(F32)
     return out[None], gin[None], mine[0], grad_qkv, gout, mine[1], up, down
 
 

time: 428 us -> 321 us (0.75)
  Pallas kernels: 363 us -> 260 us
    pallas_call x3 -> x1, Pallas kernels: 237 us -> 129 us  [back(): pl.pallas_call(functools.partial(back_kernel, n), name='back', out_shape=...]
    pallas_call x1, Pallas kernels: 58.2 us -> 63.3 us  [mlp(): pl.pallas_call(functools.partial(mlp_kernel, n), name='mlp', out_shape=(s...]
where the time goes in v2:
time: 321 us; the launch traced here: 320 us
  Pallas kernels  260 us (81%)
  local copies, waits for them, and re-layouts  48.2 us (15%)
  other arithmetic  10.9 us (3%)
    pallas_call x1, Pallas kernels, back(): pl.pallas_call(functools.partial(back_kernel, n), name='back', out_shape=...  129 us
    pallas_call x1, Pallas kernels, mlp(): pl.pallas_call(functools.partial(mlp_kernel, n), name='mlp', out_shape=(s...  63.3 us
    pallas_call x1, Pallas kernels, project(): pl.pallas_call(functools.partial(project_kernel, n), name='project', out_...  47.4 us
    pallas_call x1, Pallas kernels, attend(): pl.pallas_call(attend_kernel, name='attend', out_shape=(sds((GROUPS, rows...  19.5 us
    transpose x2, local copies, waits for them, and re-layouts, from_groups(): t = g.reshape(GROUPS, r, 10, HD).transpose(1, 0, 2, 3)  14.7 us
    unnamed x12, local copies, waits for them, and re-layouts  10.6 us

profile of v2, /device:TPU:0, one launch (start us, length us, event | category | flops | bytes accessed | tf_op | source)
XLA Modules:
  0.0 320.3 jit_solution(9446082706839674889)
XLA Ops:
  1.3 0.7 pad_add_fusion.meta
  1.9 1.8 pad.21.rp
  3.7 0.7 stack.34
  4.4 0.7 stack.33
  5.1 0.6 fusion.4.gains
  5.7 3.9 %copy.19 = bf16[384,2304]{0,1:T(8,128)(2,1)} copy(bf16[384,2304]{1,0:T(8,128)(2,1)} %param.12) | data formatting | bytes 3538944 | tf_op args[3]
  9.6 3.4 %copy.20 = bf16[384,3,4,3,64]{4,0,2,3,1:T(8,128)(2,1)S(1)} copy(bf16[384,3,4,3,64]{0,4,3,2,1:T(8,128)(2,1)} %bitcast.60) | data formatting | bytes 3538944 | tf_op jit(solution)/shard_map/reshape | solution.py:1287
  12.9 0.4 slice_bitcast_fusion.5
  13.3 0.1 slice_bitcast_fusion.14
  13.4 0.2 slice_bitcast_fusion.8
  13.6 0.8 broadcast_in_dim.21
  14.4 4.7 %concatenate.6.wg = bf16[4,384,640]{2,1,0:T(8,128)(2,1)} concatenate(bf16[4,384,64]{2,1,0:T(8,128)(2,1)S(1)} %get-tuple-element.79, bf16[4,384,64]{2,1,0:T(8,128)(2,1)S(1)} %get-tuple-element.78, bf16[4,384,64]{2,1,0:T(8,128)(2,1)S(1)} %get-tuple-element.77, bf16[4,384,64]{2,1,0:T(8,128)(2,1)} %broadcast_in_dim.21, bf16[4,384,64]{2,1,0:T(8,128)(2,1)S(1)} %get-tuple-element.80, ...), dimensions={2} | concatenate | bytes 3932160 | tf_op jit(solution)/shard_map/concatenate | solution.py:1290
  19.1 1.9 pad.24.wo
  21.1 47.4 %project.1 = (bf16[4,256,768]{2,1,0:T(8,128)(2,1)}, bf16[3,1024,128]{2,1,0:T(8,128)(2,1)}, bf16[4096,384]{1,0:T(8,128)(2,1)}, bf16[768,640]{1,0:T(8,128)(2,1)}, ...) custom-call(bf16[256,768]{1,0:T(8,128)(2,1)} %pad.21.rp, f32[8,384]{1,0:T(8,128)} %fusion.4.gains, ...), custom_call_target="tpu_custom_call" | custom-call | tf_op jit(solution)/shard_map/project/pallas_call | solution.py:296
  68.5 0.0 copy-start.3
  68.5 0.0 copy-start.1
  68.5 19.5 %attend.1 = (bf16[4,384,128]{2,1,0:T(8,128)(2,1)}, f32[3,1024,128]{2,1,0:T(8,128)}, f32[3,1024,128]{2,1,0:T(8,128)}) custom-call(s32[2]{0:T(128)} %pad_add_fusion.meta, bf16[3,1024,128]{2,1,0:T(8,128)(2,1)} %get-tuple-element.27.q3, bf16[4096,384]{1,0:T(8,128)(2,1)} %get-tuple-element.28.kv), custom_call_target="tpu_custom_call" | custom-call | tf_op jit(solution)/shard_map/attend/pallas_call | solution.py:387
  88.1 0.0 copy-done.3
  88.1 0.1 bitcast_select_fusion
  88.2 0.8 pad.25.cp
  89.0 0.0 copy-done.1
  89.0 1.6 pad.26.wd
  90.6 63.3 %mlp.1 = (bf16[256,767]{1,0:T(8,128)(2,1)}, f32[256,768]{1,0:T(8,128)}, bf16[4,192,768]{2,1,0:T(8,128)(2,1)}, bf16[384,768]{1,0:T(8,128)(2,1)}, bf16[4,384,128]{2,1,0:T(8,128)(2,1)}, /*index=5*/f32[8,768]{1,0:T(8,128)}) custom-call(bf16[4,384,128]{2,1,0:T(8,128)(2,1)} %get-tuple-element.29.att, bf16[256,768]{1,0:T(8,128)(2,1)} %pad.21.rp, ...), custom_call_target="tpu_custom_call" | custom-call | tf_op jit(solution)/shard_map/mlp/pallas_call | solution.py:594
  153.9 129.4 %back.1 = (f32[256,767]{1,0:T(8,128)}, bf16[4,2,192,640]{3,2,1,0:T(8,128)(2,1)}, f32[8,768]{1,0:T(8,128)}, bf16[2,2,4,192,768]{4,3,2,1,0:T(8,128)(2,1)}, bf16[2,4,48,768]{3,2,1,0:T(8,128)(2,1)}) custom-call(s32[1]{0:T(128)} %copy.25.lens, bf16[3,1024,128]{2,1,0:T(8,128)(2,1)} %get-tuple-element.27.q3, bf16[4096,384]{1,0:T(8,128)(2,1)} %get-tuple-element.28.kv, ...), custom_call_target="tpu_custom_call" | custom-call | tf_op jit(solution)/shard_map/back/pallas_call | solution.py:1216
  283.4 3.0 copy.22
  286.4 1.4 dynamic-slice_reduce_fusion
  287.8 7.6 %copy.21 = f32[4,2,192,640]{2,1,3,0:T(2,128)} copy(bf16[4,2,192,640]{3,2,1,0:T(8,128)(2,1)} %get-tuple-element.43) | data formatting | bytes 5898240 | tf_op jit(solution)/shard_map/transpose | solution.py:1299
  295.5 7.1 %reshape.46 = f32[4,384,10,64]{1,3,2,0:T(8,128)} reshape(f32[4,2,192,640]{2,1,3,0:T(2,128)} %copy.21) | data formatting | bytes 7864320 | tf_op jit(solution)/shard_map/transpose | solution.py:1299
  302.6 0.0 copy-start
  302.6 1.2 slice.105
  303.8 1.3 slice.104
  305.1 0.1 maximum_bitcast_fusion
  305.2 0.0 copy-done
  305.2 0.2 slice_bitcast_fusion.4
  305.3 0.2 pad_maximum_fusion
  305.6 2.9 copy.23
  308.5 2.2 slice_convert_fusion
  310.7 1.8 slice_bitcast_fusion.2
  312.5 2.8 maximum_convert_fusion
  315.3 0.0 copy-start.2
  315.3 4.3 %fusion = f32[1536,767]{1,0:T(8,128)} fusion(bf16[2,1536,768]{2,1,0:T(8,128)(2,1)} %bitcast.62), kind=kLoop, calls=%fused_computation.2 | loop fusion | flops 1178112 | bytes 7068672 | tf_op jit(solution)/shard_map/convert_element_type | solution.py:1334
  319.6 0.0 copy-done.2
  319.6 0.7 copy.26
  (1 shorter events, 0.0 us)
Async XLA Ops:
  68.5 19.6 %copy-start.3 = (bf16[1,256,767]{2,1,0:T(8,128)(2,1)S(1)}, bf16[1,256,767]{2,1,0:T(8,128)(2,1)}, u32[]{:S(2)}) copy-start(bf16[1,256,767]{2,1,0:T(8,128)(2,1)} %param.17) | copy-start | bytes 1178116
  68.5 20.5 %copy-start.1 = (bf16[1536,767]{1,0:T(8,128)(2,1)S(1)}, bf16[1536,767]{1,0:T(8,128)(2,1)}, u32[]{:S(2)}) copy-start(bf16[1536,767]{1,0:T(8,128)(2,1)} %param.16) | copy-start | bytes 7068676
  302.6 2.6 copy-start
  315.3 4.3 %copy-start.2 = (bf16[256,767]{1,0:T(8,128)(2,1)S(1)}, bf16[256,767]{1,0:T(8,128)(2,1)}, u32[]{:S(2)}) copy-start(bf16[256,767]{1,0:T(8,128)(2,1)} %get-tuple-element.32) | copy-start | bytes 1178116

commit v3 on v2

--- a/solution.py
+++ b/solution.py
@@ -124,56 +124,164 @@
     return jnp.where(low, zero, t), jnp.where(low, zero, pltpu.roll(t, HD, 1))
 
 
-def project_kernel(n, rp, gains, wg, wo, h1, q3, kv, wa, woa, gfull, ss, rs, ls, hs, hr, ks, kr, fs):
+def causal(shape, sub, size, first_query):
+    col = lax.broadcasted_iota(jnp.int32, shape, 1) + sub * size
+    row = lax.broadcasted_iota(jnp.int32, shape, 0) + first_query
+    return col <= row
+
+
+def gelu_both(a):
+    c = 0.7978845608028654
+    a2 = a * a
+    t = jnp.tanh(c * a * (1.0 + 0.044715 * a2))
+    half = 0.5 * (1.0 + t)
+    slope = half + 0.5 * a * (1.0 - t * t) * (c * (1.0 + 0.134145 * a2))
+    return a * half, slope
+
+
+def group_columns(wq, wg):
+    width = wq.shape[1] // 3
+    low = low_half((wq.shape[0], 128))
+    zero = jnp.zeros((wq.shape[0], 128), wq.dtype)
+
+    def swap(t):
+        return pltpu.roll(t, HD, 1)
+
+    for j in range(GROUPS // 2):
+        a, b = 2 * j, 2 * j + 1
+        for i in range(3):
+            at = i * width + j * 384
+            t0, t1, t2 = (wq[:, at + 128 * t : at + 128 * t + 128] for t in range(3))
+            pair = (t0, swap(jnp.where(low, t2, t1)))
+            if i < 2:
+                third = (jnp.where(low, t1, zero), jnp.where(low, swap(t2), zero))
+                for g, p, t in zip((a, b), pair, third):
+                    wg[g, :, i * 256 : i * 256 + 128] = p
+                    wg[g, :, i * 256 + 128 : i * 256 + 256] = t
+            else:
+                third = (jnp.where(low, zero, swap(t1)), jnp.where(low, zero, t2))
+                for g, p, t in zip((a, b), pair, third):
+                    wg[g, :, 512:640] = p
+                    wg[g, :, 384:512] = wg[g, :, 384:512] + t
+
+
+def front_kernel(
+    n, lens, ri, ci, g1, g2, wq, wo, wuh, wdh,
+    out, gmid, ysum, go, dog, dg2, rp, wg, h1, q3, kv, o3, l3, gfull,
+    gains, wop, wa, woa, wu, wdr, wd, att, attg, attp, wide, hid, gmb, act, gpre, esum, dsend, gbb, mid, gk,
+    ss, rs, ls, hs, hr, vs, kr, fs, xs, xr, cs, cr, ts, tr, as_, ar, ds_, dr, ks, ks_r,
+):
     p = Place(n)
-    rows, width = rp.shape
+    rows, narrow = ri.shape
+    width = narrow + 1
     half = width // 2
+    ff = wuh.shape[1]
+    pk = rows * 3 // 2
+    keys = p.m * rows
+    size = min(SUB, keys)
+    subs = keys // size
+    other = 1 - p.x
+    others = [(p.chip + d) % p.chips for d in range(1, p.chips)]
+    line = [(p.a + d) % GROUPS for d in range(1, GROUPS)]
     ready = greet(p, xpeer=True, sibling=True, chips=True, line=True)
-    own = pltpu.make_async_copy(
-        wg.at[p.a], wa.at[pl.ds(pl.multiple_of(p.x * half, half), half)], ls.at[0]
-    )
-    own.start()
+    own_u = pltpu.make_async_copy(wuh, wu.at[p.x], ls.at[5])
+    own_d = pltpu.make_async_copy(wdh, wdr.at[p.x], ls.at[6])
+    own_u.start()
+    own_d.start()
+
+    rp[:, :narrow] = ri[...]
+    rp[:, narrow:] = jnp.zeros((rows, 1), BF16)
+    group_columns(wq, wg)
+    gains[0:1, :] = g1[...].astype(F32).reshape(1, half)
+    gains[1:2, :] = g2[...].astype(F32).reshape(1, half)
+    gfull[p.x] = gains[...]
+    ready()
+
+    def xc(i, src, dst):
+        return rcopy(src, dst, ss.at[i], rs.at[i], p.xpeer())
+
+    at_x = pl.ds(pl.multiple_of(p.x * half, half), half)
+    x_gain = xc(0, gains, gfull.at[p.x])
+    x_gain.start()
+    x_wa = xc(1, wg.at[p.a], wa.at[at_x])
+    x_wa.start()
+
+    def cut(i, chip, core):
+        size_i = (width, ff)[i] // p.m
+        return pl.ds(pl.multiple_of((chip * 2 + core) * size_i, size_i), size_i)
+
+    def weight_x(i):
+        at = cut(i, p.chip, p.k)
+        return rcopy((wuh, wdh)[i].at[at], (wu, wdr)[i].at[p.x, at], xs.at[i], xr.at[i], p.xpeer())
+
+    def weight_chip(i, owner, to):
+        r = (wu, wdr)[i].at[other, cut(i, owner, p.k)]
+        return rcopy(r, r, cs.at[i, to], cr.at[i, owner], p.on_chip(to))
+
+    def weight_core(i, owner, core):
+        r = (wu, wdr)[i].at[other, cut(i, owner, core)]
+        return rcopy(r, r, ts.at[i, owner], tr.at[i, owner], p.sibling())
+
+    def weight_spread(i):
+        weight_x(i).wait_recv()
+        for c in others:
+            weight_chip(i, p.chip, c).start()
+        weight_core(i, p.chip, p.k).start()
+
+    def weight_pass(i):
+        for c in others:
+            weight_chip(i, c, c).wait_recv()
+            weight_core(i, c, p.k).start()
+
+    def weight_end(i):
+        for c in range(p.chips):
+            weight_core(i, c, 1 - p.k).wait_recv()
+
+    weight_x(0).start()
+    weight_x(1).start()
+
+    wop[:, :narrow] = wo[...]
+    wop[:, narrow:] = jnp.zeros((half, 1), BF16)
+    xo = []
+    local = []
+    for i in range(2):
+        g = p.x * 2 + i
+        for j, (src, count, dst) in enumerate(((0, 128, 0), (128, 64, 192))):
+            s_ = wop.at[pl.ds(i * 192 + src, count)]
+            d_ = woa.at[pl.ds(pl.multiple_of(g * 256 + dst, 64), count)]
+            xo.append(xc(2 + 2 * i + j, s_, d_))
+            local.append(pltpu.make_async_copy(s_, d_, ls.at[1 + 2 * i + j]))
     zero_rows = jnp.zeros((HD, width), BF16)
     for g in range(GROUPS):
         woa[pl.ds(g * 256 + 128, HD), :] = zero_rows
-    local = []
-    for i in range(2):
-        g = p.x * 2 + i
-        for j, (src, size, dst) in enumerate(((0, 128, 0), (128, 64, 192))):
-            c = pltpu.make_async_copy(
-                wo.at[pl.ds(i * 192 + src, size)],
-                woa.at[pl.ds(pl.multiple_of(g * 256 + dst, 64), size)],
-                ls.at[1 + 2 * i + j],
-            )
-            c.start()
-            local.append(c)
-    gfull[p.x] = gains[...]
+    for c in xo:
+        c.start()
+    for c in local:
+        c.start()
+    slot = (p.a * p.m + p.b) * rows + lax.broadcasted_iota(jnp.int32, (rows, width), 0)
+    live = slot < lens[0]
+    gmb[0, :, :narrow] = ci[...]
+    gmb[0, :, narrow:] = jnp.zeros((rows, 1), BF16)
+    gmb[0] = jnp.where(live, gmb[0].astype(F32), 0.0).astype(BF16)
+    x_gm = xc(6, gmb.at[0], gmb.at[1])
+    x_gm.start()
+    own_a = pltpu.make_async_copy(wg.at[p.a], wa.at[at_x], ls.at[0])
+    own_a.start()
     u = ext_of(rp[...].astype(F32))
     normed = u * inv_rms(u)
-    ready()
-    xg = rcopy(gains, gfull.at[p.x], ss.at[0], rs.at[0], p.xpeer())
-    xg.start()
-    xw = rcopy(
-        wg.at[p.a],
-        wa.at[pl.ds(pl.multiple_of(p.x * half, half), half)],
-        ss.at[1],
-        rs.at[1],
-        p.xpeer(),
-    )
-    xw.start()
-    xg.wait()
+    x_gain.wait()
     gain = jnp.concatenate([gfull[0, 0:1, :], gfull[1, 0:1, :]], axis=1)
     h1[p.a] = (normed * gain).astype(BF16)
 
     def line_copy(block, dst, sem):
         return rcopy(h1.at[block], h1.at[block], hs.at[sem], hr.at[block], p.on_line(dst))
 
-    def kv_rows(block, b):
-        return kv.at[pl.ds(pl.multiple_of((block * p.m + b) * rows, rows), rows)]
-
     def kv_copy(block, b, dev, send):
-        r = kv_rows(block, b)
+        r = kv.at[pl.ds(pl.multiple_of((block * p.m + b) * rows, rows), rows)]
         return rcopy(r, r, send, kr.at[block, b], dev)
+
+    def ac(i, to):
+        return rcopy(att.at[to], attg.at[i], as_.at[to], ar.at[i], p.on_line(to))
 
     @pl.when(p.a < GROUPS - 1)
     def _():
@@ -183,21 +291,8 @@
     def _():
         line_copy(p.a, p.a - 1, 1).start()
 
-    xo = []
-    for i in range(2):
-        g = p.x * 2 + i
-        for j, (src, size, dst) in enumerate(((0, 128, 0), (128, 64, 192))):
-            c = rcopy(
-                wo.at[pl.ds(i * 192 + src, size)],
-                woa.at[pl.ds(pl.multiple_of(g * 256 + dst, 64), size)],
-                ss.at[2 + 2 * i + j],
-                rs.at[2 + 2 * i + j],
-                p.xpeer(),
-            )
-            c.start()
-            xo.append(c)
-    own.wait()
-    xw.wait()
+    own_a.wait()
+    x_wa.wait()
 
     def produce(block):
         y = dot(h1[block], wa[...]).astype(BF16)
@@ -209,8 +304,8 @@
         q3[2, at, :] = y[:, 128:256]
         kv[pl.ds(pl.multiple_of((block * p.m + p.b) * rows, rows), rows), :] = y[:, 256:]
         for d in range(1, p.chips):
-            kv_copy(block, p.b, p.on_chip((p.chip + d) % p.chips), ks.at[block, d]).start()
-        kv_copy(block, p.b, p.sibling(), ks.at[block, 0]).start()
+            kv_copy(block, p.b, p.on_chip((p.chip + d) % p.chips), vs.at[block, d]).start()
+        kv_copy(block, p.b, p.sibling(), vs.at[block, 0]).start()
 
     def pass_on(block):
         for d in range(1, p.chips):
@@ -218,239 +313,167 @@
             kv_copy(block, b, p.sibling(), fs.at[block, d]).wait_recv()
             kv_copy(block, b, p.sibling(), fs.at[block, d]).start()
 
-    produce(p.a)
-    for s in range(1, GROUPS):
-
-        @pl.when(p.a - s >= 0)
-        def _():
-            line_copy(p.a - s, p.a, 0).wait_recv()
+    def complete(block):
+        for c in range(p.chips):
+            kv_copy(block, c * 2 + 1 - p.k, p.sibling(), vs.at[block, 0]).wait_recv()
+
+    first_query = p.b * rows
+    dead = jnp.where(lens[0] > keys, 0.0, 1.0).astype(F32)
+
+    def pair(z, c, diagonal):
+        at_q = pl.ds(pl.multiple_of(z * rows, rows), rows)
+        gone = jnp.where(c > 0, dead, 0.0)
+        for h in range(GH):
+            kt = 128 * (h // 2)
+            vt = 128 if h == 2 else 256
+            q = q3[h, at_q, :]
+
+            def keys_of(sub, first):
+                at = pl.ds(pl.multiple_of(c * keys + sub * size, size), size)
+                scores = dg(q, kv[at, kt : kt + 128], NT) * (SCALE * LOG2E)
+                if diagonal:
+                    scores = jnp.where(causal(scores.shape, sub, size, first_query), scores, MASKED)
+                here = jnp.max(scores, axis=1, keepdims=True) + gone * MASKED
+                if first:
+                    newest = here
+                else:
+                    top = l3[h, at_q, 0:1]
+                    newest = jnp.maximum(top, here)
+                weights = jnp.exp2(scores - (newest - gone * (3.0 * MASKED)))
+                sums = jnp.sum(weights, axis=1, keepdims=True)
+                part = dot(weights.astype(BF16), kv[at, vt : vt + 128])
+                if not first:
+                    shrink = jnp.exp2(top - newest)
+                    sums = sums + l3[h, at_q, HD : HD + 1] * shrink
+                    part = part + o3[h, at_q, :] * shrink
+                o3[h, at_q, :] = part
+                l3[h, at_q, :] = jnp.where(low_half((rows, 128)), newest, sums)
+
+            keys_of(0, diagonal)
+            if subs > 1:
+
+                def rest(sub, carry):
+                    keys_of(sub, False)
+                    return carry
+
+                lax.fori_loop(1, subs, rest, 0)
+
+    def finish_row(z):
+        at_q = pl.ds(pl.multiple_of(z * rows, rows), rows)
+        heads = []
+        for h in range(GH):
+            total = l3[h, at_q, HD : HD + 1]
+            o = o3[h, at_q, :] / total
+            o3[h, at_q, :] = o
+            l3[h, at_q, :] = jnp.broadcast_to(l3[h, at_q, 0:1] + jnp.log2(total), (rows, 128))
+            heads.append(o)
+        att[z, 0:rows, :] = jnp.where(low_half((rows, 128)), heads[0], heads[1]).astype(BF16)
+        att[z, rows:pk, :] = pack_tail(heads[2]).astype(BF16)
+
+        @pl.when(z == p.a)
+        def _():
+            attg[z] = att[z]
+
+        @pl.when(z != p.a)
+        def _():
+            ac(p.a, z).start()
+
+    def far(z):
+        return jnp.abs(z - p.a)
+
+    def pairs(t):
+        def row(z, carry):
+            @pl.when(far(z) == t)
+            def _():
+                pair(z, z, True)
+
+            def key(d, carry):
+                @pl.when(jnp.maximum(far(z), far(z - d)) == t)
+                def _():
+                    pair(z, z - d, False)
+
+                return carry
+
+            lax.fori_loop(1, z + 1, key, 0)
+
+            @pl.when(jnp.maximum(far(z), p.a) == t)
+            def _():
+                finish_row(z)
+
+            return carry
+
+        lax.fori_loop(0, GROUPS, row, 0)
+
+    def step(s, carry):
+        below = p.a - s
+        above = p.a + s
+
+        @pl.when((s > 0) & (below >= 0))
+        def _():
+            line_copy(below, p.a, 0).wait_recv()
 
             @pl.when(p.a < GROUPS - 1)
             def _():
-                line_copy(p.a - s, p.a + 1, 2 * s).start()
-
-        @pl.when(p.a + s < GROUPS)
-        def _():
-            line_copy(p.a + s, p.a, 0).wait_recv()
+                line_copy(below, p.a + 1, 2 * s).start()
+
+        @pl.when((s > 0) & (above < GROUPS))
+        def _():
+            line_copy(above, p.a, 0).wait_recv()
 
             @pl.when(p.a > 0)
             def _():
-                line_copy(p.a + s, p.a - 1, 2 * s + 1).start()
-
-        @pl.when(p.a - s >= 0)
-        def _():
-            produce(p.a - s)
-
-        @pl.when(p.a + s < GROUPS)
-        def _():
-            produce(p.a + s)
-
-        @pl.when(p.a - s + 1 >= 0)
-        def _():
-            pass_on(p.a - s + 1)
-
-        if s > 1:
-
-            @pl.when(p.a + s - 1 < GROUPS)
-            def _():
-                pass_on(p.a + s - 1)
-
-    @pl.when(p.a - GROUPS + 1 >= 0)
-    def _():
-        pass_on(p.a - GROUPS + 1)
-
-    @pl.when(p.a + GROUPS - 1 < GROUPS)
-    def _():
-        pass_on(p.a + GROUPS - 1)
-
-    for block in range(GROUPS):
-        kv_copy(block, p.b, p.sibling(), ks.at[block, 0]).wait_send()
-        sib = p.chip * 2 + 1 - p.k
-        kv_copy(block, sib, p.sibling(), ks.at[block, 0]).wait_recv()
-        for d in range(1, p.chips):
-            kv_copy(block, p.b, p.sibling(), ks.at[block, d]).wait_send()
-            b = ((p.chip + d) % p.chips) * 2
-            kv_copy(block, b + p.k, p.sibling(), fs.at[block, d]).wait_send()
-            kv_copy(block, b + 1 - p.k, p.sibling(), fs.at[block, d]).wait_recv()
-    for s in range(GROUPS):
-
-        @pl.when((p.a - s >= 0) & (p.a < GROUPS - 1))
-        def _():
-            line_copy(p.a - s, p.a + 1, 2 * s).wait_send()
-
-        @pl.when((p.a + s < GROUPS) & (p.a > 0))
-        def _():
-            line_copy(p.a + s, p.a - 1, 2 * s + 1).wait_send()
-
+                line_copy(above, p.a - 1, 2 * s + 1).start()
+
+        @pl.when(s == GROUPS - 1)
+        def _():
+            weight_spread(0)
+
+        @pl.when(s == GROUPS)
+        def _():
+            weight_spread(1)
+
+        @pl.when(below >= 0)
+        def _():
+            produce(below)
+
+        @pl.when((s > 0) & (above < GROUPS))
+        def _():
+            produce(above)
+
+        @pl.when((s > 0) & (below + 1 >= 0))
+        def _():
+            pass_on(below + 1)
+            complete(below + 1)
+
+        @pl.when((s > 1) & (above - 1 < GROUPS))
+        def _():
+            pass_on(above - 1)
+            complete(above - 1)
+
+        @pl.when(s > 0)
+        def _():
+            pairs(s - 1)
+
+        return carry
+
+    lax.fori_loop(0, GROUPS + 1, step, 0)
+    weight_pass(0)
+
+    own_u.wait()
+    own_d.wait()
+
+    def pad_down(f):
+        wd[f, :, :narrow] = wdr[f]
+        wd[f, :, narrow:] = jnp.zeros((ff, 1), BF16)
+
+    pad_down(p.x)
     for c in xo:
         c.wait()
     for c in local:
         c.wait()
-
-
-def project(n, rp, gains, wg, wo):
-    rows, width = rp.shape
-    m = n // GROUPS
-    lanes = wg.shape[2]
-    sds = jax.ShapeDtypeStruct
-    return pl.pallas_call(
-        functools.partial(project_kernel, n),
-        name="project",
-        out_shape=(
-            sds((GROUPS, rows, width), BF16),
-            sds((GH, GROUPS * rows, 128), BF16),
-            sds((n * rows, 384), BF16),
-            sds((width, lanes), BF16),
-            sds((GROUPS * 256, width), BF16),
-            sds((2,) + gains.shape, F32),
-        ),
-        in_specs=[VM, VM, ANY, VM],
-        out_specs=[VM] * 6,
-        scratch_shapes=[
-            DMA((6,)),
-            DMA((6,)),
-            DMA((5,)),
-            DMA((2 * GROUPS,)),
-            DMA((GROUPS,)),
-            DMA((GROUPS, m // 2)),
-            DMA((GROUPS, m)),
-            DMA((GROUPS, m // 2)),
-        ],
-        compiler_params=pltpu.CompilerParams(
-            collective_id=0, has_side_effects=True, vmem_limit_bytes=VLIM
-        ),
-    )(rp, gains, wg, wo)
-
-
-def key_steps(z, keys):
-    subs = keys // min(SUB, keys)
-    return [(z, s) for s in range(subs)] + [(c, s) for c in range(z) for s in range(subs)]
-
-
-def causal(shape, sub, size, first_query):
-    col = lax.broadcasted_iota(jnp.int32, shape, 1) + sub * size
-    row = lax.broadcasted_iota(jnp.int32, shape, 0) + first_query
-    return col <= row
-
-
-def attend_kernel(meta, q3, kv, att, o3, l3):
-    rows = q3.shape[1] // GROUPS
-    keys = kv.shape[0] // GROUPS
-    size = min(SUB, keys)
-    first_query = meta[0] * rows
-    dead = jnp.where(meta[1] > keys, 0.0, MASKED).astype(F32)
-
-    def head(h, carry):
-        kt = pl.multiple_of(128 * (h // 2), 128)
-        vt = pl.multiple_of(128 * (2 - h // 2 - (h + 1) % 2 * 0), 128)
-        vt = pl.multiple_of(jnp.where(h == 2, 128, 256), 128)
-        for z in range(GROUPS):
-            q = q3[h, pl.ds(z * rows, rows), :]
-            top = total = acc = None
-            for c, s in key_steps(z, keys):
-                at = pl.ds(c * keys + s * size, size)
-                scores = dg(q, kv[at, pl.ds(kt, 128)], NT) * (SCALE * LOG2E)
-                if c == z:
-                    scores = jnp.where(
-                        causal(scores.shape, s, size, first_query), scores, MASKED
-                    )
-                bias = dead if c > 0 else 0.0
-                if c == z and c > 0:
-                    bias = dead
-                here = jnp.max(scores, axis=1, keepdims=True) + bias
-                newest = here if top is None else jnp.maximum(top, here)
-                weights = jnp.exp2(scores - (newest - bias))
-                sums = jnp.sum(weights, axis=1, keepdims=True)
-                part = dot(weights.astype(BF16), kv[at, pl.ds(vt, 128)])
-                if top is None:
-                    total, acc = sums, part
-                else:
-                    shrink = jnp.exp2(top - newest)
-                    total = total * shrink + sums
-                    acc = acc * shrink + part
-                top = newest
-            o3[h, pl.ds(z * rows, rows), :] = acc / total
-            l3[h, pl.ds(z * rows, rows), :] = jnp.broadcast_to(top + jnp.log2(total), (rows, 128))
-        return carry
-
-    lax.fori_loop(0, GH, head, 0)
-    for z in range(GROUPS):
-        at = pl.ds(z * rows, rows)
-        both = jnp.where(low_half((rows, 128)), o3[0, at, :], o3[1, at, :])
-        att[z, 0:rows, :] = both.astype(BF16)
-        att[z, rows : rows + rows // 2, :] = pack_tail(o3[2, at, :]).astype(BF16)
-
-
-def attend(meta, q3, kv):
-    sds = jax.ShapeDtypeStruct
-    rows = q3.shape[1] // GROUPS
-    return pl.pallas_call(
-        attend_kernel,
-        name="attend",
-        out_shape=(
-            sds((GROUPS, rows * 3 // 2, 128), BF16),
-            sds(q3.shape, F32),
-            sds(q3.shape, F32),
-        ),
-        in_specs=[SM, VM, VM],
-        out_specs=[VM] * 3,
-        compiler_params=pltpu.CompilerParams(vmem_limit_bytes=VLIM),
-    )(meta, q3, kv)
-
-
-def gelu_both(a):
-    c = 0.7978845608028654
-    a2 = a * a
-    t = jnp.tanh(c * a * (1.0 + 0.044715 * a2))
-    half = 0.5 * (1.0 + t)
-    slope = half + 0.5 * a * (1.0 - t * t) * (c * (1.0 + 0.134145 * a2))
-    return a * half, slope
-
-
-def mlp_kernel(
-    n, att, rp, cp, gfull, woa, wu, wd,
-    out, gmid, red, go, dog, dg2,
-    attg, attp, wide, hid, gmb, act, gpre, osum, osend, orecv, esend, erecv, dsend, gbb, mid,
-    gm, gk, ys_, yr_,
-    ss, rs, as_, ar, ds_, dr, ks, kr, qs, qr,
-):
-    p = Place(n)
-    rows, width = rp.shape
-    ff = wu.shape[1]
-    pk = rows * 3 // 2
-    piece = red.shape[1]
-    part = GROUPS * piece
-    ready = greet(p, xpeer=True, sibling=True, chips=True, line=True)
-    gmb[0] = cp[...]
-    ready()
-
-    def xc(i, src, dst):
-        return rcopy(src, dst, ss.at[i], rs.at[i], p.xpeer())
-
-    def ac(i, to):
-        return rcopy(att.at[to], attg.at[i], as_.at[to], ar.at[i], p.on_line(to))
-
-    def dc(i, to):
-        return rcopy(dsend.at[to], dog.at[i], ds_.at[to], dr.at[i], p.on_line(to))
-
-    def kc(chip):
-        at = pl.ds(pl.multiple_of(chip * part, part), part)
-        return rcopy(gm.at[1 - p.k, at], gk.at[at], ks.at[chip], kr.at[chip], p.sibling())
-
-    def yc(chip, slot, z):
-        return rcopy(ys_.at[chip, z], yr_.at[slot, z], qs.at[chip, z], qr.at[slot, z], p.on_chip(chip))
-
-    for d in range(1, GROUPS):
-        to = (p.a + d) % GROUPS
-        ac(p.a, to).start()
-    attg[p.a] = att[p.a]
-    x_gm = xc(0, cp, gmb.at[1])
-    x_gm.start()
-    for d in range(1, GROUPS):
-        fr = (p.a + d) % GROUPS
-        ac(fr, fr).wait_recv()
-    other = 1 - p.x
-    x_att = [xc(1 + i, attg.at[other * 2 + i], attp.at[i]) for i in range(2)]
+    for g in line:
+        ac(g, g).wait_recv()
+    x_att = [xc(7 + i, attg.at[other * 2 + i], attp.at[i]) for i in range(2)]
     for g in range(GROUPS):
         wide[:, g * 256 : g * 256 + 128] = attg[g, 0:rows, :]
         top, bottom = unpack_tail(attg[g, rows:pk, :])
@@ -460,84 +483,47 @@
     u = ext_of(mid[...])
     gain = jnp.concatenate([gfull[0, 1:2, :], gfull[1, 1:2, :]], axis=1)
     hid[0] = (u * inv_rms(u) * gain).astype(BF16)
-    x_hid = xc(3, hid.at[0], hid.at[1])
+    x_hid = xc(9, hid.at[0], hid.at[1])
     x_hid.start()
     for c in x_att:
         c.start()
     tiles = ff // 256
 
-    def up(i):
+    def up(slot, token, f):
         def tile(t, carry):
             at = pl.ds(pl.multiple_of(t * 256, 256), 256)
-            a, slope = gelu_both(dot(hid[i], wu[:, at]))
-            act[i, :, at] = a.astype(BF16)
-            gpre[i, :, at] = (slope * dg(gmb[i], wd[at, :], NT)).astype(BF16)
+            a, slope = gelu_both(dot(hid[token], wu[f, :, at]))
+            act[slot, :, at] = a.astype(BF16)
+            gpre[slot, :, at] = (slope * dg(gmb[token], wd[f, at, :], NT)).astype(BF16)
             return carry
 
         lax.fori_loop(0, tiles, tile, 0)
 
-    up(0)
-    x_gm.wait()
-    x_hid.wait()
-    up(1)
-    esend[...] = dg(gpre[1], wu[...], NT).astype(BF16)
-    x_e = xc(4, esend, erecv)
-    x_e.start()
-
-    def grad_up(t, carry):
+    weight_pass(1)
+    up(0, 0, p.x)
+    weight_end(0)
+    weight_end(1)
+    pad_down(other)
+    up(2, 0, other)
+
+    def e_tile(t, carry):
         at = pl.ds(pl.multiple_of(t * 256, 256), 256)
-        g = dg(hid[0], gpre[0, :, at], TN) + dg(hid[1], gpre[1, :, at], TN)
-        per = width // 256
-        r0 = pl.multiple_of((t // per) * width, width)
-        c0 = pl.multiple_of((t % per) * 256, 256)
-        gm[0, pl.ds(r0, width), pl.ds(c0, 256)] = g.astype(BF16)
+        e = dg(gpre[0], wu[p.x, at, :], NT) + dg(gpre[2], wu[other, at, :], NT)
+        esum[t] = e
         return carry
 
-    def grad_down(t, carry):
-        at = pl.ds(pl.multiple_of(t * 256, 256), 256)
-        g = dg(act[0, :, at], gmb[0], TN) + dg(act[1, :, at], gmb[1], TN)
-        gm[1, at, :] = g.astype(BF16)
-        return carry
-
-    @pl.when(p.k == 0)
-    def _():
-        lax.fori_loop(0, tiles, grad_down, 0)
-
-    @pl.when(p.k == 1)
-    def _():
-        lax.fori_loop(0, tiles, grad_up, 0)
-
-    for d in range(1, p.chips):
-        kc((p.chip + d) % p.chips).start()
-    kc(p.chip).start()
-
-    @pl.when(p.k == 0)
-    def _():
-        lax.fori_loop(0, tiles, grad_up, 0)
-
-    @pl.when(p.k == 1)
-    def _():
-        lax.fori_loop(0, tiles, grad_down, 0)
-
-    for d in range(1, p.chips):
-        chip = (p.chip + d) % p.chips
-        kc(chip).wait()
-        for z in range(GROUPS):
-            at = pl.ds(pl.multiple_of(chip * part + z * piece, 16), piece)
-            ys_[chip, z] = (gm[p.k, at, :].astype(F32) + gk[at, :].astype(F32)).astype(BF16)
-            yc(chip, p.chip, z).start()
-    osend[...] = dot(act[1], wd[...]).astype(BF16)
-    e_own = dg(gpre[0], wu[...], NT)
-    x_e.wait()
-    x_o = xc(5, osend, orecv)
-    x_o.start()
-    e = e_own + erecv[...].astype(F32)
+    lax.fori_loop(0, width // 256, e_tile, 0)
+    e = jnp.concatenate([esum[t] for t in range(width // 256)], axis=1)
     u = ext_of(mid[...])
     inv = inv_rms(u)
-    gmid[...] = cp[...].astype(F32) + crms_back(u, inv, gain, e)
+    gmid[...] = gmb[0].astype(F32) + crms_back(u, inv, gain, e)
     gbb[0] = gmid[...].astype(BF16)
-    x_gb = xc(6, gbb.at[0], gbb.at[1])
+    x_gb = xc(10, gbb.at[0], gbb.at[1])
     x_gb.start()
+
+    def dc(i, to):
+        return rcopy(dsend.at[to], dog.at[i], ds_.at[to], dr.at[i], p.on_line(to))
+
     for d in range(1, GROUPS + 1):
         to = (p.a + d) % GROUPS
         w = woa[pl.ds(pl.multiple_of(to * 256, 256), 256), :]
@@ -549,13 +535,63 @@
         else:
             dog[to, 0:rows, :] = da[:, 0:128]
             dog[to, rows:pk, :] = pack_tail(da[:, 128:256])
+    x_gm.wait()
+    x_hid.wait()
+    up(1, 1, p.x)
+    final = mid[...] + dot(act[0], wd[p.x]) + dot(act[2], wd[other])
+    out[...] = final.astype(BF16)
+
+    gm = wd
+    piece = ysum.shape[2]
+    part = GROUPS * piece
+
+    def kc(chip):
+        at = pl.ds(pl.multiple_of(chip * part, part), part)
+        return rcopy(gm.at[1 - p.k, at], gk.at[at], ks.at[chip], ks_r.at[chip], p.sibling())
+
+    def grad_up(t, carry):
+        at = pl.ds(pl.multiple_of(t * 256, 256), 256)
+        g = dg(hid[0], gpre[0, :, at], TN) + dg(hid[1], gpre[1, :, at], TN)
+        per = width // 256
+        r0 = pl.multiple_of((t // per) * width, width)
+        c0 = pl.multiple_of((t % per) * 256, 256)
+        gm[0, pl.ds(r0, width), pl.ds(c0, 256)] = g.astype(BF16)
+        return carry
+
+    def grad_down(t, carry):
+        at = pl.ds(pl.multiple_of(t * 256, 256), 256)
+        g = dg(act[0, :, at], gmb[0], TN) + dg(act[1, :, at], gmb[1], TN)
+        gm[1, at, :] = g.astype(BF16)
+        return carry
+
+    @pl.when(p.k == 0)
+    def _():
+        lax.fori_loop(0, tiles, grad_down, 0)
+
+    @pl.when(p.k == 1)
+    def _():
+        lax.fori_loop(0, tiles, grad_up, 0)
+
+    for c in others:
+        kc(c).start()
+    kc(p.chip).start()
+
+    @pl.when(p.k == 0)
+    def _():
+        lax.fori_loop(0, tiles, grad_up, 0)
+
+    @pl.when(p.k == 1)
+    def _():
+        lax.fori_loop(0, tiles, grad_down, 0)
+
+    for chip in others + [p.chip]:
+        kc(chip).wait()
+        for z in range(GROUPS):
+            at = pl.ds(pl.multiple_of(chip * part + z * piece, 16), piece)
+            ysum[chip, z] = (gm[p.k, at, :].astype(F32) + gk[at, :].astype(F32)).astype(BF16)
     dg2[...] = jnp.broadcast_to(jnp.sum(e * (u * inv), axis=0, keepdims=True), dg2.shape)
-    osum[...] = mid[...] + dot(act[0], wd[...])
     for c in x_att:
         c.wait()
-    x_o.wait()
-    final = osum[...] + orecv[...].astype(F32)
-    out[...] = final[:, : width - 1].astype(BF16)
     x_gb.wait()
     for i in range(2):
         own_tail = jnp.concatenate(unpack_tail(attg[p.x * 2 + i, rows:pk, :]), axis=0)
@@ -564,90 +600,118 @@
         go[i * 192 : i * 192 + 128, :] = g.astype(BF16)
         g = dg(own_tail, gbb[0], TN) + dg(peer_tail, gbb[1], TN)
         go[i * 192 + 128 : i * 192 + 192, :] = g[HD:, :].astype(BF16)
-    kc(p.chip).wait()
-    for z in range(GROUPS):
-        at = pl.ds(pl.multiple_of(p.chip * part + z * piece, 16), piece)
-        total = gm[p.k, at, :].astype(F32) + gk[at, :].astype(F32)
+
+    for g in line:
+        ac(p.a, g).wait_send()
+        dc(p.a, g).wait_send()
+        dc(g, g).wait_recv()
+    for block in range(GROUPS):
+        kv_copy(block, p.b, p.sibling(), vs.at[block, 0]).wait_send()
         for d in range(1, p.chips):
-            chip = (p.chip + d) % p.chips
-            yc(chip, chip, z).wait_recv()
-            total = total + yr_[chip, z].astype(F32)
-        red[z] = total.astype(BF16)
-    for d in range(1, GROUPS):
-        to = (p.a + d) % GROUPS
-        ac(p.a, to).wait_send()
-        dc(p.a, to).wait_send()
-        dc(to, to).wait_recv()
-    for d in range(1, p.chips):
-        for z in range(GROUPS):
-            yc((p.chip + d) % p.chips, p.chip, z).wait_send()
-
-
-def mlp(n, att, rp, cp, gfull, woa, wu, wd):
-    rows, width = rp.shape
+            kv_copy(block, p.b, p.sibling(), vs.at[block, d]).wait_send()
+            b = ((p.chip + d) % p.chips) * 2
+            kv_copy(block, b + p.k, p.sibling(), fs.at[block, d]).wait_send()
+    for s in range(GROUPS):
+
+        @pl.when((p.a - s >= 0) & (p.a < GROUPS - 1))
+        def _():
+            line_copy(p.a - s, p.a + 1, 2 * s).wait_send()
+
+        @pl.when((p.a + s < GROUPS) & (p.a > 0))
+        def _():
+            line_copy(p.a + s, p.a - 1, 2 * s + 1).wait_send()
+
+    for i in range(2):
+        weight_x(i).wait_send()
+        for c in others:
+            weight_chip(i, p.chip, c).wait_send()
+        for c in range(p.chips):
+            weight_core(i, c, p.k).wait_send()
+
+
+def front(n, lens, ri, ci, g1, g2, wq, wo, wu, wd):
+    rows, narrow = ri.shape
+    width = narrow + 1
+    half = width // 2
     ff = wu.shape[1]
     pk = rows * 3 // 2
-    chips = n // GROUPS // 2
+    m = n // GROUPS
+    chips = m // 2
     piece = ff // GROUPS // chips
+    lanes = 640
     sds = jax.ShapeDtypeStruct
     v = pltpu.VMEM
+    heads = (GH, GROUPS * rows, 128)
+    sem = lambda *shape: [DMA(shape), DMA(shape)]
     return pl.pallas_call(
-        functools.partial(mlp_kernel, n),
-        name="mlp",
+        functools.partial(front_kernel, n),
+        name="front",
         out_shape=(
-            sds((rows, width - 1), BF16),
+            sds((rows, width), BF16),
             sds((rows, width), F32),
-            sds((GROUPS, piece, width), BF16),
-            sds((width // 2, width), BF16),
+            sds((chips, GROUPS, piece, width), BF16),
+            sds((half, width), BF16),
             sds((GROUPS, pk, 128), BF16),
             sds((8, width), F32),
+            sds((rows, width), BF16),
+            sds((GROUPS, half, lanes), BF16),
+            sds((GROUPS, rows, width), BF16),
+            sds(heads, BF16),
+            sds((n * rows, 384), BF16),
+            sds(heads, F32),
+            sds(heads, F32),
+            sds((2, 8, half), F32),
         ),
-        in_specs=[VM] * 7,
-        out_specs=[VM] * 6,
+        in_specs=[SM, VM, VM, VM, VM, VM, VM, ANY, ANY],
+        out_specs=[VM] * 14,
         scratch_shapes=[
+            v((8, half), F32),
+            v((half, width), BF16),
+            v((width, lanes), BF16),
+            v((GROUPS * 256, width), BF16),
+            v((2, width, ff), BF16),
+            v((2, ff, narrow), BF16),
+            v((2, ff, width), BF16),
+            v((GROUPS, pk, 128), BF16),
             v((GROUPS, pk, 128), BF16),
             v((2, pk, 128), BF16),
             v((rows, GROUPS * 256), BF16),
             v((2, rows, width), BF16),
             v((2, rows, width), BF16),
-            v((2, rows, ff), BF16),
-            v((2, rows, ff), BF16),
-            v((rows, width), F32),
-            v((rows, width), BF16),
-            v((rows, width), BF16),
-            v((rows, width), BF16),
-            v((rows, width), BF16),
+            v((3, rows, ff), BF16),
+            v((3, rows, ff), BF16),
+            v((width // 256, rows, 256), F32),
             v((GROUPS, pk, 128), BF16),
             v((2, rows, width), BF16),
             v((rows, width), F32),
-            v((2, ff, width), BF16),
             v((ff, width), BF16),
-            v((chips, GROUPS, piece, width), BF16),
-            v((chips, GROUPS, piece, width), BF16),
-            DMA((8,)),
-            DMA((8,)),
+            *sem(11),
+            DMA((7,)),
+            DMA((2 * GROUPS,)),
             DMA((GROUPS,)),
-            DMA((GROUPS,)),
-            DMA((GROUPS,)),
-            DMA((GROUPS,)),
-            DMA((chips,)),
-            DMA((chips,)),
-            DMA((chips, GROUPS)),
-            DMA((chips, GROUPS)),
+            DMA((GROUPS, chips)),
+            DMA((GROUPS, m)),
+            DMA((GROUPS, chips)),
+            *sem(2),
+            *sem(2, chips),
+            *sem(2, chips),
+            *sem(GROUPS),
+            *sem(GROUPS),
+            *sem(chips),
         ],
         compiler_params=pltpu.CompilerParams(
-            collective_id=1, has_side_effects=True, vmem_limit_bytes=VLIM
+            collective_id=0, has_side_effects=True, vmem_limit_bytes=67043328
         ),
-    )(att, rp, cp, gfull, woa, wu, wd)
+    )(lens, ri, ci, g1, g2, wq, wo, wu, wd)
 
 
 def back_kernel(
-    n, lens, q3, kv, o3, l3, dog, wg, h1, rp, gmid, gfull, dg2, red, go,
+    n, lens, q3, kv, o3, l3, dog, wg, h1, rp, gmid, gfull, dg2, ysum, go,
     gin, gq, gains, res, goo,
-    do3, dq3, kvc, dkv, dkvb, rk, ry, wfull, gps, gpr, gqb, qk, qx, qy,
+    red, ymine, yq, do3, dq3, kvc, dkv, dkvb, rk, ry, wfull, gps, gpr, gqb, qk, qx, qy,
     g0, gk, gx, gy, ga, left, right, sumr, suml, ok, os_, oy, oz, ozr,
     xs, xr, ls, vs, ks, kr, ys, yr, zs, zr, ws, wr, qs, qr, ns, nr, bs, br, cs, cr,
-    rs_, rr, ls_, lr, as_, ar, es, er, fs, fr, ts, tr, us, ur, is_, ir,
+    rs_, rr, ls_, lr, as_, ar, es, er, fs, fr, ts, tr, us, ur, is_, ir, ps, pr,
 ):
     p = Place(n)
     rows, width = rp.shape
@@ -675,11 +739,40 @@
         return pltpu.make_async_copy(src, kvc.at[i % slots], vs.at[i % slots])
 
     fetch(0).start()
+    o_in = pltpu.make_async_copy(o3, dq3, ls.at[GROUPS])
+    o_in.start()
+    y_in = pltpu.make_async_copy(ysum.at[p.chip], ymine, ls.at[GROUPS + 1])
+    y_in.start()
     for c in local:
         c.start()
     wx = [
         rcopy(wg.at[g], wfull.at[g, at_x], xs.at[g], xr.at[g], p.xpeer()) for g in range(GROUPS)
     ]
+
+    def over_chips(chip, slot, z):
+        return rcopy(ysum.at[chip, z], yq.at[slot, z], ps.at[chip, z], pr.at[slot, z], p.on_chip(chip))
+
+    def turn(j):
+        outer = jnp.where(p.a == 0, last - j, j)
+        inner = (0, last, 1, last - 1)[j]
+        return jnp.where((p.a == 0) | (p.a == last), outer, jnp.where(p.a == 1, last - inner, inner))
+
+    def chip_sum(j):
+        z = turn(j)
+        total = ymine[z].astype(F32)
+        for c in others:
+            over_chips(c, c, z).wait_recv()
+            total = total + yq[c, z].astype(F32)
+        red[z] = total.astype(BF16)
+        if j < last:
+
+            @pl.when(p.a == 0)
+            def _():
+                rightward(z, red.at[z]).start()
+
+            @pl.when(p.a == last)
+            def _():
+                leftward(z, red.at[z]).start()
 
     def rightward(z, src):
         return rcopy(src, left.at[z], rs_.at[z], rr.at[z], p.on_line(p.a + 1))
@@ -871,22 +964,16 @@
 
     ready()
     out_core().start()
-
-    @pl.when(p.a == 0)
-    def _():
-        for z in range(last, 0, -1):
-            rightward(z, red.at[z]).start()
-
-    @pl.when(p.a == last)
-    def _():
-        for z in range(last):
-            leftward(z, red.at[z]).start()
-
+    for j in range(GROUPS):
+        for c in others:
+            over_chips(c, p.chip, turn(j)).start()
     for c in wx:
         c.start()
 
     first_query = p.b * rows
     low = low_half((rows, 128))
+    o_in.wait()
+    y_in.wait()
     for z in range(GROUPS):
         at = pl.ds(z * rows, rows)
         both = dog[z, 0:rows, :]
@@ -897,7 +984,7 @@
         do3[2, pl.ds(z * rows, rows // 2), :] = top
         do3[2, pl.ds(z * rows + rows // 2, rows // 2), :] = bottom
         for h in range(GH):
-            delta = jnp.sum(o3[h, at, :] * do3[h, at, :].astype(F32), axis=1, keepdims=True)
+            delta = jnp.sum(dq3[h, at, :] * do3[h, at, :].astype(F32), axis=1, keepdims=True)
             gqb[h * rows : (h + 1) * rows, z * 128 : (z + 1) * 128] = jnp.broadcast_to(delta, (rows, 128))
     dq3[...] = jnp.zeros_like(dq3)
     gone = jnp.where(lens[0] > keys, 0.0, -MASKED).astype(F32)
@@ -927,8 +1014,8 @@
                     pl.ds(pl.multiple_of(h * rows, rows), rows),
                     pl.ds(pl.multiple_of(z * 128, 128), 128),
                 ][:, 0:1]
-                for sub in range(subs):
-                    at = pl.ds(sub * size, size)
+                def keys_of(sub, carry):
+                    at = pl.ds(pl.multiple_of(sub * size, size), size)
                     k = kvc[i % slots, at, pl.ds(kt, 128)]
                     v = kvc[i % slots, at, pl.ds(vt, 128)]
                     scores = dg(q, k, NT) * (SCALE * LOG2E)
@@ -948,6 +1035,12 @@
                     else:
                         dkv[at, pl.ds(kt, 128)] += gk_
                         dkv[at, pl.ds(vt, 128)] += gv
+                    return carry
+
+                if subs > 1:
+                    lax.fori_loop(0, subs, keys_of, 0)
+                else:
+                    keys_of(0, 0)
 
             step(c, True)
 
@@ -971,27 +1064,31 @@
 
                 @pl.when(i == 2)
                 def _():
+                    chip_sum(2)
                     reduce_step(2)
-
-                @pl.when(i == 3)
-                def _():
-                    reduce_step(3)
-                    gather_first()
 
             @pl.when(h == 2)
             def _():
                 @pl.when(i == 0)
                 def _():
                     out_1()
+                    chip_sum(0)
 
                 @pl.when(i == 1)
                 def _():
+                    chip_sum(1)
                     reduce_step(1)
                     out_2()
 
                 @pl.when(i == 2)
                 def _():
                     out_3()
+
+                @pl.when(i == 3)
+                def _():
+                    chip_sum(3)
+                    reduce_step(3)
+                    gather_first()
 
             return carry
 
@@ -1087,7 +1184,7 @@
     inv = inv_rms(u)
     gain = jnp.concatenate([gfull[0, 0:1, :], gfull[1, 0:1, :]], axis=1)
     result = gmid[...] + crms_back(u, inv, gain, h)
-    gin[...] = result[:, : width - 1]
+    gin[...] = result
     first = jnp.sum(h * (u * inv), axis=0, keepdims=True)
     which = lax.broadcasted_iota(jnp.int32, (8, width), 0)
     g0[...] = jnp.where(which == 0, first, dg2[...])
@@ -1169,6 +1266,7 @@
         for c in others:
             chip_share(p.chip, g, c).wait_send()
             yc(g, c, p.chip).wait_send()
+            over_chips(c, p.chip, g).wait_send()
     for c in others:
         qc(c, p.chip).wait_send()
         gc(c, p.chip).wait_send()
@@ -1202,13 +1300,13 @@
                 leftward(p.a - s, red.at[0]).wait_send()
 
 
-def back(n, lens, q3, kv, o3, l3, dog, wg, h1, rp, gmid, gfull, dg2, red, go):
+def back(n, lens, q3, kv, o3, l3, dog, wg, h1, rp, gmid, gfull, dg2, ysum, go):
     rows, width = rp.shape
     quarter = width // 4
     lanes = wg.shape[2]
     chips = n // GROUPS // 2
     keys = kv.shape[0] // GROUPS
-    piece = red.shape[1]
+    piece = ysum.shape[2]
     orow = go.shape[0] // 2
     sds = jax.ShapeDtypeStruct
     v = pltpu.VMEM
@@ -1217,15 +1315,18 @@
         functools.partial(back_kernel, n),
         name="back",
         out_shape=(
-            sds((rows, width - 1), F32),
+            sds((rows, width), F32),
             sds((GROUPS, 2, quarter, lanes), BF16),
             sds((8, width), F32),
             sds((2, chips, GROUPS, piece, width), BF16),
             sds((2, GROUPS, orow // GROUPS, width), BF16),
         ),
-        in_specs=[SM, VM, ANY, VM, VM, VM, ANY] + [VM] * 7,
+        in_specs=[SM, VM, ANY, ANY, VM, VM, ANY] + [VM] * 5 + [ANY, VM],
         out_specs=[VM] * 5,
         scratch_shapes=[
+            v((GROUPS, piece, width), BF16),
+            v((GROUPS, piece, width), BF16),
+            v(ysum.shape, BF16),
             v(q3.shape, BF16),
             v(q3.shape, F32),
             v((2 if keys <= SUB else 1, keys, 384), BF16),
@@ -1255,7 +1356,7 @@
             v((GROUPS, orow // GROUPS, width), BF16),
             v((GROUPS, orow // GROUPS, width), BF16),
             *sem(GROUPS),
-            DMA((GROUPS,)),
+            DMA((GROUPS + 2,)),
             DMA((2,)),
             *sem(GROUPS, chips),
             *sem(GROUPS + 1, chips),
@@ -1275,65 +1376,112 @@
             *sem(chips),
             *sem(2 * GROUPS),
             *sem(1 + GROUPS),
+            *sem(chips, GROUPS),
         ],
         compiler_params=pltpu.CompilerParams(
             collective_id=2, has_side_effects=True, vmem_limit_bytes=67043328
         ),
-    )(lens, q3, kv, o3, l3, dog, wg, h1, rp, gmid, gfull, dg2, red, go)
-
-
-def by_group(w):
-    r = w.shape[0]
-    w = w.reshape(r, 3, GROUPS, GH, HD).transpose(2, 0, 1, 3, 4)
-    q, k, v = w[:, :, 0], w[:, :, 1], w[:, :, 2]
-    zero = jnp.zeros_like(q[:, :, 0])
-    return jnp.concatenate(
-        [q[:, :, 0], q[:, :, 1], q[:, :, 2], zero, k[:, :, 0], k[:, :, 1], k[:, :, 2], v[:, :, 2],
-         v[:, :, 0], v[:, :, 1]],
-        axis=-1,
+    )(lens, q3, kv, o3, l3, dog, wg, h1, rp, gmid, gfull, dg2, ysum, go)
+
+
+def deliver_kernel(gq, ra, rb, rd, goo, gsum, gin, out, out_, gin_, g1_, qkv_, go_, g2_, up_, down_):
+    narrow = gin_.shape[2]
+    half = g1_.shape[0]
+    width = 2 * half
+    out_[0] = out[:, :narrow]
+    gin_[0] = gin[:, :narrow]
+    go_[...] = goo[:, :narrow].astype(F32)
+    down_[...] = rd[0, :, :narrow].astype(F32)
+    up_[:, :width] = ra[0].astype(F32)
+    up_[:, width:] = rb[0].astype(F32)
+    first = lax.axis_index("fsdp") == 0
+    g1_[...] = jnp.where(first, gsum[0, :half], gsum[0, half:])
+    g2_[...] = jnp.where(first, gsum[1, :half], gsum[1, half:])
+    low = low_half((gq.shape[1], 128))
+
+    def tile(g, t):
+        return gq[g, :, t * 128 : (t + 1) * 128].astype(F32)
+
+    def swap(t):
+        return pltpu.roll(t, HD, 1)
+
+    for j in range(GROUPS // 2):
+        a, b = 2 * j, 2 * j + 1
+        parts = []
+        for t in (0, 2):
+            pair = swap(tile(b, t))
+            parts.append(
+                (tile(a, t), jnp.where(low, tile(a, t + 1), pair), jnp.where(low, pair, swap(tile(b, t + 1))))
+            )
+        pair = swap(tile(b, 4))
+        parts.append(
+            (tile(a, 4), jnp.where(low, swap(tile(a, 3)), pair), jnp.where(low, pair, tile(b, 3)))
+        )
+        for i, three in enumerate(parts):
+            for t, value in enumerate(three):
+                at = i * width + j * 384 + t * 128
+                qkv_[:, at : at + 128] = value
+
+
+def deliver(gq, res, goo, gsum, gin, out):
+    rows, width = gin.shape
+    half = width // 2
+    ff = res.shape[1]
+    steps = 4
+    sds = jax.ShapeDtypeStruct
+    spec = pl.BlockSpec
+    return pl.pallas_call(
+        deliver_kernel,
+        name="deliver",
+        grid=(steps,),
+        out_shape=(
+            sds((1, rows, width - 1), BF16),
+            sds((1, rows, width - 1), F32),
+            sds((half,), F32),
+            sds((half, 3 * width), F32),
+            sds((half, width - 1), F32),
+            sds((half,), F32),
+            sds((width, ff), F32),
+            sds((ff, width - 1), F32),
+        ),
+        in_specs=[
+            spec((GROUPS, half // steps, gq.shape[2]), lambda i: (0, i, 0)),
+            spec((1, width // steps, width), lambda i: (0, i, 0)),
+            spec((1, width // steps, width), lambda i: (0, steps + i, 0)),
+            spec((1, ff // steps, width), lambda i: (1, i, 0)),
+            spec((half // steps, width), lambda i: (i, 0)),
+            spec(gsum.shape, lambda i: (0, 0)),
+            spec((rows // steps, width), lambda i: (i, 0)),
+            spec((rows // steps, width), lambda i: (i, 0)),
+        ],
+        out_specs=[
+            spec((1, rows // steps, width - 1), lambda i: (0, i, 0)),
+            spec((1, rows // steps, width - 1), lambda i: (0, i, 0)),
+            spec((half,), lambda i: (0,)),
+            spec((half // steps, 3 * width), lambda i: (i, 0)),
+            spec((half // steps, width - 1), lambda i: (i, 0)),
+            spec((half,), lambda i: (0,)),
+            spec((width // steps, ff), lambda i: (i, 0)),
+            spec((ff // steps, width - 1), lambda i: (i, 0)),
+        ],
+        compiler_params=pltpu.CompilerParams(vmem_limit_bytes=VLIM),
+    )(gq, res, res, res, goo, gsum, gin, out)
+
+
+def shards(n, resid, lengths, gain_one, w_qkv, w_out, gain_two, w_up, w_down, cotangent):
+    width = resid.shape[2] + 1
+    ff = w_up.shape[1]
+    out, gmid, ysum, go, dog, dg2, rp, wg, h1, q3, kv, o3, l3, gfull = front(
+        n, lengths, resid[0], cotangent[0], gain_one, gain_two, w_qkv, w_out, w_up, w_down
     )
-
-
-def from_groups(g):
-    r = g.shape[1]
-    t = g.reshape(GROUPS, r, 10, HD).transpose(1, 0, 2, 3)
-    q = t[:, :, 0:3]
-    k = t[:, :, 4:7]
-    v = jnp.stack([t[:, :, 8], t[:, :, 9], t[:, :, 7]], axis=2)
-    return jnp.stack([q, k, v], axis=1).reshape(r, 3 * GROUPS * GH * HD)
-
-
-def shards(n, resid, lengths, gain_one, w_qkv, w_out, gain_two, w_up, w_down, cotangent):
-    _, rows, narrow = resid.shape
-    width = narrow + 1
-    ff = w_up.shape[1]
-    c = lax.axis_index("ctx")
-    pos = c * rows + jnp.arange(rows, dtype=jnp.int32)
-    pad = ((0, 0), (0, 1))
-    rp = jnp.pad(resid[0], pad)
-    live = pos[:, None] < lengths[0]
-    cp = jnp.pad(jnp.where(live, cotangent[0], jnp.zeros_like(cotangent[0])), pad)
-    wo = jnp.pad(w_out, pad)
-    wd = jnp.pad(w_down, pad)
-    gains = jnp.pad(jnp.stack([gain_one, gain_two]).astype(F32), ((0, 6), (0, 0)))
-    wg = by_group(w_qkv)
-    meta = jnp.stack([c % (n // GROUPS), lengths[0]]).astype(jnp.int32)
-
-    h1, q3, kv, _, woa, gfull = project(n, rp, gains, wg, wo)
-    att, o3, l3 = attend(meta, q3, kv)
-    out, gmid, red, go, dog, dg2 = mlp(n, att, rp, cp, gfull, woa, w_up, wd)
     gin, gq, gsum, res, goo = back(
-        n, lengths, q3, kv, o3, l3, dog, wg, h1, rp, gmid, gfull, dg2, red, go
+        n, lengths, q3, kv, o3, l3, dog, wg, h1, rp, gmid, gfull, dg2, ysum, go
     )
 
     half = width // 2
-    grad_qkv = from_groups(gq.reshape(GROUPS, half, -1).astype(F32))
-    mine = lax.dynamic_slice_in_dim(gsum, lax.axis_index("fsdp") * half, half, 1)
-    res = res.reshape(2, ff, width)
-    up = jnp.concatenate([res[0, :width], res[0, width:]], axis=1).astype(F32)
-    down = res[1, :, :narrow].astype(F32)
-    gout = goo.reshape(half, width)[:, :narrow].astype(F32)
-    return out[None], gin[None], mine[0], grad_qkv, gout, mine[1], up, down
+    return deliver(
+        gq.reshape(GROUPS, half, -1), res.reshape(2, ff, width), goo.reshape(half, width), gsum, gin, out
+    )
 
 
 def solution(mesh):

time: 321 us -> 256 us (0.80)
  local copies, waits for them, and re-layouts: 48.2 us -> 3.02 us
  other arithmetic: 10.9 us -> 0 us
  Pallas kernels: 260 us -> 252 us
    pallas_call x3 -> x2, Pallas kernels: 130 us -> 109 us  [the longest x1 100 us: front(): pl.pallas_call(functools.partial(front_kernel, n), name='front', out_shap...]
    transpose x2 -> x0, local copies, waits for them, and re-layouts: 14.7 us -> none  [from_groups(): t = g.reshape(GROUPS, r, 10, HD).transpose(1, 0, 2, 3)]
    pallas_call x1, Pallas kernels: 129 us -> 142 us  [back(): pl.pallas_call(functools.partial(back_kernel, n), name='back', out_shape=...]
    unnamed x12 -> x0, local copies, waits for them, and re-layouts: 10.6 us -> none
    convert_element_type x3 -> x0, other arithmetic: 9.24 us -> none  [the longest x1 4.26 us: shards(): down = res[1, :, :narrow].astype(F32)]
    pad x4 -> x0, local copies, waits for them, and re-layouts: 6.13 us -> none  [the longest x1 1.93 us: shards(): wo = jnp.pad(w_out, pad)]
    concatenate x1 -> x0, local copies, waits for them, and re-layouts: 4.71 us -> none  [by_group(): jnp.concatenate([q[:, :, 0], q[:, :, 1], q[:, :, 2], zero, k[:, :, 0], k[...]
    slice x3 -> x0, local copies, waits for them, and re-layouts: 3.93 us -> none  [the longest x2 2.48 us: from_groups(): v = jnp.stack([t[:, :, 8], t[:, :, 9], t[:, :, 7]], axis=2)]
where the time goes in v3:
time: 256 us
  Pallas kernels  252 us (98%)
  local copies, waits for them, and re-layouts  3.02 us (1%)
    pallas_call x1, Pallas kernels, back(): pl.pallas_call(functools.partial(back_kernel, n), name='back', out_shape=...  142 us
    pallas_call x1, Pallas kernels, front(): pl.pallas_call(functools.partial(front_kernel, n), name='front', out_shap...  100 us
    pallas_call x1, Pallas kernels, deliver(): pl.pallas_call(deliver_kernel, name='deliver', grid=(steps,), out_shape=(...  9.19 us

profile of v3, /device:TPU:0, one launch (start us, length us, event | category | flops | bytes accessed | tf_op | source)
XLA Modules:
  0.0 255.9 jit_solution(15560587009955529124)
XLA Ops:
  1.3 100.0 %front.1 = (bf16[256,768]{1,0:T(8,128)(2,1)}, f32[256,768]{1,0:T(8,128)}, bf16[2,4,192,768]{3,2,1,0:T(8,128)(2,1)}, bf16[384,768]{1,0:T(8,128)(2,1)}, bf16[4,384...) custom-call(s32[1]{0:T(128)S(6)} %copy.18.lens, ...), custom_call_target="tpu_custom_call" | custom-call | tf_op jit(solution)/shard_map/front/pallas_call | solution.py:646
  101.2 142.4 %back.1 = (f32[256,768]{1,0:T(8,128)}, bf16[4,2,192,640]{3,2,1,0:T(8,128)(2,1)}, f32[8,768]{1,0:T(8,128)}, bf16[2,2,4,192,768]{4,3,2,1,0:T(8,128)(2,1)}, bf16[2,4,48,768]{3,2,1,0:T(8,128)(2,1)}) custom-call(s32[1]{0:T(128)S(6)} %copy.18.lens, bf16[3,1024,128]{2,1,0:T(8,128)(2,1)} %get-tuple-element.27.q3, bf16[4096,384]{1,0:T(8,128)(2,1)} %get-tuple-element.28.kv, ...), custom_call_target="tpu_custom_call" | custom-call | tf_op jit(solution)/shard_map/back/pallas_call | solution.py:1314
  243.7 9.2 %deliver.1 = (bf16[1,256,767]{2,1,0:T(8,128)(2,1)}, f32[1,256,767]{2,1,0:T(8,128)}, f32[384]{0:T(512)}, f32[384,2304]{1,0:T(8,128)}, f32[384,767]{1,0:T(8,128)},...) custom-call(bf16[4,384,640]{2,1,0:T(8,128)(2,1)} %bitcast.8, bf16[2,1536,768]{2,1,0:T(8,128)(2,1)} %bitcast.5, ...), custom_call_target="tpu_custom_call" | custom-call | tf_op jit(solution)/shard_map/deliver/pallas_call | solution.py:1433
  252.9 3.0 %copy.17 = f32[1,256,767]{1,0,2:T(1,128)} copy(f32[1,256,767]{2,1,0:T(8,128)} %get-tuple-element.47) | data formatting | bytes 1570816 | tf_op jit(solution)/shard_map/deliver/pallas_call | solution.py:1433

commit v4 on v3

--- a/solution.py
+++ b/solution.py
@@ -91,6 +91,13 @@
     return lambda: pl.semaphore_wait(bar, count)
 
 
+def turn(p, j):
+    last = GROUPS - 1
+    outer = jnp.where(p.a == 0, last - j, j)
+    inner = (0, last, 1, last - 1)[j]
+    return jnp.where((p.a == 0) | (p.a == last), outer, jnp.where(p.a == 1, last - inner, inner))
+
+
 def ext_of(v):
     last = lax.broadcasted_iota(jnp.int32, v.shape, 1) == v.shape[1] - 1
     return jnp.where(last, -jnp.sum(v, axis=1, keepdims=True), v)
@@ -167,9 +174,9 @@
 
 def front_kernel(
     n, lens, ri, ci, g1, g2, wq, wo, wuh, wdh,
-    out, gmid, ysum, go, dog, dg2, rp, wg, h1, q3, kv, o3, l3, gfull,
-    gains, wop, wa, woa, wu, wdr, wd, att, attg, attp, wide, hid, gmb, act, gpre, esum, dsend, gbb, mid, gk,
-    ss, rs, ls, hs, hr, vs, kr, fs, xs, xr, cs, cr, ts, tr, as_, ar, ds_, dr, ks, ks_r,
+    out, gmid_, ysum_, y0, gb_, attg, dog, dg2, rp_, wg_, h1_, q3_, kv_, o3_, l3_, gfull,
+    gmid, ysum, rp, wg, h1, q3, kv, o3, l3, gains, wop, wa, woa, wu, wdr, wd, att, wide, hid, gmb, act, gpre, esum, dsend, gb, mid, gk,
+    ss, rs, ls, hs, hr, vs, kr, fs, xs, xr, cs, cr, ts, tr, as_, ar, ds_, dr, ks, ks_r, ys, yr, us,
 ):
     p = Place(n)
     rows, narrow = ri.shape
@@ -189,9 +196,13 @@
     own_u.start()
     own_d.start()
 
-    rp[:, :narrow] = ri[...]
-    rp[:, narrow:] = jnp.zeros((rows, 1), BF16)
-    group_columns(wq, wg)
+    leaving = []
+
+    def leave(src, dst):
+        c = pltpu.make_async_copy(src, dst, us.at[len(leaving)])
+        c.start()
+        leaving.append(c)
+
     gains[0:1, :] = g1[...].astype(F32).reshape(1, half)
     gains[1:2, :] = g2[...].astype(F32).reshape(1, half)
     gfull[p.x] = gains[...]
@@ -203,42 +214,79 @@
     at_x = pl.ds(pl.multiple_of(p.x * half, half), half)
     x_gain = xc(0, gains, gfull.at[p.x])
     x_gain.start()
+    rp[:, :narrow] = ri[...]
+    rp[:, narrow:] = jnp.zeros((rows, 1), BF16)
+    u = ext_of(rp[...].astype(F32))
+    normed = u * inv_rms(u)
+    x_gain.wait()
+    gain = jnp.concatenate([gfull[0, 0:1, :], gfull[1, 0:1, :]], axis=1)
+    h1[p.a] = (normed * gain).astype(BF16)
+
+    def line_copy(block, dst, sem):
+        return rcopy(h1.at[block], h1.at[block], hs.at[sem], hr.at[block], p.on_line(dst))
+
+    @pl.when(p.a < GROUPS - 1)
+    def _():
+        line_copy(p.a, p.a + 1, 0).start()
+
+    @pl.when(p.a > 0)
+    def _():
+        line_copy(p.a, p.a - 1, 1).start()
+
+    group_columns(wq, wg)
     x_wa = xc(1, wg.at[p.a], wa.at[at_x])
     x_wa.start()
-
-    def cut(i, chip, core):
-        size_i = (width, ff)[i] // p.m
+    own_a = pltpu.make_async_copy(wg.at[p.a], wa.at[at_x], ls.at[0])
+    own_a.start()
+    leave(rp, rp_)
+    leave(wg, wg_)
+
+    def up_rows(j, chip, core):
+        size_i = width // p.m // 3
+        return pl.ds(pl.multiple_of(((chip * 2 + core) * 3 + j) * size_i, size_i), size_i)
+
+    def up_x(j):
+        at = up_rows(j, p.chip, p.k)
+        return rcopy(wuh.at[at], wu.at[p.x, at], xs.at[j], xr.at[j], p.xpeer())
+
+    def up_chip(j, owner, to):
+        r = wu.at[other, up_rows(j, owner, p.k)]
+        return rcopy(r, r, cs.at[j, to], cr.at[j, owner], p.on_chip(to))
+
+    def up_core(j, owner, core):
+        r = wu.at[other, up_rows(j, owner, core)]
+        return rcopy(r, r, ts.at[j, owner], tr.at[j, owner], p.sibling())
+
+    def up_spread(j):
+        up_x(j).wait_recv()
+        for c in others:
+            up_chip(j, p.chip, c).start()
+        up_core(j, p.chip, p.k).start()
+
+    def up_pass(j):
+        for c in others:
+            up_chip(j, c, c).wait_recv()
+            up_core(j, c, p.k).start()
+
+    def down_rows(chip, core):
+        size_i = ff // p.m
         return pl.ds(pl.multiple_of((chip * 2 + core) * size_i, size_i), size_i)
 
-    def weight_x(i):
-        at = cut(i, p.chip, p.k)
-        return rcopy((wuh, wdh)[i].at[at], (wu, wdr)[i].at[p.x, at], xs.at[i], xr.at[i], p.xpeer())
-
-    def weight_chip(i, owner, to):
-        r = (wu, wdr)[i].at[other, cut(i, owner, p.k)]
-        return rcopy(r, r, cs.at[i, to], cr.at[i, owner], p.on_chip(to))
-
-    def weight_core(i, owner, core):
-        r = (wu, wdr)[i].at[other, cut(i, owner, core)]
-        return rcopy(r, r, ts.at[i, owner], tr.at[i, owner], p.sibling())
-
-    def weight_spread(i):
-        weight_x(i).wait_recv()
-        for c in others:
-            weight_chip(i, p.chip, c).start()
-        weight_core(i, p.chip, p.k).start()
-
-    def weight_pass(i):
-        for c in others:
-            weight_chip(i, c, c).wait_recv()
-            weight_core(i, c, p.k).start()
-
-    def weight_end(i):
-        for c in range(p.chips):
-            weight_core(i, c, 1 - p.k).wait_recv()
-
-    weight_x(0).start()
-    weight_x(1).start()
+    def down_x():
+        at = down_rows(p.chip, p.k)
+        return rcopy(wdh.at[at], wdr.at[p.x, at], xs.at[3], xr.at[3], p.xpeer())
+
+    def down_chip(owner, to):
+        r = wdr.at[other, down_rows(owner, p.k)]
+        return rcopy(r, r, cs.at[3, to], cr.at[3, owner], p.on_chip(to))
+
+    def down_core(owner, core):
+        r = wdr.at[other, down_rows(owner, core)]
+        return rcopy(r, r, ts.at[3, owner], tr.at[3, owner], p.sibling())
+
+    for j in range(3):
+        up_x(j).start()
+    down_x().start()
 
     wop[:, :narrow] = wo[...]
     wop[:, narrow:] = jnp.zeros((half, 1), BF16)
@@ -265,31 +313,12 @@
     gmb[0] = jnp.where(live, gmb[0].astype(F32), 0.0).astype(BF16)
     x_gm = xc(6, gmb.at[0], gmb.at[1])
     x_gm.start()
-    own_a = pltpu.make_async_copy(wg.at[p.a], wa.at[at_x], ls.at[0])
-    own_a.start()
-    u = ext_of(rp[...].astype(F32))
-    normed = u * inv_rms(u)
-    x_gain.wait()
-    gain = jnp.concatenate([gfull[0, 0:1, :], gfull[1, 0:1, :]], axis=1)
-    h1[p.a] = (normed * gain).astype(BF16)
-
-    def line_copy(block, dst, sem):
-        return rcopy(h1.at[block], h1.at[block], hs.at[sem], hr.at[block], p.on_line(dst))
-
     def kv_copy(block, b, dev, send):
         r = kv.at[pl.ds(pl.multiple_of((block * p.m + b) * rows, rows), rows)]
         return rcopy(r, r, send, kr.at[block, b], dev)
 
     def ac(i, to):
         return rcopy(att.at[to], attg.at[i], as_.at[to], ar.at[i], p.on_line(to))
-
-    @pl.when(p.a < GROUPS - 1)
-    def _():
-        line_copy(p.a, p.a + 1, 0).start()
-
-    @pl.when(p.a > 0)
-    def _():
-        line_copy(p.a, p.a - 1, 1).start()
 
     own_a.wait()
     x_wa.wait()
@@ -424,21 +453,26 @@
             def _():
                 line_copy(above, p.a - 1, 2 * s + 1).start()
 
-        @pl.when(s == GROUPS - 1)
-        def _():
-            weight_spread(0)
+        @pl.when(below >= 0)
+        def _():
+            produce(below)
+
+        @pl.when((s > 0) & (above < GROUPS))
+        def _():
+            produce(above)
+
+        for j in range(3):
+
+            @pl.when(s == j + 1)
+            def _():
+                up_spread(j)
 
         @pl.when(s == GROUPS)
         def _():
-            weight_spread(1)
-
-        @pl.when(below >= 0)
-        def _():
-            produce(below)
-
-        @pl.when((s > 0) & (above < GROUPS))
-        def _():
-            produce(above)
+            down_x().wait_recv()
+            for c in others:
+                down_chip(p.chip, c).start()
+            down_core(p.chip, p.k).start()
 
         @pl.when((s > 0) & (below + 1 >= 0))
         def _():
@@ -454,10 +488,17 @@
         def _():
             pairs(s - 1)
 
+        for j in range(3):
+
+            @pl.when(s == j + 2)
+            def _():
+                up_pass(j)
+
         return carry
 
     lax.fori_loop(0, GROUPS + 1, step, 0)
-    weight_pass(0)
+    for src, dst in ((h1, h1_), (q3, q3_), (kv, kv_), (o3, o3_), (l3, l3_)):
+        leave(src, dst)
 
     own_u.wait()
     own_d.wait()
@@ -473,7 +514,6 @@
         c.wait()
     for g in line:
         ac(g, g).wait_recv()
-    x_att = [xc(7 + i, attg.at[other * 2 + i], attp.at[i]) for i in range(2)]
     for g in range(GROUPS):
         wide[:, g * 256 : g * 256 + 128] = attg[g, 0:rows, :]
         top, bottom = unpack_tail(attg[g, rows:pk, :])
@@ -485,8 +525,6 @@
     hid[0] = (u * inv_rms(u) * gain).astype(BF16)
     x_hid = xc(9, hid.at[0], hid.at[1])
     x_hid.start()
-    for c in x_att:
-        c.start()
     tiles = ff // 256
 
     def up(slot, token, f):
@@ -499,10 +537,15 @@
 
         lax.fori_loop(0, tiles, tile, 0)
 
-    weight_pass(1)
     up(0, 0, p.x)
-    weight_end(0)
-    weight_end(1)
+    for c in others:
+        down_chip(c, c).wait_recv()
+        down_core(c, p.k).start()
+    for j in range(3):
+        for c in range(p.chips):
+            up_core(j, c, 1 - p.k).wait_recv()
+    for c in range(p.chips):
+        down_core(c, 1 - p.k).wait_recv()
     pad_down(other)
     up(2, 0, other)
 
@@ -517,9 +560,9 @@
     u = ext_of(mid[...])
     inv = inv_rms(u)
     gmid[...] = gmb[0].astype(F32) + crms_back(u, inv, gain, e)
-    gbb[0] = gmid[...].astype(BF16)
-    x_gb = xc(10, gbb.at[0], gbb.at[1])
-    x_gb.start()
+    leave(gmid, gmid_)
+    gb[...] = gmid[...].astype(BF16)
+    leave(gb, gb_)
 
     def dc(i, to):
         return rcopy(dsend.at[to], dog.at[i], ds_.at[to], dr.at[i], p.on_line(to))
@@ -527,7 +570,7 @@
     for d in range(1, GROUPS + 1):
         to = (p.a + d) % GROUPS
         w = woa[pl.ds(pl.multiple_of(to * 256, 256), 256), :]
-        da = dg(gbb[0], w, NT).astype(BF16)
+        da = dg(gb[...], w, NT).astype(BF16)
         if d < GROUPS:
             dsend[to, 0:rows, :] = da[:, 0:128]
             dsend[to, rows:pk, :] = pack_tail(da[:, 128:256])
@@ -584,23 +627,30 @@
     def _():
         lax.fori_loop(0, tiles, grad_down, 0)
 
-    for chip in others + [p.chip]:
+    def over_chips(chip, slot):
+        return rcopy(ysum.at[chip, turn(p, 0)], y0.at[slot], ys.at[chip], yr.at[slot], p.on_chip(chip))
+
+    def core_sum(chip, z):
+        at = pl.ds(pl.multiple_of(chip * part + z * piece, 16), piece)
+        ysum[chip, z] = (gm[p.k, at, :].astype(F32) + gk[at, :].astype(F32)).astype(BF16)
+
+    for chip in others:
         kc(chip).wait()
-        for z in range(GROUPS):
-            at = pl.ds(pl.multiple_of(chip * part + z * piece, 16), piece)
-            ysum[chip, z] = (gm[p.k, at, :].astype(F32) + gk[at, :].astype(F32)).astype(BF16)
+        core_sum(chip, turn(p, 0))
+        over_chips(chip, p.chip).start()
+    for j in range(1, GROUPS):
+        for chip in others:
+            core_sum(chip, turn(p, j))
+    kc(p.chip).wait()
+    for j in range(GROUPS):
+        core_sum(p.chip, turn(p, j))
+    y0[p.chip] = ysum[p.chip, turn(p, 0)]
+    leave(ysum, ysum_)
     dg2[...] = jnp.broadcast_to(jnp.sum(e * (u * inv), axis=0, keepdims=True), dg2.shape)
-    for c in x_att:
-        c.wait()
-    x_gb.wait()
-    for i in range(2):
-        own_tail = jnp.concatenate(unpack_tail(attg[p.x * 2 + i, rows:pk, :]), axis=0)
-        peer_tail = jnp.concatenate(unpack_tail(attp[i, rows:pk, :]), axis=0)
-        g = dg(attg[p.x * 2 + i, 0:rows, :], gbb[0], TN) + dg(attp[i, 0:rows, :], gbb[1], TN)
-        go[i * 192 : i * 192 + 128, :] = g.astype(BF16)
-        g = dg(own_tail, gbb[0], TN) + dg(peer_tail, gbb[1], TN)
-        go[i * 192 + 128 : i * 192 + 192, :] = g[HD:, :].astype(BF16)
-
+
+    for c in others:
+        over_chips(c, p.chip).wait_send()
+        over_chips(c, c).wait_recv()
     for g in line:
         ac(p.a, g).wait_send()
         dc(p.a, g).wait_send()
@@ -621,12 +671,19 @@
         def _():
             line_copy(p.a + s, p.a - 1, 2 * s + 1).wait_send()
 
-    for i in range(2):
-        weight_x(i).wait_send()
+    for j in range(3):
+        up_x(j).wait_send()
         for c in others:
-            weight_chip(i, p.chip, c).wait_send()
+            up_chip(j, p.chip, c).wait_send()
         for c in range(p.chips):
-            weight_core(i, c, p.k).wait_send()
+            up_core(j, c, p.k).wait_send()
+    down_x().wait_send()
+    for c in others:
+        down_chip(p.chip, c).wait_send()
+    for c in range(p.chips):
+        down_core(c, p.k).wait_send()
+    for c in leaving:
+        c.wait()
 
 
 def front(n, lens, ri, ci, g1, g2, wq, wo, wu, wd):
@@ -650,7 +707,9 @@
             sds((rows, width), BF16),
             sds((rows, width), F32),
             sds((chips, GROUPS, piece, width), BF16),
-            sds((half, width), BF16),
+            sds((chips, piece, width), BF16),
+            sds((rows, width), BF16),
+            sds((GROUPS, pk, 128), BF16),
             sds((GROUPS, pk, 128), BF16),
             sds((8, width), F32),
             sds((rows, width), BF16),
@@ -663,8 +722,17 @@
             sds((2, 8, half), F32),
         ),
         in_specs=[SM, VM, VM, VM, VM, VM, VM, ANY, ANY],
-        out_specs=[VM] * 14,
+        out_specs=[VM, ANY, ANY, VM, ANY] + [VM] * 3 + [ANY] * 7 + [VM],
         scratch_shapes=[
+            v((rows, width), F32),
+            v((chips, GROUPS, piece, width), BF16),
+            v((rows, width), BF16),
+            v((GROUPS, half, lanes), BF16),
+            v((GROUPS, rows, width), BF16),
+            v(heads, BF16),
+            v((n * rows, 384), BF16),
+            v(heads, F32),
+            v(heads, F32),
             v((8, half), F32),
             v((half, width), BF16),
             v((width, lanes), BF16),
@@ -673,8 +741,6 @@
             v((2, ff, narrow), BF16),
             v((2, ff, width), BF16),
             v((GROUPS, pk, 128), BF16),
-            v((GROUPS, pk, 128), BF16),
-            v((2, pk, 128), BF16),
             v((rows, GROUPS * 256), BF16),
             v((2, rows, width), BF16),
             v((2, rows, width), BF16),
@@ -682,22 +748,24 @@
             v((3, rows, ff), BF16),
             v((width // 256, rows, 256), F32),
             v((GROUPS, pk, 128), BF16),
-            v((2, rows, width), BF16),
+            v((rows, width), BF16),
             v((rows, width), F32),
             v((ff, width), BF16),
-            *sem(11),
+            *sem(10),
             DMA((7,)),
             DMA((2 * GROUPS,)),
             DMA((GROUPS,)),
             DMA((GROUPS, chips)),
             DMA((GROUPS, m)),
             DMA((GROUPS, chips)),
-            *sem(2),
-            *sem(2, chips),
-            *sem(2, chips),
+            *sem(4),
+            *sem(4, chips),
+            *sem(4, chips),
             *sem(GROUPS),
             *sem(GROUPS),
             *sem(chips),
+            *sem(chips),
+            DMA((10,)),
         ],
         compiler_params=pltpu.CompilerParams(
             collective_id=0, has_side_effects=True, vmem_limit_bytes=67043328
@@ -706,15 +774,15 @@
 
 
 def back_kernel(
-    n, lens, q3, kv, o3, l3, dog, wg, h1, rp, gmid, gfull, dg2, ysum, go,
+    n, lens, q3, kv, o3, l3, dog, wg, h1_, rp_, gmid_, gfull, dg2, ysum, y0, gb_, att_,
     gin, gq, gains, res, goo,
-    red, ymine, yq, do3, dq3, kvc, dkv, dkvb, rk, ry, wfull, gps, gpr, gqb, qk, qx, qy,
+    h1, rp, gmid, go, gb, att, red, ymine, yq, do3, dq3, kvc, dkv, dkvb, rk, ry, wfull, gps, gpr, gqb, qk, qx, qy,
     g0, gk, gx, gy, ga, left, right, sumr, suml, ok, os_, oy, oz, ozr,
     xs, xr, ls, vs, ks, kr, ys, yr, zs, zr, ws, wr, qs, qr, ns, nr, bs, br, cs, cr,
-    rs_, rr, ls_, lr, as_, ar, es, er, fs, fr, ts, tr, us, ur, is_, ir, ps, pr,
+    rs_, rr, ls_, lr, as_, ar, es, er, fs, fr, ts, tr, us, ur, is_, ir, ps, pr, ws2, wr2, zs2, zr2,
 ):
     p = Place(n)
-    rows, width = rp.shape
+    rows, width = rp_.shape
     half = width // 2
     quarter = width // 4
     last = GROUPS - 1
@@ -743,26 +811,48 @@
     o_in.start()
     y_in = pltpu.make_async_copy(ysum.at[p.chip], ymine, ls.at[GROUPS + 1])
     y_in.start()
+    late = [
+        pltpu.make_async_copy(src, dst, ls.at[GROUPS + 2 + i])
+        for i, (src, dst) in enumerate(((h1_, h1), (rp_, rp), (gmid_, gmid)))
+    ]
+    for c in late:
+        c.start()
+    gos = [
+        pltpu.make_async_copy(src, dst, ls.at[GROUPS + 5 + i])
+        for i, (src, dst) in enumerate(((gb_, gb.at[0]), (att_.at[pl.ds(p.x * 2, 2)], att.at[0])))
+    ]
+    for c in gos:
+        c.start()
+    gox = [
+        rcopy(src, dst, zs2.at[i], zr2.at[i], p.xpeer())
+        for i, (src, dst) in enumerate(((gb_, gb.at[1]), (att_.at[pl.ds((1 - p.x) * 2, 2)], att.at[1])))
+    ]
     for c in local:
         c.start()
-    wx = [
-        rcopy(wg.at[g], wfull.at[g, at_x], xs.at[g], xr.at[g], p.xpeer()) for g in range(GROUPS)
-    ]
+
+    def weight_rows(x, core):
+        return pl.ds(pl.multiple_of(x * half + core * quarter, quarter), quarter)
+
+    def weight_x(g):
+        src = wg.at[g, pl.ds(pl.multiple_of(p.k * quarter, quarter), quarter)]
+        return rcopy(src, wfull.at[g, weight_rows(p.x, p.k)], xs.at[g], xr.at[g], p.xpeer())
+
+    def weight_core(g, core):
+        r = wfull.at[g, weight_rows(1 - p.x, core)]
+        return rcopy(r, r, ws2.at[g], wr2.at[g], p.sibling())
 
     def over_chips(chip, slot, z):
         return rcopy(ysum.at[chip, z], yq.at[slot, z], ps.at[chip, z], pr.at[slot, z], p.on_chip(chip))
 
-    def turn(j):
-        outer = jnp.where(p.a == 0, last - j, j)
-        inner = (0, last, 1, last - 1)[j]
-        return jnp.where((p.a == 0) | (p.a == last), outer, jnp.where(p.a == 1, last - inner, inner))
-
     def chip_sum(j):
-        z = turn(j)
+        z = turn(p, j)
         total = ymine[z].astype(F32)
         for c in others:
-            over_chips(c, c, z).wait_recv()
-            total = total + yq[c, z].astype(F32)
+            if j > 0:
+                over_chips(c, c, z).wait_recv()
+                total = total + yq[c, z].astype(F32)
+            else:
+                total = total + y0[c].astype(F32)
         red[z] = total.astype(BF16)
         if j < last:
 
@@ -835,8 +925,6 @@
         def _():
             line_share(z, p.a - 1, 1).start()
 
-        spread(z)
-
     def gather_step(s):
         @pl.when(p.a - s >= 0)
         def _():
@@ -863,18 +951,18 @@
             chip_share(c, z, c).wait_recv()
             core_share(p.k, c, z).start()
 
-    orow = go.shape[0] // 2
+    orow = half // 2
     opart = orow // GROUPS
 
     def out_core():
         at = pl.ds(pl.multiple_of((1 - p.k) * orow, orow), orow)
         return rcopy(go.at[at], ok, is_.at[0], ir.at[0], p.sibling())
 
+    def out_line(slot, to):
+        return rcopy(oz.at[to], ozr.at[slot], us.at[to], ur.at[slot], p.on_line(to))
+
     def out_chip(chip, slot):
         return rcopy(os_, oy.at[slot], ts.at[chip], tr.at[slot], p.on_chip(chip))
-
-    def out_line(slot, to):
-        return rcopy(oz.at[to], ozr.at[slot], us.at[to], ur.at[slot], p.on_line(to))
 
     def out_back(slot, to):
         r = goo.at[p.k, slot]
@@ -884,28 +972,40 @@
         r = goo.at[core, z]
         return rcopy(r, r, is_.at[1 + z], ir.at[1 + z], p.sibling())
 
+    def out_0():
+        for c in gos + gox:
+            c.wait()
+        for i in range(2):
+            tails = [jnp.concatenate(unpack_tail(att[s, i, rows:, :]), axis=0) for s in range(2)]
+            g = dg(att[0, i, 0:rows, :], gb[0], TN) + dg(att[1, i, 0:rows, :], gb[1], TN)
+            go[i * 192 : i * 192 + 128, :] = g.astype(BF16)
+            g = dg(tails[0], gb[0], TN) + dg(tails[1], gb[1], TN)
+            go[i * 192 + 128 : i * 192 + 192, :] = g[HD:, :].astype(BF16)
+        out_core().start()
+
     def out_1():
         out_core().wait()
         at = pl.ds(pl.multiple_of(p.k * orow, orow), orow)
-        os_[...] = (go[at, :].astype(F32) + ok[...].astype(F32)).astype(BF16)
+        total = go[at, :].astype(F32) + ok[...].astype(F32)
+        for z in range(GROUPS):
+            oz[z] = total[z * opart : (z + 1) * opart].astype(BF16)
+        for z in line:
+            out_line(p.a, z).start()
+
+    def out_2():
+        total = oz[p.a].astype(F32)
+        for z in line:
+            out_line(z, z).wait_recv()
+            total = total + ozr[z].astype(F32)
+        os_[...] = total.astype(BF16)
         for c in others:
             out_chip(c, p.chip).start()
 
-    def out_2():
+    def out_3():
         total = os_[...].astype(F32)
         for c in others:
             out_chip(c, c).wait_recv()
             total = total + oy[c].astype(F32)
-        for z in range(GROUPS):
-            oz[z] = total[z * opart : (z + 1) * opart].astype(BF16)
-        for z in line:
-            out_line(p.a, z).start()
-
-    def out_3():
-        total = oz[p.a].astype(F32)
-        for z in line:
-            out_line(z, z).wait_recv()
-            total = total + ozr[z].astype(F32)
         goo[p.k, p.a] = total.astype(BF16)
         for z in line:
             out_back(p.a, z).start()
@@ -963,17 +1063,19 @@
             zkv(p.a, c).start()
 
     ready()
-    out_core().start()
-    for j in range(GROUPS):
+    for j in range(1, last):
         for c in others:
-            over_chips(c, p.chip, turn(j)).start()
-    for c in wx:
+            over_chips(c, p.chip, turn(p, j)).start()
+    for c in gox:
         c.start()
+    for g in range(GROUPS):
+        weight_x(g).start()
 
     first_query = p.b * rows
     low = low_half((rows, 128))
     o_in.wait()
     y_in.wait()
+    chip_sum(0)
     for z in range(GROUPS):
         at = pl.ds(z * rows, rows)
         both = dog[z, 0:rows, :]
@@ -1056,33 +1158,16 @@
                 def _():
                     kv_2(i - 1)
 
-            @pl.when(h == 1)
-            def _():
-                @pl.when(i >= 2)
+                @pl.when(i == 1)
                 def _():
-                    kv_3(i - 2, True)
+                    for c in others:
+                        over_chips(c, p.chip, turn(p, last)).start()
+                    chip_sum(1)
+                    reduce_step(1)
 
                 @pl.when(i == 2)
                 def _():
-                    chip_sum(2)
                     reduce_step(2)
-
-            @pl.when(h == 2)
-            def _():
-                @pl.when(i == 0)
-                def _():
-                    out_1()
-                    chip_sum(0)
-
-                @pl.when(i == 1)
-                def _():
-                    chip_sum(1)
-                    reduce_step(1)
-                    out_2()
-
-                @pl.when(i == 2)
-                def _():
-                    out_3()
 
                 @pl.when(i == 3)
                 def _():
@@ -1090,6 +1175,27 @@
                     reduce_step(3)
                     gather_first()
 
+            @pl.when((h == 1) & (i >= 2))
+            def _():
+                kv_3(i - 2, True)
+
+            @pl.when(h == 2)
+            def _():
+                @pl.when(i == 1)
+                def _():
+                    chip_sum(2)
+                    out_0()
+
+                @pl.when(i == 2)
+                def _():
+                    out_1()
+
+                @pl.when(i == last)
+                def _():
+                    for g in range(GROUPS):
+                        weight_x(g).wait_recv()
+                        weight_core(g, p.k).start()
+
             return carry
 
         lax.fori_loop(0, GH, head, 0)
@@ -1103,6 +1209,8 @@
         return carry
 
     lax.fori_loop(0, GROUPS, chunk, 0)
+    kv_2(3)
+    spread(p.a)
     kv_3(2, True)
     for d in range(1, GROUPS + 1):
         z = (p.a + d) % GROUPS
@@ -1111,24 +1219,31 @@
         gps[z, :, 128:256] = (jnp.where(low, dq3[2, at, :], 0.0) * SCALE).astype(BF16)
         if d < GROUPS:
             zq(p.a, z).start()
-    kv_2(3)
-    gather_step(1)
-    kv_3(3, False)
-    gpr[p.a] = gps[p.a]
-
-    gqb[...] = jnp.zeros_like(gqb)
-
-    def rowdot(z, carry):
+
+    def rows_of(i, core):
+        return pl.ds(pl.multiple_of(i * half + core * quarter, quarter), quarter)
+
+    for c in late:
+        c.wait()
+    for t in range(width // 256):
+        at = pl.ds(t * 256, 256)
+        gqb[at, 0:256] = dg(h1[p.a, :, at], gps[p.a, :, 0:256], TN)
+        gqb[at, 256:640] = jnp.zeros((256, 384), F32)
+
+    def rowdot(d, carry):
+        z = (p.a + d) % GROUPS
         for t in range(width // 256):
             at = pl.ds(t * 256, 256)
             gqb[at, :] += dg(h1[z, :, at], gps[z], TN)
         return carry
 
-    lax.fori_loop(0, GROUPS, rowdot, 0)
-
-    def rows_of(i, core):
-        return pl.ds(pl.multiple_of(i * half + core * quarter, quarter), quarter)
-
+    lax.fori_loop(1, GROUPS, rowdot, 0)
+    gather_step(1)
+    kv_3(3, False)
+    gpr[p.a] = gps[p.a]
+    for t in range(width // 256):
+        at = pl.ds(t * 256, 256)
+        gqb[at, 256:640] += dg(h1[p.a, :, at], gps[p.a, :, 256:640], TN)
     for i in range(2):
         qk[0, i] = gqb[rows_of(i, 1 - p.k), :].astype(BF16)
     q_k = rcopy(qk.at[0], qk.at[1], qs.at[0], qr.at[0], p.sibling())
@@ -1141,7 +1256,7 @@
     qx[0] = gqb[rows_of(1 - p.x, p.k), :].astype(BF16)
     q_x = rcopy(qx.at[0], qx.at[1], qs.at[1], qr.at[1], p.xpeer())
     q_x.start()
-    gather_step(2)
+    out_2()
     q_x.wait()
     gqb[rows_of(p.x, p.k), :] += qx[1].astype(F32)
     qy[p.chip] = gqb[rows_of(p.x, p.k), :].astype(BF16)
@@ -1151,8 +1266,11 @@
 
     for c in others:
         qc(c, p.chip).start()
-    for c in wx:
-        c.wait()
+    gather_step(2)
+    for g in range(GROUPS):
+        weight_core(g, 1 - p.k).wait_recv()
+        weight_core(g, p.k).wait_send()
+        weight_x(g).wait_send()
     h = dg(gpr[p.a], wfull[p.a], NT)
     for g in line:
         zkv(g, g).wait_recv()
@@ -1180,19 +1298,18 @@
         bc(p.a, p.a - 1, 1).start()
 
     sc(p.a, p.k).start()
+    out_3()
     u = ext_of(rp[...].astype(F32))
     inv = inv_rms(u)
     gain = jnp.concatenate([gfull[0, 0:1, :], gfull[1, 0:1, :]], axis=1)
     result = gmid[...] + crms_back(u, inv, gain, h)
-    gin[...] = result
+    gin[...] = result.T
     first = jnp.sum(h * (u * inv), axis=0, keepdims=True)
     which = lax.broadcasted_iota(jnp.int32, (8, width), 0)
     g0[...] = jnp.where(which == 0, first, dg2[...])
     g_k = rcopy(g0, gk, qs.at[2], qr.at[2], p.sibling())
     g_k.start()
     gather_step(3)
-    for z in range(GROUPS):
-        pass_on(z)
     g_k.wait()
     g0[...] += gk[...]
     g_x = rcopy(g0, gx, qs.at[3], qr.at[3], p.xpeer())
@@ -1232,6 +1349,8 @@
             for c in others:
                 gc(c, p.chip).start()
         if s == 2:
+            for z in range(GROUPS):
+                pass_on(z)
             for c in others:
                 gc(c, c).wait_recv()
             total = gy[0]
@@ -1266,8 +1385,9 @@
         for c in others:
             chip_share(p.chip, g, c).wait_send()
             yc(g, c, p.chip).wait_send()
-            over_chips(c, p.chip, g).wait_send()
     for c in others:
+        for j in range(1, GROUPS):
+            over_chips(c, p.chip, turn(p, j)).wait_send()
         qc(c, p.chip).wait_send()
         gc(c, p.chip).wait_send()
         out_chip(c, p.chip).wait_send()
@@ -1300,14 +1420,15 @@
                 leftward(p.a - s, red.at[0]).wait_send()
 
 
-def back(n, lens, q3, kv, o3, l3, dog, wg, h1, rp, gmid, gfull, dg2, ysum, go):
+def back(n, lens, q3, kv, o3, l3, dog, wg, h1, rp, gmid, gfull, dg2, ysum, y0, gb, att):
     rows, width = rp.shape
     quarter = width // 4
     lanes = wg.shape[2]
     chips = n // GROUPS // 2
     keys = kv.shape[0] // GROUPS
     piece = ysum.shape[2]
-    orow = go.shape[0] // 2
+    half = width // 2
+    orow = half // 2
     sds = jax.ShapeDtypeStruct
     v = pltpu.VMEM
     sem = lambda *shape: [DMA(shape), DMA(shape)]
@@ -1315,15 +1436,21 @@
         functools.partial(back_kernel, n),
         name="back",
         out_shape=(
-            sds((rows, width), F32),
+            sds((width, rows), F32),
             sds((GROUPS, 2, quarter, lanes), BF16),
             sds((8, width), F32),
             sds((2, chips, GROUPS, piece, width), BF16),
             sds((2, GROUPS, orow // GROUPS, width), BF16),
         ),
-        in_specs=[SM, VM, ANY, ANY, VM, VM, ANY] + [VM] * 5 + [ANY, VM],
+        in_specs=[SM, VM, ANY, ANY, VM, VM, ANY, ANY, ANY, ANY, VM, VM, ANY, VM, ANY, ANY],
         out_specs=[VM] * 5,
         scratch_shapes=[
+            v(h1.shape, BF16),
+            v(rp.shape, BF16),
+            v(gmid.shape, F32),
+            v((half, width), BF16),
+            v((2, rows, width), BF16),
+            v((2, 2) + att.shape[1:], BF16),
             v((GROUPS, piece, width), BF16),
             v((GROUPS, piece, width), BF16),
             v(ysum.shape, BF16),
@@ -1351,12 +1478,12 @@
             v((GROUPS, piece, width), BF16),
             v((GROUPS, piece, width), BF16),
             v((orow, width), BF16),
-            v((orow, width), BF16),
-            v((chips, orow, width), BF16),
+            v((orow // GROUPS, width), BF16),
+            v((chips, orow // GROUPS, width), BF16),
             v((GROUPS, orow // GROUPS, width), BF16),
             v((GROUPS, orow // GROUPS, width), BF16),
             *sem(GROUPS),
-            DMA((GROUPS + 2,)),
+            DMA((GROUPS + 7,)),
             DMA((2,)),
             *sem(GROUPS, chips),
             *sem(GROUPS + 1, chips),
@@ -1377,19 +1504,21 @@
             *sem(2 * GROUPS),
             *sem(1 + GROUPS),
             *sem(chips, GROUPS),
+            *sem(GROUPS),
+            *sem(2),
         ],
         compiler_params=pltpu.CompilerParams(
             collective_id=2, has_side_effects=True, vmem_limit_bytes=67043328
         ),
-    )(lens, q3, kv, o3, l3, dog, wg, h1, rp, gmid, gfull, dg2, ysum, go)
+    )(lens, q3, kv, o3, l3, dog, wg, h1, rp, gmid, gfull, dg2, ysum, y0, gb, att)
 
 
 def deliver_kernel(gq, ra, rb, rd, goo, gsum, gin, out, out_, gin_, g1_, qkv_, go_, g2_, up_, down_):
-    narrow = gin_.shape[2]
+    narrow = gin_.shape[0]
     half = g1_.shape[0]
     width = 2 * half
     out_[0] = out[:, :narrow]
-    gin_[0] = gin[:, :narrow]
+    gin_[:, 0, :] = gin[:narrow, :]
     go_[...] = goo[:, :narrow].astype(F32)
     down_[...] = rd[0, :, :narrow].astype(F32)
     up_[:, :width] = ra[0].astype(F32)
@@ -1424,7 +1553,7 @@
 
 
 def deliver(gq, res, goo, gsum, gin, out):
-    rows, width = gin.shape
+    width, rows = gin.shape
     half = width // 2
     ff = res.shape[1]
     steps = 4
@@ -1436,7 +1565,7 @@
         grid=(steps,),
         out_shape=(
             sds((1, rows, width - 1), BF16),
-            sds((1, rows, width - 1), F32),
+            sds((width - 1, 1, rows), F32),
             sds((half,), F32),
             sds((half, 3 * width), F32),
             sds((half, width - 1), F32),
@@ -1451,12 +1580,12 @@
             spec((1, ff // steps, width), lambda i: (1, i, 0)),
             spec((half // steps, width), lambda i: (i, 0)),
             spec(gsum.shape, lambda i: (0, 0)),
-            spec((rows // steps, width), lambda i: (i, 0)),
+            spec((width, rows), lambda i: (0, 0)),
             spec((rows // steps, width), lambda i: (i, 0)),
         ],
         out_specs=[
             spec((1, rows // steps, width - 1), lambda i: (0, i, 0)),
-            spec((1, rows // steps, width - 1), lambda i: (0, i, 0)),
+            spec((width - 1, 1, rows), lambda i: (0, 0, 0)),
             spec((half,), lambda i: (0,)),
             spec((half // steps, 3 * width), lambda i: (i, 0)),
             spec((half // steps, width - 1), lambda i: (i, 0)),
@@ -1471,17 +1600,18 @@
 def shards(n, resid, lengths, gain_one, w_qkv, w_out, gain_two, w_up, w_down, cotangent):
     width = resid.shape[2] + 1
     ff = w_up.shape[1]
-    out, gmid, ysum, go, dog, dg2, rp, wg, h1, q3, kv, o3, l3, gfull = front(
+    out, gmid, ysum, y0, gb, attg, dog, dg2, rp, wg, h1, q3, kv, o3, l3, gfull = front(
         n, lengths, resid[0], cotangent[0], gain_one, gain_two, w_qkv, w_out, w_up, w_down
     )
     gin, gq, gsum, res, goo = back(
-        n, lengths, q3, kv, o3, l3, dog, wg, h1, rp, gmid, gfull, dg2, ysum, go
+        n, lengths, q3, kv, o3, l3, dog, wg, h1, rp, gmid, gfull, dg2, ysum, y0, gb, attg
     )
 
     half = width // 2
-    return deliver(
+    delivered = deliver(
         gq.reshape(GROUPS, half, -1), res.reshape(2, ff, width), goo.reshape(half, width), gsum, gin, out
     )
+    return delivered[0], jnp.transpose(delivered[1], (1, 2, 0)), *delivered[2:]
 
 
 def solution(mesh):

time: 256 us -> 232 us (0.906)
  Pallas kernels: 252 us -> 230 us
  local copies, waits for them, and re-layouts: 3.02 us -> 0 us
    pallas_call x1, Pallas kernels: 142 us -> 124 us  [back(): pl.pallas_call(functools.partial(back_kernel, n), name='back', out_shape=...]
    pallas_call x1 -> x0, local copies, waits for them, and re-layouts: 3.02 us -> none  [deliver(): pl.pallas_call(deliver_kernel, name='deliver', grid=(steps,), out_shape=(...]
    pallas_call x1, Pallas kernels: 100 us -> 97 us  [front(): pl.pallas_call(functools.partial(front_kernel, n), name='front', out_shap...]
where the time goes in v4:
time: 232 us
  Pallas kernels  230 us (99%)
    pallas_call x1, Pallas kernels, back(): pl.pallas_call(functools.partial(back_kernel, n), name='back', out_shape=...  124 us
    pallas_call x1, Pallas kernels, front(): pl.pallas_call(functools.partial(front_kernel, n), name='front', out_shap...  97 us
    pallas_call x1, Pallas kernels, deliver(): pl.pallas_call(deliver_kernel, name='deliver', grid=(steps,), out_shape=(...  9.49 us

profile of v4, /device:TPU:0, one launch (start us, length us, event | category | flops | bytes accessed | tf_op | source)
XLA Modules:
  0.0 231.5 jit_solution(8806731251647716154)
XLA Ops:
  1.3 97.0 %front.1 = (bf16[256,768]{1,0:T(8,128)(2,1)}, f32[256,768]{1,0:T(8,128)}, bf16[2,4,192,768]{3,2,1,0:T(8,128)(2,1)}, bf16[2,192,768]{2,1,0:T(8,128)(2,1)}, bf16[2...) custom-call(s32[1]{0:T(128)S(6)} %copy.17.lens, ...), custom_call_target="tpu_custom_call" | custom-call | tf_op jit(solution)/shard_map/front/pallas_call | solution.py:703
  98.3 123.6 %back.1 = (f32[768,256]{1,0:T(8,128)}, bf16[4,2,192,640]{3,2,1,0:T(8,128)(2,1)}, f32[8,768]{1,0:T(8,128)}, bf16[2,2,4,192,768]{4,3,2,1,0:T(8,128)(2,1)}, bf16[2,4,48,768]{3,2,1,0:T(8,128)(2,1)}) custom-call(s32[1]{0:T(128)S(6)} %copy.17.lens, bf16[3,1024,128]{2,1,0:T(8,128)(2,1)} %get-tuple-element.37.q3, bf16[4096,384]{1,0:T(8,128)(2,1)} %get-tuple-element.38.kv, ...), custom_call_target="tpu_custom_call" | custom-call | tf_op jit(solution)/shard_map/back/pallas_call | solution.py:1435
  221.9 9.5 %deliver.1 = (bf16[1,256,767]{2,1,0:T(8,128)(2,1)}, f32[767,1,256]{2,1,0:T(1,128)}, f32[384]{0:T(512)}, f32[384,2304]{1,0:T(8,128)}, f32[384,767]{1,0:T(8,128)},...) custom-call(bf16[4,384,640]{2,1,0:T(8,128)(2,1)} %bitcast.9, bf16[2,1536,768]{2,1,0:T(8,128)(2,1)} %bitcast.6, ...), custom_call_target="tpu_custom_call" | custom-call | tf_op jit(solution)/shard_map/deliver/pallas_call | solution.py:1562

commit v5 on v4

--- a/solution.py
+++ b/solution.py
@@ -777,9 +777,9 @@
     n, lens, q3, kv, o3, l3, dog, wg, h1_, rp_, gmid_, gfull, dg2, ysum, y0, gb_, att_,
     gin, gq, gains, res, goo,
     h1, rp, gmid, go, gb, att, red, ymine, yq, do3, dq3, kvc, dkv, dkvb, rk, ry, wfull, gps, gpr, gqb, qk, qx, qy,
-    g0, gk, gx, gy, ga, left, right, sumr, suml, ok, os_, oy, oz, ozr,
+    qs_, qz_, qr_, g0, gk, gx, gy, ga, left, right, sumr, suml, ok, os_, oy, oz, ozr,
     xs, xr, ls, vs, ks, kr, ys, yr, zs, zr, ws, wr, qs, qr, ns, nr, bs, br, cs, cr,
-    rs_, rr, ls_, lr, as_, ar, es, er, fs, fr, ts, tr, us, ur, is_, ir, ps, pr, ws2, wr2, zs2, zr2,
+    rs_, rr, ls_, lr, as_, ar, es, er, fs, fr, ts, tr, us, ur, is_, ir, ps, pr, ws2, wr2, zs2, zr2, vs2, vr2, fs2, fr2,
 ):
     p = Place(n)
     rows, width = rp_.shape
@@ -934,7 +934,13 @@
             def _():
                 line_share(p.a - s, p.a + 1, 2 * s).start()
 
-            spread(p.a - s)
+            if s > 1:
+                spread(p.a - s)
+            else:
+
+                @pl.when(p.a == last)
+                def _():
+                    spread(p.a - s)
 
         @pl.when(p.a + s <= last)
         def _():
@@ -952,25 +958,33 @@
             core_share(p.k, c, z).start()
 
     orow = half // 2
-    opart = orow // GROUPS
+    oc = os_.shape[0]
+    oyrow = orow // oc
+    opart = oyrow // GROUPS
+    my = p.chip if oc > 1 else 0
 
     def out_core():
         at = pl.ds(pl.multiple_of((1 - p.k) * orow, orow), orow)
         return rcopy(go.at[at], ok, is_.at[0], ir.at[0], p.sibling())
 
+    def out_chip(chip, slot):
+        return rcopy(os_.at[chip if oc > 1 else 0], oy.at[slot], ts.at[chip], tr.at[slot], p.on_chip(chip))
+
     def out_line(slot, to):
         return rcopy(oz.at[to], ozr.at[slot], us.at[to], ur.at[slot], p.on_line(to))
 
-    def out_chip(chip, slot):
-        return rcopy(os_, oy.at[slot], ts.at[chip], tr.at[slot], p.on_chip(chip))
-
     def out_back(slot, to):
-        r = goo.at[p.k, slot]
+        r = goo.at[p.k, my, slot]
         return rcopy(r, r, us.at[GROUPS + to], ur.at[GROUPS + slot], p.on_line(to))
 
-    def out_share(core, z):
-        r = goo.at[core, z]
-        return rcopy(r, r, is_.at[1 + z], ir.at[1 + z], p.sibling())
+    def out_spread(chip, z, to):
+        r = goo.at[p.k, chip, z]
+        return rcopy(r, r, fs2.at[z, to], fr2.at[z, chip], p.on_chip(to))
+
+    def out_share(core, chip, z):
+        r = goo.at[core, chip, z]
+        i = 1 + chip * GROUPS + z
+        return rcopy(r, r, is_.at[i], ir.at[i], p.sibling())
 
     def out_0():
         for c in gos + gox:
@@ -987,29 +1001,38 @@
         out_core().wait()
         at = pl.ds(pl.multiple_of(p.k * orow, orow), orow)
         total = go[at, :].astype(F32) + ok[...].astype(F32)
+        for c in range(oc):
+            os_[c] = total[c * oyrow : (c + 1) * oyrow].astype(BF16)
+        for c in others:
+            out_chip(c, p.chip).start()
+
+    def out_2():
+        total = os_[my].astype(F32)
+        for c in others:
+            out_chip(c, c).wait_recv()
+            total = total + oy[c].astype(F32)
         for z in range(GROUPS):
             oz[z] = total[z * opart : (z + 1) * opart].astype(BF16)
         for z in line:
             out_line(p.a, z).start()
 
-    def out_2():
+    def out_3():
         total = oz[p.a].astype(F32)
         for z in line:
             out_line(z, z).wait_recv()
             total = total + ozr[z].astype(F32)
-        os_[...] = total.astype(BF16)
-        for c in others:
-            out_chip(c, p.chip).start()
-
-    def out_3():
-        total = os_[...].astype(F32)
-        for c in others:
-            out_chip(c, c).wait_recv()
-            total = total + oy[c].astype(F32)
-        goo[p.k, p.a] = total.astype(BF16)
+        goo[p.k, my, p.a] = total.astype(BF16)
         for z in line:
             out_back(p.a, z).start()
-        out_share(p.k, p.a).start()
+
+    def out_4():
+        for z in line:
+            out_back(z, z).wait_recv()
+        for z in range(GROUPS):
+            if oc > 1:
+                for c in others:
+                    out_spread(p.chip, z, c).start()
+            out_share(p.k, my, z).start()
 
     def kc(i, chip):
         c = chunk_of(i)
@@ -1028,10 +1051,7 @@
         )
 
     def zq(slot, to):
-        lanes = pl.ds(0, 256)
-        return rcopy(
-            gps.at[to, :, lanes], gpr.at[slot, :, lanes], ws.at[to], wr.at[slot], p.on_line(to)
-        )
+        return rcopy(qz_.at[to], qr_.at[slot], ws.at[to], wr.at[slot], p.on_line(to))
 
     def mine(chip):
         at = pl.ds(pl.multiple_of((chip * 2 + p.k) * rows, rows), rows)
@@ -1216,9 +1236,14 @@
         z = (p.a + d) % GROUPS
         at = pl.ds(pl.multiple_of(z * rows, rows), rows)
         gps[z, :, 0:128] = (jnp.where(low, dq3[0, at, :], dq3[1, at, :]) * SCALE).astype(BF16)
-        gps[z, :, 128:256] = (jnp.where(low, dq3[2, at, :], 0.0) * SCALE).astype(BF16)
+        third = (jnp.where(low, dq3[2, at, :], 0.0) * SCALE).astype(BF16)
+        gps[z, :, 128:256] = third
         if d < GROUPS:
+            qz_[z, 0:rows, :] = gps[z, :, 0:128]
+            bottom = pltpu.roll(third[rows // 2 :], HD, 1)
+            qz_[z, rows:, :] = jnp.where(low[: rows // 2], third[: rows // 2], bottom)
             zq(p.a, z).start()
+    out_2()
 
     def rows_of(i, core):
         return pl.ds(pl.multiple_of(i * half + core * quarter, quarter), quarter)
@@ -1253,20 +1278,62 @@
     q_k.wait()
     for i in range(2):
         gqb[rows_of(i, p.k), :] += qk[1, i].astype(F32)
-    qx[0] = gqb[rows_of(1 - p.x, p.k), :].astype(BF16)
-    q_x = rcopy(qx.at[0], qx.at[1], qs.at[1], qr.at[1], p.xpeer())
+    qk[0, 0] = gqb[rows_of(1 - p.x, p.k), :].astype(BF16)
+    q_x = rcopy(qk.at[0, 0], qx, qs.at[1], qr.at[1], p.xpeer())
     q_x.start()
-    out_2()
     q_x.wait()
-    gqb[rows_of(p.x, p.k), :] += qx[1].astype(F32)
-    qy[p.chip] = gqb[rows_of(p.x, p.k), :].astype(BF16)
+    gqb[rows_of(p.x, p.k), :] += qx[...].astype(F32)
+    share = quarter // p.chips
+
+    def own_rows(chip):
+        start = p.x * half + p.k * quarter + chip * share
+        return pl.ds(pl.multiple_of(start, share), share)
 
     def qc(chip, slot):
-        return rcopy(qy.at[p.chip], qy.at[slot], ns.at[chip], nr.at[slot], p.on_chip(chip))
+        return rcopy(qs_.at[chip], qy.at[slot], ns.at[chip], nr.at[slot], p.on_chip(chip))
 
     for c in others:
+        qs_[c] = gqb[own_rows(c), :].astype(BF16)
         qc(c, p.chip).start()
+
+    @pl.when((p.a > 0) & (p.a < last))
+    def _():
+        spread(p.a - 1)
+
+    out_3()
     gather_step(2)
+    total = gqb[own_rows(p.chip), :]
+    for c in others:
+        qc(c, c).wait_recv()
+        total = total + qy[c].astype(F32)
+    gq[p.a, p.k, p.chip] = total.astype(BF16)
+
+    def bc(slot, to, sem):
+        r = gq.at[slot, p.k, p.chip]
+        return rcopy(r, r, bs.at[sem], br.at[slot], p.on_line(to))
+
+    def qshare(slot, chip, to):
+        r = gq.at[slot, p.k, chip]
+        return rcopy(r, r, vs2.at[slot, to], vr2.at[slot, chip], p.on_chip(to))
+
+    def sc(slot, core, chip):
+        r = gq.at[slot, core, chip]
+        return rcopy(r, r, cs.at[slot, chip], cr.at[slot, chip], p.sibling())
+
+    def qspread(slot):
+        for c in others:
+            qshare(slot, p.chip, c).start()
+        sc(slot, p.k, p.chip).start()
+
+    @pl.when(p.a < last)
+    def _():
+        bc(p.a, p.a + 1, 0).start()
+
+    @pl.when(p.a > 0)
+    def _():
+        bc(p.a, p.a - 1, 1).start()
+
+    qspread(p.a)
     for g in range(GROUPS):
         weight_core(g, 1 - p.k).wait_recv()
         weight_core(g, p.k).wait_send()
@@ -1275,30 +1342,14 @@
     for g in line:
         zkv(g, g).wait_recv()
         zq(g, g).wait_recv()
+        gpr[g, :, 0:128] = qr_[g, 0:rows, :]
+        t = qr_[g, rows:, :]
+        zero = jnp.zeros_like(t)
+        at_low = low_half(t.shape)
+        gpr[g, 0 : rows // 2, 128:256] = jnp.where(at_low, t, zero)
+        gpr[g, rows // 2 :, 128:256] = jnp.where(at_low, pltpu.roll(t, HD, 1), zero)
         h = h + dg(gpr[g], wfull[g], NT)
-    total = gqb[rows_of(p.x, p.k), :]
-    for c in others:
-        qc(c, c).wait_recv()
-        total = total + qy[c].astype(F32)
-    gq[p.a, p.k] = total.astype(BF16)
-
-    def bc(slot, to, sem):
-        r = gq.at[slot, p.k]
-        return rcopy(r, r, bs.at[sem], br.at[slot], p.on_line(to))
-
-    def sc(slot, core):
-        return rcopy(gq.at[slot, core], gq.at[slot, core], cs.at[slot], cr.at[slot], p.sibling())
-
-    @pl.when(p.a < last)
-    def _():
-        bc(p.a, p.a + 1, 0).start()
-
-    @pl.when(p.a > 0)
-    def _():
-        bc(p.a, p.a - 1, 1).start()
-
-    sc(p.a, p.k).start()
-    out_3()
+    out_4()
     u = ext_of(rp[...].astype(F32))
     inv = inv_rms(u)
     gain = jnp.concatenate([gfull[0, 0:1, :], gfull[1, 0:1, :]], axis=1)
@@ -1324,7 +1375,7 @@
             def _():
                 bc(p.a - s, p.a + 1, 2 * s).start()
 
-            sc(p.a - s, p.k).start()
+            qspread(p.a - s)
 
         @pl.when(p.a + s <= last)
         def _():
@@ -1334,7 +1385,7 @@
             def _():
                 bc(p.a + s, p.a - 1, 2 * s + 1).start()
 
-            sc(p.a + s, p.k).start()
+            qspread(p.a + s)
 
         if s == 1:
             g_x.wait()
@@ -1371,14 +1422,26 @@
     for g in range(1, GROUPS):
         total = total + ga[g]
     gains[...] = total
-    for g in line:
-        out_back(g, g).wait_recv()
-        out_share(p.k, g).start()
+    for c in others:
+        if oc > 1:
+            for g in range(GROUPS):
+                out_spread(c, g, c).wait_recv()
+                out_share(p.k, c, g).start()
+    for g in [p.a] + line:
+        for c in others:
+            qshare(g, c, c).wait_recv()
+            sc(g, p.k, c).start()
     for g in range(GROUPS):
-        sc(g, 1 - p.k).wait_recv()
-        sc(g, p.k).wait_send()
-        out_share(1 - p.k, g).wait_recv()
-        out_share(p.k, g).wait_send()
+        for c in range(p.chips):
+            sc(g, 1 - p.k, c).wait_recv()
+            sc(g, p.k, c).wait_send()
+        for c in others:
+            qshare(g, p.chip, c).wait_send()
+            if oc > 1:
+                out_spread(p.chip, g, c).wait_send()
+        for c in range(oc):
+            out_share(1 - p.k, c, g).wait_recv()
+            out_share(p.k, c, g).wait_send()
         for c in range(p.chips):
             core_share(1 - p.k, c, g).wait_recv()
             core_share(p.k, c, g).wait_send()
@@ -1429,6 +1492,8 @@
     piece = ysum.shape[2]
     half = width // 2
     orow = half // 2
+    oc = chips if orow % (chips * GROUPS * 8) == 0 else 1
+    oyrow = orow // oc
     sds = jax.ShapeDtypeStruct
     v = pltpu.VMEM
     sem = lambda *shape: [DMA(shape), DMA(shape)]
@@ -1437,10 +1502,10 @@
         name="back",
         out_shape=(
             sds((width, rows), F32),
-            sds((GROUPS, 2, quarter, lanes), BF16),
+            sds((GROUPS, 2, chips, quarter // chips, lanes), BF16),
             sds((8, width), F32),
             sds((2, chips, GROUPS, piece, width), BF16),
-            sds((2, GROUPS, orow // GROUPS, width), BF16),
+            sds((2, oc, GROUPS, oyrow // GROUPS, width), BF16),
         ),
         in_specs=[SM, VM, ANY, ANY, VM, VM, ANY, ANY, ANY, ANY, VM, VM, ANY, VM, ANY, ANY],
         out_specs=[VM] * 5,
@@ -1466,8 +1531,11 @@
             v((GROUPS, rows, lanes), BF16),
             v((width, lanes), F32),
             v((2, 2, quarter, lanes), BF16),
-            v((2, quarter, lanes), BF16),
-            v((chips, quarter, lanes), BF16),
+            v((quarter, lanes), BF16),
+            v((chips, quarter // chips, lanes), BF16),
+            v((chips, quarter // chips, lanes), BF16),
+            v((GROUPS, rows * 3 // 2, 128), BF16),
+            v((GROUPS, rows * 3 // 2, 128), BF16),
             v((8, width), F32),
             v((8, width), F32),
             v((8, width), F32),
@@ -1478,10 +1546,10 @@
             v((GROUPS, piece, width), BF16),
             v((GROUPS, piece, width), BF16),
             v((orow, width), BF16),
-            v((orow // GROUPS, width), BF16),
-            v((chips, orow // GROUPS, width), BF16),
-            v((GROUPS, orow // GROUPS, width), BF16),
-            v((GROUPS, orow // GROUPS, width), BF16),
+            v((oc, oyrow, width), BF16),
+            v((chips, oyrow, width), BF16),
+            v((GROUPS, oyrow // GROUPS, width), BF16),
+            v((GROUPS, oyrow // GROUPS, width), BF16),
             *sem(GROUPS),
             DMA((GROUPS + 7,)),
             DMA((2,)),
@@ -1493,7 +1561,7 @@
             *sem(chips),
             DMA((2 * GROUPS,)),
             DMA((GROUPS,)),
-            *sem(GROUPS),
+            *sem(GROUPS, chips),
             *sem(GROUPS),
             *sem(GROUPS),
             DMA((2 * GROUPS,)),
@@ -1502,10 +1570,12 @@
             *sem(chips, GROUPS),
             *sem(chips),
             *sem(2 * GROUPS),
-            *sem(1 + GROUPS),
+            *sem(1 + chips * GROUPS),
             *sem(chips, GROUPS),
             *sem(GROUPS),
             *sem(2),
+            *sem(GROUPS, chips),
+            *sem(GROUPS, chips),
         ],
         compiler_params=pltpu.CompilerParams(
             collective_id=2, has_side_effects=True, vmem_limit_bytes=67043328

time: 232 us -> 223 us (0.961)
  Pallas kernels: 230 us -> 221 us
    pallas_call x1, Pallas kernels: 124 us -> 115 us  [back(): pl.pallas_call(functools.partial(back_kernel, n), name='back', out_shape=...]
where the time goes in v5:
time: 223 us
  Pallas kernels  221 us (99%)
    pallas_call x1, Pallas kernels, back(): pl.pallas_call(functools.partial(back_kernel, n), name='back', out_shape=...  115 us
    pallas_call x1, Pallas kernels, front(): pl.pallas_call(functools.partial(front_kernel, n), name='front', out_shap...  97 us
    pallas_call x1, Pallas kernels, deliver(): pl.pallas_call(deliver_kernel, name='deliver', grid=(steps,), out_shape=(...  9.49 us

profile of v5, /device:TPU:0, one launch (start us, length us, event | category | flops | bytes accessed | tf_op | source)
XLA Modules:
  0.0 222.9 jit_solution(11676607155542817691)
XLA Ops:
  1.3 97.0 %front.1 = (bf16[256,768]{1,0:T(8,128)(2,1)}, f32[256,768]{1,0:T(8,128)}, bf16[2,4,192,768]{3,2,1,0:T(8,128)(2,1)}, bf16[2,192,768]{2,1,0:T(8,128)(2,1)}, bf16[2...) custom-call(s32[1]{0:T(128)S(6)} %copy.17.lens, ...), custom_call_target="tpu_custom_call" | custom-call | tf_op jit(solution)/shard_map/front/pallas_call | solution.py:703
  98.3 115.0 %back.1 = (f32[768,256]{1,0:T(8,128)}, bf16[4,2,2,96,640]{4,3,2,1,0:T(8,128)(2,1)}, f32[8,768]{1,0:T(8,128)}, bf16[2,2,4,192,768]{4,3,2,1,0:T(8,128)(2,1)}, bf16[2,2,4,24,768]{4,3,2,1,0:T(8,128)(2,1)}) custom-call(s32[1]{0:T(128)S(6)} %copy.17.lens, bf16[3,1024,128]{2,1,0:T(8,128)(2,1)} %get-tuple-element.37.q3, bf16[4096,384]{1,0:T(8,128)(2,1)} %get-tuple-element.38.kv, ...), custom_call_target="tpu_custom_call" | custom-call | tf_op jit(solution)/shard_map/back/pallas_call | solution.py:1500
  213.3 9.5 %deliver.1 = (bf16[1,256,767]{2,1,0:T(8,128)(2,1)}, f32[767,1,256]{2,1,0:T(1,128)}, f32[384]{0:T(512)}, f32[384,2304]{1,0:T(8,128)}, f32[384,767]{1,0:T(8,128)},...) custom-call(bf16[4,384,640]{2,1,0:T(8,128)(2,1)} %bitcast.9, bf16[2,1536,768]{2,1,0:T(8,128)(2,1)} %bitcast.6, ...), custom_call_target="tpu_custom_call" | custom-call | tf_op jit(solution)/shard_map/deliver/pallas_call | solution.py:1632

commit v6 on v5

--- a/solution.py
+++ b/solution.py
@@ -175,7 +175,7 @@
 def front_kernel(
     n, lens, ri, ci, g1, g2, wq, wo, wuh, wdh,
     out, gmid_, ysum_, y0, gb_, attg, dog, dg2, rp_, wg_, h1_, q3_, kv_, o3_, l3_, gfull,
-    gmid, ysum, rp, wg, h1, q3, kv, o3, l3, gains, wop, wa, woa, wu, wdr, wd, att, wide, hid, gmb, act, gpre, esum, dsend, gb, mid, gk,
+    gmid, ysum, rp, wg, h1, q3, kv, o3, l3, gains, wop, wa, woa, wu, wdr, wd, att, wide, hid, gmb, act, gpre, esum, dsend, gb, mid, gk, grads,
     ss, rs, ls, hs, hr, vs, kr, fs, xs, xr, cs, cr, ts, tr, as_, ar, ds_, dr, ks, ks_r, ys, yr, us,
 ):
     p = Place(n)
@@ -526,16 +526,17 @@
     x_hid = xc(9, hid.at[0], hid.at[1])
     x_hid.start()
     tiles = ff // 256
+    wide_tile = 512
 
     def up(slot, token, f):
         def tile(t, carry):
-            at = pl.ds(pl.multiple_of(t * 256, 256), 256)
+            at = pl.ds(pl.multiple_of(t * wide_tile, wide_tile), wide_tile)
             a, slope = gelu_both(dot(hid[token], wu[f, :, at]))
             act[slot, :, at] = a.astype(BF16)
             gpre[slot, :, at] = (slope * dg(gmb[token], wd[f, at, :], NT)).astype(BF16)
             return carry
 
-        lax.fori_loop(0, tiles, tile, 0)
+        lax.fori_loop(0, ff // wide_tile, tile, 0)
 
     up(0, 0, p.x)
     for c in others:
@@ -581,10 +582,15 @@
     x_gm.wait()
     x_hid.wait()
     up(1, 1, p.x)
-    final = mid[...] + dot(act[0], wd[p.x]) + dot(act[2], wd[other])
-    out[...] = final.astype(BF16)
-
-    gm = wd
+
+    def finish_out():
+        final = mid[...] + dot(act[0], wd[p.x]) + dot(act[2], wd[other])
+        out[...] = final.astype(BF16)
+
+    shared = grads.shape != wd.shape
+    gm = wd if shared else grads
+    if shared:
+        finish_out()
     piece = ysum.shape[2]
     part = GROUPS * piece
 
@@ -638,6 +644,8 @@
         kc(chip).wait()
         core_sum(chip, turn(p, 0))
         over_chips(chip, p.chip).start()
+    if not shared:
+        finish_out()
     for j in range(1, GROUPS):
         for chip in others:
             core_sum(chip, turn(p, j))
@@ -751,6 +759,7 @@
             v((rows, width), BF16),
             v((rows, width), F32),
             v((ff, width), BF16),
+            v((2, ff, width) if m * rows <= SUB else (8, 128), BF16),
             *sem(10),
             DMA((7,)),
             DMA((2 * GROUPS,)),
@@ -774,9 +783,9 @@
 
 
 def back_kernel(
-    n, lens, q3, kv, o3, l3, dog, wg, h1_, rp_, gmid_, gfull, dg2, ysum, y0, gb_, att_,
-    gin, gq, gains, res, goo,
-    h1, rp, gmid, go, gb, att, red, ymine, yq, do3, dq3, kvc, dkv, dkvb, rk, ry, wfull, gps, gpr, gqb, qk, qx, qy,
+    n, lens, q3_, kv, o3, l3_, dog_, wg, h1_, rp_, gmid_, gfull, dg2, ysum, y0, gb_, att_,
+    gin, gq, gains, res_, goo,
+    q3, l3, dog, res, h1, rp, gmid, go, gb, att, red, ymine, yq, do3, dq3, kvc, dkv, dkvb, rk, ry, wfull, gps, gpr, gqb, qk, qx, qy,
     qs_, qz_, qr_, g0, gk, gx, gy, ga, left, right, sumr, suml, ok, os_, oy, oz, ozr,
     xs, xr, ls, vs, ks, kr, ys, yr, zs, zr, ws, wr, qs, qr, ns, nr, bs, br, cs, cr,
     rs_, rr, ls_, lr, as_, ar, es, er, fs, fr, ts, tr, us, ur, is_, ir, ps, pr, ws2, wr2, zs2, zr2, vs2, vr2, fs2, fr2,
@@ -806,6 +815,12 @@
         src = kv.at[pl.ds(pl.multiple_of(c * keys, keys), keys)]
         return pltpu.make_async_copy(src, kvc.at[i % slots], vs.at[i % slots])
 
+    first_in = [
+        pltpu.make_async_copy(src, dst, ls.at[GROUPS + 7 + i])
+        for i, (src, dst) in enumerate(((dog_, dog), (q3_, q3), (l3_, l3)))
+    ]
+    for c in first_in:
+        c.start()
     fetch(0).start()
     o_in = pltpu.make_async_copy(o3, dq3, ls.at[GROUPS])
     o_in.start()
@@ -1093,6 +1108,8 @@
 
     first_query = p.b * rows
     low = low_half((rows, 128))
+    for c in first_in:
+        c.wait()
     o_in.wait()
     y_in.wait()
     chip_sum(0)
@@ -1206,10 +1223,6 @@
                     chip_sum(2)
                     out_0()
 
-                @pl.when(i == 2)
-                def _():
-                    out_1()
-
                 @pl.when(i == last)
                 def _():
                     for g in range(GROUPS):
@@ -1231,7 +1244,7 @@
     lax.fori_loop(0, GROUPS, chunk, 0)
     kv_2(3)
     spread(p.a)
-    kv_3(2, True)
+    out_1()
     for d in range(1, GROUPS + 1):
         z = (p.a + d) % GROUPS
         at = pl.ds(pl.multiple_of(z * rows, rows), rows)
@@ -1243,7 +1256,7 @@
             bottom = pltpu.roll(third[rows // 2 :], HD, 1)
             qz_[z, rows:, :] = jnp.where(low[: rows // 2], third[: rows // 2], bottom)
             zq(p.a, z).start()
-    out_2()
+    kv_3(2, True)
 
     def rows_of(i, core):
         return pl.ds(pl.multiple_of(i * half + core * quarter, quarter), quarter)
@@ -1263,7 +1276,6 @@
         return carry
 
     lax.fori_loop(1, GROUPS, rowdot, 0)
-    gather_step(1)
     kv_3(3, False)
     gpr[p.a] = gps[p.a]
     for t in range(width // 256):
@@ -1273,6 +1285,7 @@
         qk[0, i] = gqb[rows_of(i, 1 - p.k), :].astype(BF16)
     q_k = rcopy(qk.at[0], qk.at[1], qs.at[0], qr.at[0], p.sibling())
     q_k.start()
+    gather_step(1)
     for c in local:
         c.wait()
     q_k.wait()
@@ -1281,6 +1294,7 @@
     qk[0, 0] = gqb[rows_of(1 - p.x, p.k), :].astype(BF16)
     q_x = rcopy(qk.at[0, 0], qx, qs.at[1], qr.at[1], p.xpeer())
     q_x.start()
+    out_2()
     q_x.wait()
     gqb[rows_of(p.x, p.k), :] += qx[...].astype(F32)
     share = quarter // p.chips
@@ -1300,7 +1314,6 @@
     def _():
         spread(p.a - 1)
 
-    out_3()
     gather_step(2)
     total = gqb[own_rows(p.chip), :]
     for c in others:
@@ -1349,7 +1362,7 @@
         gpr[g, 0 : rows // 2, 128:256] = jnp.where(at_low, t, zero)
         gpr[g, rows // 2 :, 128:256] = jnp.where(at_low, pltpu.roll(t, HD, 1), zero)
         h = h + dg(gpr[g], wfull[g], NT)
-    out_4()
+    out_3()
     u = ext_of(rp[...].astype(F32))
     inv = inv_rms(u)
     gain = jnp.concatenate([gfull[0, 0:1, :], gfull[1, 0:1, :]], axis=1)
@@ -1388,6 +1401,7 @@
             qspread(p.a + s)
 
         if s == 1:
+            out_4()
             g_x.wait()
             gy[p.chip] = g0[...] + gx[...]
 
@@ -1416,6 +1430,11 @@
 
             for g in line:
                 lc(p.a, g).start()
+    for g in range(GROUPS):
+        for c in range(p.chips):
+            core_share(1 - p.k, c, g).wait_recv()
+    res_out = pltpu.make_async_copy(res, res_, ls.at[0])
+    res_out.start()
     for g in line:
         lc(g, g).wait_recv()
     total = ga[0]
@@ -1443,7 +1462,6 @@
             out_share(1 - p.k, c, g).wait_recv()
             out_share(p.k, c, g).wait_send()
         for c in range(p.chips):
-            core_share(1 - p.k, c, g).wait_recv()
             core_share(p.k, c, g).wait_send()
         for c in others:
             chip_share(p.chip, g, c).wait_send()
@@ -1481,6 +1499,8 @@
             @pl.when(p.a - s >= 0)
             def _():
                 leftward(p.a - s, red.at[0]).wait_send()
+
+    res_out.wait()
 
 
 def back(n, lens, q3, kv, o3, l3, dog, wg, h1, rp, gmid, gfull, dg2, ysum, y0, gb, att):
@@ -1507,9 +1527,13 @@
             sds((2, chips, GROUPS, piece, width), BF16),
             sds((2, oc, GROUPS, oyrow // GROUPS, width), BF16),
         ),
-        in_specs=[SM, VM, ANY, ANY, VM, VM, ANY, ANY, ANY, ANY, VM, VM, ANY, VM, ANY, ANY],
-        out_specs=[VM] * 5,
+        in_specs=[SM, ANY, ANY, ANY, ANY, ANY, ANY, ANY, ANY, ANY, VM, VM, ANY, VM, ANY, ANY],
+        out_specs=[VM, VM, VM, ANY, VM],
         scratch_shapes=[
+            v(q3.shape, BF16),
+            v(l3.shape, F32),
+            v(dog.shape, BF16),
+            v((2, chips, GROUPS, piece, width), BF16),
             v(h1.shape, BF16),
             v(rp.shape, BF16),
             v(gmid.shape, F32),
@@ -1551,7 +1575,7 @@
             v((GROUPS, oyrow // GROUPS, width), BF16),
             v((GROUPS, oyrow // GROUPS, width), BF16),
             *sem(GROUPS),
-            DMA((GROUPS + 7,)),
+            DMA((GROUPS + 10,)),
             DMA((2,)),
             *sem(GROUPS, chips),
             *sem(GROUPS + 1, chips),
@@ -1588,7 +1612,11 @@
     half = g1_.shape[0]
     width = 2 * half
     out_[0] = out[:, :narrow]
-    gin_[:, 0, :] = gin[:narrow, :]
+
+    @pl.when(pl.program_id(0) == 0)
+    def _():
+        gin_[:, 0, :] = gin[:narrow, :]
+
     go_[...] = goo[:, :narrow].astype(F32)
     down_[...] = rd[0, :, :narrow].astype(F32)
     up_[:, :width] = ra[0].astype(F32)
@@ -1626,7 +1654,7 @@
     width, rows = gin.shape
     half = width // 2
     ff = res.shape[1]
-    steps = 4
+    steps = 2
     sds = jax.ShapeDtypeStruct
     spec = pl.BlockSpec
     return pl.pallas_call(

time: 223 us -> 216 us (0.969)
  Pallas kernels: 221 us -> 215 us
    pallas_call x1, Pallas kernels: 115 us -> 112 us  [back(): pl.pallas_call(functools.partial(back_kernel, n), name='back', out_shape=...]
where the time goes in v6:
time: 216 us
  Pallas kernels  215 us (100%)
    pallas_call x1, Pallas kernels, back(): pl.pallas_call(functools.partial(back_kernel, n), name='back', out_shape=...  112 us
    pallas_call x1, Pallas kernels, front(): pl.pallas_call(functools.partial(front_kernel, n), name='front', out_shap...  94.8 us
    pallas_call x1, Pallas kernels, deliver(): pl.pallas_call(deliver_kernel, name='deliver', grid=(steps,), out_shape=(...  8.3 us

profile of v6, /device:TPU:0, one launch (start us, length us, event | category | flops | bytes accessed | tf_op | source)
XLA Modules:
  0.0 216.2 jit_solution(6406188660644791389)
XLA Ops:
  1.3 94.8 %front.1 = (bf16[256,768]{1,0:T(8,128)(2,1)}, f32[256,768]{1,0:T(8,128)}, bf16[2,4,192,768]{3,2,1,0:T(8,128)(2,1)}, bf16[2,192,768]{2,1,0:T(8,128)(2,1)}, bf16[2...) custom-call(s32[1]{0:T(128)S(6)} %copy.17.lens, ...), custom_call_target="tpu_custom_call" | custom-call | tf_op jit(solution)/shard_map/front/pallas_call | solution.py:711
  96.1 111.6 %back.1 = (f32[768,256]{1,0:T(8,128)}, bf16[4,2,2,96,640]{4,3,2,1,0:T(8,128)(2,1)}, f32[8,768]{1,0:T(8,128)}, bf16[2,2,4,192,768]{4,3,2,1,0:T(8,128)(2,1)}, bf16[2,2,4,24,768]{4,3,2,1,0:T(8,128)(2,1)}) custom-call(s32[1]{0:T(128)S(6)} %copy.17.lens, bf16[3,1024,128]{2,1,0:T(8,128)(2,1)} %get-tuple-element.37.q3_, bf16[4096,384]{1,0:T(8,128)(2,1)} %get-tuple-element.38.kv, ...), custom_call_target="tpu_custom_call" | custom-call | tf_op jit(solution)/shard_map/back/pallas_call | solution.py:1520
  207.7 8.3 %deliver.1 = (bf16[1,256,767]{2,1,0:T(8,128)(2,1)}, f32[767,1,256]{2,1,0:T(1,128)}, f32[384]{0:T(512)}, f32[384,2304]{1,0:T(8,128)}, f32[384,767]{1,0:T(8,128)},...) custom-call(bf16[4,384,640]{2,1,0:T(8,128)(2,1)} %bitcast.9, bf16[2,1536,768]{2,1,0:T(8,128)(2,1)} %bitcast.6, ...), custom_call_target="tpu_custom_call" | custom-call | tf_op jit(solution)/shard_map/deliver/pallas_call | solution.py:1660

commit v7 on v6

--- a/solution.py
+++ b/solution.py
@@ -525,7 +525,6 @@
     hid[0] = (u * inv_rms(u) * gain).astype(BF16)
     x_hid = xc(9, hid.at[0], hid.at[1])
     x_hid.start()
-    tiles = ff // 256
     wide_tile = 512
 
     def up(slot, token, f):
@@ -599,27 +598,27 @@
         return rcopy(gm.at[1 - p.k, at], gk.at[at], ks.at[chip], ks_r.at[chip], p.sibling())
 
     def grad_up(t, carry):
-        at = pl.ds(pl.multiple_of(t * 256, 256), 256)
+        at = pl.ds(pl.multiple_of(t * 384, 384), 384)
         g = dg(hid[0], gpre[0, :, at], TN) + dg(hid[1], gpre[1, :, at], TN)
-        per = width // 256
+        per = width // 384
         r0 = pl.multiple_of((t // per) * width, width)
-        c0 = pl.multiple_of((t % per) * 256, 256)
-        gm[0, pl.ds(r0, width), pl.ds(c0, 256)] = g.astype(BF16)
+        c0 = pl.multiple_of((t % per) * 384, 384)
+        gm[0, pl.ds(r0, width), pl.ds(c0, 384)] = g.astype(BF16)
         return carry
 
     def grad_down(t, carry):
-        at = pl.ds(pl.multiple_of(t * 256, 256), 256)
+        at = pl.ds(pl.multiple_of(t * 384, 384), 384)
         g = dg(act[0, :, at], gmb[0], TN) + dg(act[1, :, at], gmb[1], TN)
         gm[1, at, :] = g.astype(BF16)
         return carry
 
     @pl.when(p.k == 0)
     def _():
-        lax.fori_loop(0, tiles, grad_down, 0)
+        lax.fori_loop(0, ff // 384, grad_down, 0)
 
     @pl.when(p.k == 1)
     def _():
-        lax.fori_loop(0, tiles, grad_up, 0)
+        lax.fori_loop(0, ff // 384, grad_up, 0)
 
     for c in others:
         kc(c).start()
@@ -627,11 +626,11 @@
 
     @pl.when(p.k == 0)
     def _():
-        lax.fori_loop(0, tiles, grad_up, 0)
+        lax.fori_loop(0, ff // 384, grad_up, 0)
 
     @pl.when(p.k == 1)
     def _():
-        lax.fori_loop(0, tiles, grad_down, 0)
+        lax.fori_loop(0, ff // 384, grad_down, 0)
 
     def over_chips(chip, slot):
         return rcopy(ysum.at[chip, turn(p, 0)], y0.at[slot], ys.at[chip], yr.at[slot], p.on_chip(chip))
@@ -880,10 +879,10 @@
                 leftward(z, red.at[z]).start()
 
     def rightward(z, src):
-        return rcopy(src, left.at[z], rs_.at[z], rr.at[z], p.on_line(p.a + 1))
+        return rcopy(src, left.at[z], rs_.at[z], rr.at[z], p.on_line(jnp.minimum(p.a + 1, last)))
 
     def leftward(z, src):
-        return rcopy(src, right.at[z], ls_.at[z], lr.at[z], p.on_line(p.a - 1))
+        return rcopy(src, right.at[z], ls_.at[z], lr.at[z], p.on_line(jnp.maximum(p.a - 1, 0)))
 
     def reduce_step(s):
         @pl.when((p.a >= 1) & (p.a <= s))

time: 216 us -> 216 us (level)
  no operation moved by 1% of the time
where the time goes in v7:
time: 216 us
  Pallas kernels  214 us (99%)
    pallas_call x1, Pallas kernels, back(): pl.pallas_call(functools.partial(back_kernel, n), name='back', out_shape=...  112 us
    pallas_call x1, Pallas kernels, front(): pl.pallas_call(functools.partial(front_kernel, n), name='front', out_shap...  94.5 us
    pallas_call x1, Pallas kernels, deliver(): pl.pallas_call(deliver_kernel, name='deliver', grid=(steps,), out_shape=(...  8.3 us

profile of v7, /device:TPU:0, one launch (start us, length us, event | category | flops | bytes accessed | tf_op | source)
XLA Modules:
  0.0 215.7 jit_solution(16777871056568074581)
XLA Ops:
  1.3 94.5 %front.1 = (bf16[256,768]{1,0:T(8,128)(2,1)}, f32[256,768]{1,0:T(8,128)}, bf16[2,4,192,768]{3,2,1,0:T(8,128)(2,1)}, bf16[2,192,768]{2,1,0:T(8,128)(2,1)}, bf16[2...) custom-call(s32[1]{0:T(128)S(6)} %copy.17.lens, ...), custom_call_target="tpu_custom_call" | custom-call | tf_op jit(solution)/shard_map/front/pallas_call | solution.py:710
  95.8 111.5 %back.1 = (f32[768,256]{1,0:T(8,128)}, bf16[4,2,2,96,640]{4,3,2,1,0:T(8,128)(2,1)}, f32[8,768]{1,0:T(8,128)}, bf16[2,2,4,192,768]{4,3,2,1,0:T(8,128)(2,1)}, bf16[2,2,4,24,768]{4,3,2,1,0:T(8,128)(2,1)}) custom-call(s32[1]{0:T(128)S(6)} %copy.17.lens, bf16[3,1024,128]{2,1,0:T(8,128)(2,1)} %get-tuple-element.37.q3_, bf16[4096,384]{1,0:T(8,128)(2,1)} %get-tuple-element.38.kv, ...), custom_call_target="tpu_custom_call" | custom-call | tf_op jit(solution)/shard_map/back/pallas_call | solution.py:1519
  207.3 8.3 %deliver.1 = (bf16[1,256,767]{2,1,0:T(8,128)(2,1)}, f32[767,1,256]{2,1,0:T(1,128)}, f32[384]{0:T(512)}, f32[384,2304]{1,0:T(8,128)}, f32[384,767]{1,0:T(8,128)},...) custom-call(bf16[4,384,640]{2,1,0:T(8,128)(2,1)} %bitcast.9, bf16[2,1536,768]{2,1,0:T(8,128)(2,1)} %bitcast.6, ...), custom_call_target="tpu_custom_call" | custom-call | tf_op jit(solution)/shard_map/deliver/pallas_call | solution.py:1659

commit v8 on v7

--- a/solution.py
+++ b/solution.py
@@ -1220,6 +1220,9 @@
                 @pl.when(i == 1)
                 def _():
                     chip_sum(2)
+
+                @pl.when(i == 2)
+                def _():
                     out_0()
 
                 @pl.when(i == last)

time: 216 us -> 215 us (level)
  no operation moved by 1% of the time
where the time goes in v8:
time: 215 us
  Pallas kernels  213 us (99%)
    pallas_call x1, Pallas kernels, back(): pl.pallas_call(functools.partial(back_kernel, n), name='back', out_shape=...  111 us
    pallas_call x1, Pallas kernels, front(): pl.pallas_call(functools.partial(front_kernel, n), name='front', out_shap...  94.5 us
    pallas_call x1, Pallas kernels, deliver(): pl.pallas_call(deliver_kernel, name='deliver', grid=(steps,), out_shape=(...  8.3 us

profile of v8, /device:TPU:0, one launch (start us, length us, event | category | flops | bytes accessed | tf_op | source)
XLA Modules:
  0.0 214.8 jit_solution(14587125235670099995)
XLA Ops:
  1.3 94.5 %front.1 = (bf16[256,768]{1,0:T(8,128)(2,1)}, f32[256,768]{1,0:T(8,128)}, bf16[2,4,192,768]{3,2,1,0:T(8,128)(2,1)}, bf16[2,192,768]{2,1,0:T(8,128)(2,1)}, bf16[2...) custom-call(s32[1]{0:T(128)S(6)} %copy.17.lens, ...), custom_call_target="tpu_custom_call" | custom-call | tf_op jit(solution)/shard_map/front/pallas_call | solution.py:710
  95.8 110.5 %back.1 = (f32[768,256]{1,0:T(8,128)}, bf16[4,2,2,96,640]{4,3,2,1,0:T(8,128)(2,1)}, f32[8,768]{1,0:T(8,128)}, bf16[2,2,4,192,768]{4,3,2,1,0:T(8,128)(2,1)}, bf16[2,2,4,24,768]{4,3,2,1,0:T(8,128)(2,1)}) custom-call(s32[1]{0:T(128)S(6)} %copy.17.lens, bf16[3,1024,128]{2,1,0:T(8,128)(2,1)} %get-tuple-element.37.q3_, bf16[4096,384]{1,0:T(8,128)(2,1)} %get-tuple-element.38.kv, ...), custom_call_target="tpu_custom_call" | custom-call | tf_op jit(solution)/shard_map/back/pallas_call | solution.py:1522
  206.3 8.3 %deliver.1 = (bf16[1,256,767]{2,1,0:T(8,128)(2,1)}, f32[767,1,256]{2,1,0:T(1,128)}, f32[384]{0:T(512)}, f32[384,2304]{1,0:T(8,128)}, f32[384,767]{1,0:T(8,128)},...) custom-call(bf16[4,384,640]{2,1,0:T(8,128)(2,1)} %bitcast.9, bf16[2,1536,768]{2,1,0:T(8,128)(2,1)} %bitcast.6, ...), custom_call_target="tpu_custom_call" | custom-call | tf_op jit(solution)/shard_map/deliver/pallas_call | solution.py:1662
